TPU v7x, 32 devices: a whole 2x2x4 slice. The times are simulated.
32 devices in a mesh: gx: 8 (over z, core), gy: 4 (over y, x).
Axes of the slice: x: 2, y: 2, z: 4, core: 2. Of those that a mesh axis runs over, the one named last changes fastest.
Arguments:
- basis: float32 [8, 4, 96, 2048], P('gx', 'gy')
- block_vals: float32 [8, 4, 16, 5, 128, 128], P('gx', 'gy'), as said below
- block_cols: int32 [8, 4, 16, 5], P('gx', 'gy'), may hold values from 0 to 15, as said below
- edge_rows: int32 [8, 4, 4, 256], P('gx', 'gy'), may hold values from 0 to 2047, as said below
- live_counts: int32 [8, 4], P('gx', 'gy'), may hold values from 1024 to 2048, as said below
Outputs:
- encoding: float32 [8, 4, 96, 2048], P('gx', 'gy')
Inputs may be any that keep to these rules, and one draw needn't show every extreme that they name: `live_counts`: every tile has 1024 or more live cells, and some tile is full. `block_cols`: entries name blocks of the same tile. `block_vals`: weights are nonnegative; the weight between two cells is the same in both stored blocks that hold it, and a cell has no weight to itself. `edge_rows`: every entry is a live cell of its tile.
All inputs are finite; a program needn't handle non-finite values.
Results may differ from a plain program's by a relative error of at most 0.0001.
Values sent between devices are 32-bit elements; how exact they have to be, the bound alone decides.
No kernel may reach another device: no remote copies, remote signals or barrier semaphores. Data moves between devices by JAX's collectives and lax.ppermute only.
A program may use at most 64 MiB of HBM per device.

v0:
```python
import functools
import math

import jax
import jax.numpy as jnp
from jax import lax
from jax.experimental import pallas as pl
from jax.experimental.pallas import tpu as pltpu
from jax.sharding import PartitionSpec as P


LOWER_FRACTION = 0.125
LANES = 128
CHUNK = 256
F32 = jnp.float32
BF16 = jnp.bfloat16
NT = (((1,), (1,)), ((), ()))
VM = pl.BlockSpec(memory_space=pltpu.VMEM)
SM = pl.BlockSpec(memory_space=pltpu.SMEM)
HBM = pl.BlockSpec(memory_space=pltpu.HBM)
LIMIT = 24 << 20
SIDES = (("gx", 1), ("gy", 1), ("gy", 0), ("gx", 0))


def split(x):
    hi = x.astype(BF16)
    return hi, (x - hi.astype(F32)).astype(BF16)


def stacked(x):
    return jnp.concatenate(split(x), axis=0)


def folded(x):
    half = x.shape[0] // 2
    return x[:half] + x[half:]


def dot(a, b):
    return jnp.dot(a, b, preferred_element_type=F32)


def dot_nt(a, b):
    return lax.dot_general(a, b, NT, preferred_element_type=F32)


def product_nt(a, b):
    left, right = stacked(a), stacked(b)
    product = folded(dot_nt(left, right))
    half = product.shape[1] // 2
    return product[:, :half] + product[:, half:]


def near_pairs(size):
    return [(i, i ^ 1) for i in range(size)]


def far_pairs(size):
    return [(i, (i + 1 if i % 2 else i - 1) % size) for i in range(size)]


def turn_pairs(size):
    up = [(i, i + 2 if i + 2 < size else i + 1) for i in range(0, size, 2)]
    down = [(i, i - 2 if i > 1 else 0) for i in range(1, size, 2)]
    return up + down


def xor_pairs(size, bit):
    return [(i, i ^ bit) for i in range(size)]


def live_lanes(count, start, width):
    return lax.broadcasted_iota(jnp.int32, (1, width), 1) + start < count


def left_rows(value):
    hi, lo = split(value)
    return jnp.concatenate(
        [
            jnp.concatenate([hi, hi], axis=1),
            jnp.concatenate([lo, jnp.zeros_like(lo)], axis=1),
        ],
        axis=0,
    )


def scalars(peak):
    upper = 2.0 * peak[0:1, 0:1]
    lower = LOWER_FRACTION * upper
    return (upper + lower) / 2.0, (upper - lower) / 2.0


def first_kernel(sizes, cols, counts, lists_any, basis_any, weights_any, *refs):
    place, stored, begin, degree, peak, marks = refs[:6]
    outs = refs[6:10]
    lists, basis, weights, sems = refs[10:]
    blocks, slots = weights.shape[:2]
    cells, edges = place.shape
    width = edges // len(outs)
    loads = [
        pltpu.make_async_copy(lists_any.at[0, 0], lists, sems.at[blocks]),
        pltpu.make_async_copy(basis_any.at[0, 0], basis, sems.at[blocks + 1]),
    ]
    blocks_in = [
        pltpu.make_async_copy(weights_any.at[0, 0, m], weights.at[m], sems.at[m]) for m in range(blocks)
    ]
    for load in loads + blocks_in:
        load.start()
    count = counts[...]
    degree[...] = jnp.zeros_like(degree)
    loads[0].wait()
    order = []
    for axis, shift in SIDES:
        dim = ("gx", "gy").index(axis)
        me = lax.axis_index(axis)
        upward = me % 2 == shift
        low, high = lists[2 * dim : 2 * dim + 1], lists[2 * dim + 1 : 2 * dim + 2]
        low, high = jnp.where(me > 0, low, -1), jnp.where(me < sizes[dim] - 1, high, -1)
        order.append(jnp.where(upward, high, low))
    targets = jnp.concatenate(order, axis=1)
    marks[...] = jnp.broadcast_to(targets, marks.shape)
    for start in range(0, cells, CHUNK):
        spot = lax.broadcasted_iota(jnp.int32, (CHUNK, edges), 0) + start
        place[start : start + CHUNK] = (spot == targets).astype(F32).astype(BF16)
    loads[1].wait()
    begin[...] = jnp.where(live_lanes(count, 0, cells), basis[...], 0.0)
    picked = folded(dot(stacked(begin[...]), place[...]))
    for i, out in enumerate(outs):
        out[...] = picked[:, i * width : (i + 1) * width]
    joined = dot_nt(jnp.ones((16, edges), BF16), place[...])[:8]
    for m in range(blocks):
        blocks_in[m].wait()
        for j in range(slots):
            hi, lo = split(weights[m, j])
            stored[m, 0:LANES, j * LANES : (j + 1) * LANES] = hi
            stored[m, LANES : 2 * LANES, j * LANES : (j + 1) * LANES] = lo
        live = live_lanes(count, m * LANES, LANES)
        ones = jnp.broadcast_to(live.astype(F32), (16, LANES)).astype(BF16)
        sums = dot(jnp.concatenate([ones, ones], axis=1), stored[m])[:8]
        for j in range(slots):
            spot = pl.ds(pl.multiple_of(cols[0, j, 0, m] * LANES, LANES), LANES)
            degree[:, spot] += sums[:, j * LANES : (j + 1) * LANES]
    value = jnp.where(live_lanes(count, 0, cells), degree[...] + joined, 0.0)
    degree[...] = value
    peak[...] = jnp.full(peak.shape, jnp.max(value), F32)


def multiply(cols, values, stored, inside):
    blocks, _, width = stored.shape
    inside[...] = jnp.zeros_like(inside)
    for m in range(blocks):
        product = folded(dot(left_rows(values[:, m * LANES : (m + 1) * LANES]), stored[m]))
        for j in range(width // LANES):
            spot = pl.ds(pl.multiple_of(cols[0, j, 0, m] * LANES, LANES), LANES)
            inside[:, spot] += product[:, j * LANES : (j + 1) * LANES]


def gather(values, place):
    return folded(dot(stacked(values), place[...]))


def joined_up(parts):
    return jnp.concatenate([part[...] for part in parts], axis=1)


def chunks(cells):
    return [slice(start, start + CHUNK) for start in range(0, cells, CHUNK)]


def open_kernel(cols, counts, begin, stored, degree, place, marks, local, edge_local, same, inside):
    cells, edges = place.shape
    targets = marks[0:1]
    for start in range(0, edges, LANES):
        across = jnp.broadcast_to(targets[:, start : start + LANES], (LANES, LANES))
        down = across.astype(F32).T.astype(jnp.int32)
        down = jnp.where(down < 0, -2, down)
        for other in range(0, edges, LANES):
            equal = down == targets[:, other : other + LANES]
            same[start : start + LANES, other : other + LANES] = equal.astype(F32).astype(BF16)
    multiply(cols, begin, stored, inside)
    for part in chunks(cells):
        live = live_lanes(counts[...], part.start, CHUNK)
        local[:, part] = degree[0:1, part] * begin[:, part] - jnp.where(live, inside[:, part], 0.0)
    edge_local[...] = gather(local[...], place)


def edges_kernel(number, r0, r1, r2, r3, edge_local, same, own, peak, before, *outs):
    crossed = folded(dot(stacked(joined_up((r0, r1, r2, r3))), same[...]))
    if number == 0:
        value = edge_local[...] - crossed
    elif number == 1:
        centre, half = scalars(peak)
        top = own[0:1, 0:1]
        first, second = joined_up(before[:4]), joined_up(before[4:])
        value = second_field(centre, half, top, edge_local[...] - crossed / top, second, first)[1]
    else:
        _, half = scalars(peak)
        value = edge_local[...] - (2.0 / half) * crossed
    width = value.shape[1] // len(outs)
    for i, out in enumerate(outs):
        out[...] = value[:, i * width : (i + 1) * width]


def second_field(centre, half, top, twice, once, begin):
    ratio = centre / half
    shrunk = once / half
    first = shrunk - ratio * begin
    second = (2.0 / half) * (top / half) * twice - 2.0 * ratio * (shrunk + first) - begin
    return first, second


def field_kernel(number, cols, counts, r0, r1, r2, r3, local, stored, degree, place, own, peak, begin, once, *refs):
    field, later, edge_local = refs[:3]
    inside = refs[-1]
    cells = place.shape[0]
    top = own[0:1, 0:1]
    centre, half = scalars(peak)
    arrived = stacked(joined_up((r0, r1, r2, r3)))
    for part in chunks(cells):
        crossed = folded(dot_nt(arrived, place[part]))
        if number == 0:
            field[:, part] = (local[:, part] - crossed) / top
        elif number == 1:
            first, field[:, part] = second_field(
                centre, half, top, local[:, part] - crossed / top, once[:, part] * top, begin[:, part]
            )
            later[:, part] = first
        else:
            field[:, part] = local[:, part] - (2.0 / half) * crossed
            later[:, part] = begin[:, part]
    multiply(cols, field, stored, inside)
    for part in chunks(cells):
        live = live_lanes(counts[...], part.start, CHUNK)
        kept = jnp.where(live, inside[:, part], 0.0)
        if number == 0:
            later[:, part] = degree[0:1, part] * field[:, part] - kept
        else:
            value = (degree[0:1, part] - centre) * field[:, part] - kept
            later[:, part] = (2.0 / half) * value - later[:, part]
    edge_local[...] = gather(later[...], place)
    if number == 2:
        refs[3][...] = product_nt(later[...], later[...])


def gram_kernel(r0, r1, r2, r3, edge_local, same, peak, base, gram):
    _, half = scalars(peak)
    scale = 2.0 / half
    arrived = joined_up((r0, r1, r2, r3))
    crossed = folded(dot(stacked(arrived), same[...]))
    mixed = product_nt(scale * (edge_local[...] - (0.5 * scale) * crossed), arrived)
    gram[...] = base[...] - mixed - mixed.T


def last_kernel(r0, r1, r2, r3, local, place, peak, terms):
    _, half = scalars(peak)
    arrived = stacked(joined_up((r0, r1, r2, r3)))
    for part in chunks(place.shape[0]):
        hi, lo = split(local[:, part] - (2.0 / half) * folded(dot_nt(arrived, place[part])))
        terms[:, part] = jnp.concatenate([hi, lo, hi], axis=0)


def small_inverse(rows, start, size, width):
    near = [
        [jnp.broadcast_to(rows[i : i + 1, start + j : start + j + 1], (size, width)) for j in range(i + 1)]
        for i in range(size)
    ]
    far = [[None] * size for _ in range(size)]
    for k in range(size):
        pivot = near[k][k]
        inverse = 1.0 / pivot
        for i in range(k + 1, size):
            factor = near[i][k] * inverse
            for j in range(k + 1, i + 1):
                near[i][j] = near[i][j] - factor * near[j][k]
            for j in range(k):
                far[i][j] = far[i][j] - factor * far[k][j]
            far[i][k] = -factor
        root = lax.rsqrt(pivot)
        near[k] = root
    return [
        [far[i][j] * near[i] for j in range(i)] + [near[i]] for i in range(size)
    ]


def total(terms):
    terms = list(terms)
    while len(terms) > 1:
        terms = [a + b for a, b in zip(terms[::2], terms[1::2])] + terms[len(terms) & ~1 :]
    return terms[0]


def encode_kernel(root, first, second, values, out):
    gram = first[...] + second[...]
    vecs = gram.shape[0]
    size = 8
    lane = lax.broadcasted_iota(jnp.int32, (size, vecs), 1)
    sub = lax.broadcasted_iota(jnp.int32, (size, vecs), 0)
    rows = [gram[i * size : (i + 1) * size] for i in range(vecs // size)]
    for g in range(vecs // size):
        start = g * size
        inside = jnp.logical_and(lane >= start, lane < start + size)
        small = small_inverse(rows[g], start, size, vecs)
        unit = jnp.where(inside, (lane - start == sub).astype(F32), rows[g])
        spread_rows = [jnp.broadcast_to(unit[j : j + 1], (size, vecs)) for j in range(size)]
        half = [
            total(small[i][j] * spread_rows[j] for j in range(i + 1)) for i in range(size)
        ]
        whole = [
            total(small[i][j] * half[i] for i in range(j, size)) for j in range(size)
        ]
        for i in range(g + 1, vecs // size):
            kept = jnp.where(inside, 0.0, rows[i])
            rows[i] = kept - total(
                jnp.broadcast_to(rows[i][:, start + j : start + j + 1], (size, vecs)) * whole[j]
                for j in range(size)
            )
        done = half[0]
        for j in range(1, size):
            done = jnp.where(sub == j, half[j], done)
        rows[g] = jnp.where(lane < start + size, done, 0.0)
    hi, lo = split(jnp.concatenate(rows, axis=0) * root)
    out[0, 0] = dot(jnp.concatenate([hi, hi, lo], axis=1), values[...])


def call(kernel, shapes, specs, **extra):
    many = isinstance(shapes, (tuple, list))
    return pl.pallas_call(
        kernel,
        out_shape=shapes,
        in_specs=specs,
        out_specs=[VM] * len(shapes) if many else VM,
        compiler_params=pltpu.CompilerParams(vmem_limit_bytes=LIMIT),
        **extra,
    )


def shape(*dims, dtype=F32):
    return jax.ShapeDtypeStruct(dims, dtype)


def spread(value, combine, stages):
    for axis, bit in stages:
        pairs = xor_pairs(lax.axis_size(axis), bit)
        value = combine(value, lax.ppermute(value, axis, pairs))
    return value


def per_device(basis, block_vals, block_cols, edge_rows, live_counts):
    vecs, cells = basis.shape[2:]
    blocks, slots, block = block_vals.shape[2:5]
    edges = edge_rows.shape[3]
    sizes = (lax.axis_size("gx"), lax.axis_size("gy"))
    field = shape(vecs, cells)
    sends = [shape(vecs, edges)] * 4
    edge_field = shape(vecs, 4 * edges)
    scratch = [pltpu.VMEM((vecs, cells), F32)]

    def exchange(parts):
        x_far, y_far, y_near, x_near = parts
        x_far = lax.ppermute(x_far, "gx", near_pairs(sizes[0]))
        y_far = lax.ppermute(y_far, "gy", far_pairs(sizes[1]))
        y_near = lax.ppermute(y_near, "gy", near_pairs(sizes[1]))
        x_far = lax.ppermute(x_far, "gx", turn_pairs(sizes[0]))
        x_near = lax.ppermute(x_near, "gx", near_pairs(sizes[0]))
        return [x_far, y_far, y_near, x_near]

    cols = jnp.transpose(block_cols, (0, 3, 1, 2))
    place, stored, begin, degree, own, marks, *outgoing = call(
        functools.partial(first_kernel, sizes),
        [
            shape(cells, 4 * edges, dtype=BF16),
            shape(blocks, 2 * block, slots * block, dtype=BF16),
            field,
            shape(8, cells),
            shape(8, LANES),
            shape(8, 4 * edges, dtype=jnp.int32),
        ]
        + sends,
        [SM, VM] + [HBM] * 3,
        scratch_shapes=[
            pltpu.VMEM((4, edges), jnp.int32),
            pltpu.VMEM((vecs, cells), F32),
            pltpu.VMEM((blocks, slots, block, block), F32),
            pltpu.SemaphoreType.DMA((blocks + 2,)),
        ],
    )(
        cols,
        live_counts,
        *(pltpu.with_memory_space_constraint(x, pltpu.HBM) for x in (edge_rows, basis, block_vals)),
    )
    stages = [
        (axis, 1 << b) for axis, size in zip(("gx", "gy"), sizes) for b in range(size.bit_length() - 1)
    ]
    arrived = exchange(outgoing)
    peak = spread(own, jnp.maximum, stages)
    local, edge_local, same = call(
        open_kernel,
        [field, edge_field, shape(4 * edges, 4 * edges, dtype=BF16)],
        [SM] + [VM] * 6,
        scratch_shapes=scratch,
    )(cols, live_counts, begin, stored, degree, place, marks)

    history, earlier = [outgoing], [begin, begin]
    for number in range(3):
        bound = peak if number else own
        before = [x for parts in history for x in parts] if number == 1 else []
        outgoing = call(
            lambda *refs, number=number, count=len(before): edges_kernel(
                number, *refs[:8], refs[8 : 8 + count], *refs[8 + count :]
            ),
            sends,
            [VM] * (8 + len(before)),
        )(*arrived, edge_local, same, own, bound, *before)
        history.append(outgoing)
        coming = exchange(outgoing)
        now, local, edge_local, *base = call(
            functools.partial(field_kernel, number),
            [field, field, edge_field] + [shape(vecs, vecs)] * (number == 2),
            [SM] + [VM] * 13,
            scratch_shapes=scratch,
        )(cols, live_counts, *arrived, local, stored, degree, place, own, bound, *earlier)
        earlier = [begin, now] if number == 0 else [now, now]
        arrived = coming

    gram = call(gram_kernel, shape(vecs, vecs), [VM] * 8)(*arrived, edge_local, same, peak, *base)
    gram = spread(gram, jnp.add, stages[:-1])
    axis, bit = stages[-1]
    other = lax.ppermute(gram, axis, xor_pairs(lax.axis_size(axis), bit))
    now = call(last_kernel, shape(3 * vecs, cells, dtype=BF16), [VM] * 7)(*arrived, local, place, peak)
    root = math.sqrt(cells * sizes[0] * sizes[1])
    return call(functools.partial(encode_kernel, root), shape(1, 1, vecs, cells), [VM] * 3)(gram, other, now)


def solution(mesh):
    in_specs = (
        P("gx", "gy", None, None),
        P("gx", "gy", None, None, None, None),
        P("gx", "gy", None, None),
        P("gx", "gy", None, None),
        P("gx", "gy"),
    )
    out_specs = P("gx", "gy", None, None)

    return jax.shard_map(
        per_device, mesh=mesh, in_specs=in_specs, out_specs=out_specs, check_vma=False
    )
```

profile of v0, /device:TPU:0, one launch (start us, length us, event | category | flops | bytes accessed | tf_op | source)
XLA Modules:
  0.0 90.2 jit_solution(4868522986553425647)
XLA Ops:
  0.7 0.7 copy-done
  1.3 7.7 %shard_map.55 = (bf16[2048,1024]{1,0:T(8,128)(2,1)S(1)}, bf16[16,256,640]{2,1,0:T(8,128)(2,1)S(1)}, f32[96,2048]{1,0:T(8,128)S(1)}, f32[8,2048]{1,0:T(8,128)S(1)...) custom-call(s32[1,5,1,16]{3,2,1,0:T(1,128)S(1)} %bitcast.1, ...), custom_call_target="tpu_custom_call" | custom-call | tf_op jit(solution)/shard_map/pallas_call | solution.py:368
  9.1 0.6 collective-permute-start
  9.6 3.5 %collective-permute-start.2 = (f32[96,256]{1,0:T(8,128)S(1)}, f32[96,256]{1,0:T(8,128)S(1)}, u32[]{:S(2)}, u32[]{:S(2)}) collective-permute-start(f32[96,256]{1,0:T(8,128)S(1)} %get-tuple-element.40.refs_9_), channel_id=1, source_target_pairs={{0,3},{1,2},{2,1},{3,0},{4,7},{5,6},{6,5},{7,4},{8,11},{9,10},{10,... | collective-permute-start | bytes 294920 | tf_op jit(solution)/shard_map/ppermute | solution.py:361
  13.1 0.5 collective-permute-start.3
  13.7 1.6 %collective-permute-start.1 = (f32[96,256]{1,0:T(8,128)S(1)}, f32[96,256]{1,0:T(8,128)S(1)}, u32[]{:S(2)}, u32[]{:S(2)}) collective-permute-start(f32[96,256]{1,0:T(8,128)S(1)} %collective-permute-done), channel_id=1, source_target_pairs={{0,8},{8,16},{16,24},{24,28},{4,0},{12,4},{20,12},{28,20},{1,9},{9... | collective-permute-start | bytes 294920 | tf_op jit(solution)/shard_map/ppermute | solution.py:363
  15.2 3.6 %shard_map.56 = (f32[96,2048]{1,0:T(8,128)S(1)}, f32[96,1024]{1,0:T(8,128)S(1)}, bf16[1024,1024]{1,0:T(8,128)(2,1)S(1)}) custom-call(s32[1,5,1,16]{3,2,1,0:T(1,128)S(1)} %bitcast.2, s32[1,1]{1,0:T(1,128)S(6)} %copy.6.counts, f32[96,2048]{1,0:T(8,128)S(1)} %get-tuple-element.43.begin.once, bf16[16,256,640]{2,1,0:T(8,128)(2,1)S(1)} %get-tuple-element.44.stored, ...), custom_call_target="tpu_custom_call" | custom-call | tf_op jit(solution)/shard_map/pallas_call | solution.py:396
  18.8 0.0 collective-permute-done.3.refs_2_.r2
  18.9 0.6 shard_map.57
  19.5 0.1 collective-permute-start.5
  19.6 1.5 %collective-permute-start.7 = (f32[96,256]{1,0:T(8,128)S(1)}, f32[96,256]{1,0:T(8,128)S(1)}, u32[]{:S(2)}, u32[]{:S(2)}) collective-permute-start(f32[96,256]{1,0:T(8,128)S(1)} %get-tuple-element.52.refs_13_), channel_id=1, source_target_pairs={{0,3},{1,2},{2,1},{3,0},{4,7},{5,6},{6,5},{7,4},{8,11},{9,10},{10,... | collective-permute-start | bytes 294920 | tf_op jit(solution)/shard_map/ppermute | solution.py:361
  21.1 0.6 collective-permute-start.8
  21.6 1.6 %collective-permute-start.6 = (f32[96,256]{1,0:T(8,128)S(1)}, f32[96,256]{1,0:T(8,128)S(1)}, u32[]{:S(2)}, u32[]{:S(2)}) collective-permute-start(f32[96,256]{1,0:T(8,128)S(1)} %collective-permute-done.5), channel_id=1, source_target_pairs={{0,8},{8,16},{16,24},{24,28},{4,0},{12,4},{20,12},{28,20},{1,9},{9... | collective-permute-start | bytes 294920 | tf_op jit(solution)/shard_map/ppermute | solution.py:363
  23.2 1.2 %collective-permute-done.10 = f32[8,128]{1,0:T(8,128)S(1)} collective-permute-done((f32[8,128]{1,0:T(8,128)S(1)}, f32[8,128]{1,0:T(8,128)S(1)}, u32[]{:S(2)}, u32[]{:S(2)}) %collective-permute-start.10) | collective-permute-done | bytes 4128 | tf_op jit(solution)/shard_map/ppermute | solution.py:344
  24.4 1.6 %collective-permute-start.11 = (f32[8,128]{1,0:T(8,128)S(1)}, f32[8,128]{1,0:T(8,128)S(1)}, u32[]{:S(2)}, u32[]{:S(2)}) collective-permute-start(f32[8,128]{1,0:T(8,128)S(1)} %max.15), channel_id=1, source_target_pairs={{0,8},{4,12},{8,0},{12,4},{16,24},{20,28},{24,16},{28,20},{1,9},{5... | collective-permute-start | bytes 12296 | tf_op jit(solution)/shard_map/ppermute | solution.py:344
  25.9 2.0 %collective-permute-done.11 = f32[8,128]{1,0:T(8,128)S(1)} collective-permute-done((f32[8,128]{1,0:T(8,128)S(1)}, f32[8,128]{1,0:T(8,128)S(1)}, u32[]{:S(2)}, u32[]{:S(2)}) %collective-permute-start.11) | collective-permute-done | bytes 4128 | tf_op jit(solution)/shard_map/ppermute | solution.py:344
  28.0 2.6 %collective-permute-start.12 = (f32[8,128]{1,0:T(8,128)S(1)}, f32[8,128]{1,0:T(8,128)S(1)}, u32[]{:S(2)}, u32[]{:S(2)}) collective-permute-start(f32[8,128]{1,0:T(8,128)S(1)} %max.16), channel_id=1, source_target_pairs={{0,16},{4,20},{8,24},{12,28},{16,0},{20,4},{24,8},{28,12},{1,17},{... | collective-permute-start | bytes 12296 | tf_op jit(solution)/shard_map/ppermute | solution.py:344
  30.6 1.9 %collective-permute-done.12 = f32[8,128]{1,0:T(8,128)S(1)} collective-permute-done((f32[8,128]{1,0:T(8,128)S(1)}, f32[8,128]{1,0:T(8,128)S(1)}, u32[]{:S(2)}, u32[]{:S(2)}) %collective-permute-start.12) | collective-permute-done | bytes 4128 | tf_op jit(solution)/shard_map/ppermute | solution.py:344
  32.5 1.5 %collective-permute-start.13 = (f32[8,128]{1,0:T(8,128)S(1)}, f32[8,128]{1,0:T(8,128)S(1)}, u32[]{:S(2)}, u32[]{:S(2)}) collective-permute-start(f32[8,128]{1,0:T(8,128)S(1)} %max.17), channel_id=1, source_target_pairs={{0,1},{1,0},{2,3},{3,2},{4,5},{5,4},{6,7},{7,6},{8,9},{9,8},{10,11... | collective-permute-start | bytes 12296 | tf_op jit(solution)/shard_map/ppermute | solution.py:344
  34.0 2.1 %collective-permute-done.13 = f32[8,128]{1,0:T(8,128)S(1)} collective-permute-done((f32[8,128]{1,0:T(8,128)S(1)}, f32[8,128]{1,0:T(8,128)S(1)}, u32[]{:S(2)}, u32[]{:S(2)}) %collective-permute-start.13) | collective-permute-done | bytes 4128 | tf_op jit(solution)/shard_map/ppermute | solution.py:344
  36.1 1.5 %collective-permute-start.14 = (f32[8,128]{1,0:T(8,128)S(1)}, f32[8,128]{1,0:T(8,128)S(1)}, u32[]{:S(2)}, u32[]{:S(2)}) collective-permute-start(f32[8,128]{1,0:T(8,128)S(1)} %max.18), channel_id=1, source_target_pairs={{0,2},{1,3},{2,0},{3,1},{4,6},{5,7},{6,4},{7,5},{8,10},{9,11},{10,... | collective-permute-start | bytes 12296 | tf_op jit(solution)/shard_map/ppermute | solution.py:344
  37.6 2.1 %collective-permute-done.14 = f32[8,128]{1,0:T(8,128)S(1)} collective-permute-done((f32[8,128]{1,0:T(8,128)S(1)}, f32[8,128]{1,0:T(8,128)S(1)}, u32[]{:S(2)}, u32[]{:S(2)}) %collective-permute-start.14) | collective-permute-done | bytes 4128 | tf_op jit(solution)/shard_map/ppermute | solution.py:344
  39.7 4.7 %shard_map.58 = (f32[96,2048]{1,0:T(8,128)S(1)}, f32[96,2048]{1,0:T(8,128)S(1)}, f32[96,1024]{1,0:T(8,128)S(1)}) custom-call(s32[1,5,1,16]{3,2,1,0:T(1,128)S(1)} %bitcast.3, s32[1,1]{1,0:T(1,128)S(6)} %copy.6.counts, f32[96,256]{1,0:T(8,128)S(1)} %collective-permute-done.1.refs_0_.r0, f32[96,256]{1,0:T(8,128)S(1)} %collective-permute-done.2.refs_1_.r1, ...), custom_call_target="tpu_custom_call" | custom-call | tf_op jit(solution)/shard_map/pallas_call | solution.py:416
  44.4 0.7 shard_map.59
  45.1 0.1 collective-permute-start.15
  45.2 2.5 %collective-permute-start.17 = (f32[96,256]{1,0:T(8,128)S(1)}, f32[96,256]{1,0:T(8,128)S(1)}, u32[]{:S(2)}, u32[]{:S(2)}) collective-permute-start(f32[96,256]{1,0:T(8,128)S(1)} %get-tuple-element.58), channel_id=1, source_target_pairs={{0,3},{1,2},{2,1},{3,0},{4,7},{5,6},{6,5},{7,4},{8,11},{9,10},{10,... | collective-permute-start | bytes 294920 | tf_op jit(solution)/shard_map/ppermute | solution.py:361
  47.7 0.5 collective-permute-start.18
  48.2 1.6 %collective-permute-start.16 = (f32[96,256]{1,0:T(8,128)S(1)}, f32[96,256]{1,0:T(8,128)S(1)}, u32[]{:S(2)}, u32[]{:S(2)}) collective-permute-start(f32[96,256]{1,0:T(8,128)S(1)} %collective-permute-done.15), channel_id=1, source_target_pairs={{0,8},{8,16},{16,24},{24,28},{4,0},{12,4},{20,12},{28,20},{1,9},{9... | collective-permute-start | bytes 294920 | tf_op jit(solution)/shard_map/ppermute | solution.py:363
  49.9 5.2 %shard_map.60 = (f32[96,2048]{1,0:T(8,128)S(1)}, f32[96,2048]{1,0:T(8,128)S(1)}, f32[96,1024]{1,0:T(8,128)S(1)}) custom-call(s32[1,5,1,16]{3,2,1,0:T(1,128)S(1)} %bitcast.4, s32[1,1]{1,0:T(1,128)S(6)} %copy.6.counts, f32[96,256]{1,0:T(8,128)S(1)} %collective-permute-done.6.refs_0_.r0, f32[96,256]{1,0:T(8,128)S(1)} %collective-permute-done.7.refs_1_.r1, ...), custom_call_target="tpu_custom_call" | custom-call | tf_op jit(solution)/shard_map/pallas_call | solution.py:416
  55.1 0.6 shard_map.61
  55.7 0.1 collective-permute-start.20
  55.8 1.5 %collective-permute-start.22 = (f32[96,256]{1,0:T(8,128)S(1)}, f32[96,256]{1,0:T(8,128)S(1)}, u32[]{:S(2)}, u32[]{:S(2)}) collective-permute-start(f32[96,256]{1,0:T(8,128)S(1)} %get-tuple-element.65), channel_id=1, source_target_pairs={{0,3},{1,2},{2,1},{3,0},{4,7},{5,6},{6,5},{7,4},{8,11},{9,10},{10,... | collective-permute-start | bytes 294920 | tf_op jit(solution)/shard_map/ppermute | solution.py:361
  57.2 0.5 collective-permute-start.23
  57.8 1.6 %collective-permute-start.21 = (f32[96,256]{1,0:T(8,128)S(1)}, f32[96,256]{1,0:T(8,128)S(1)}, u32[]{:S(2)}, u32[]{:S(2)}) collective-permute-start(f32[96,256]{1,0:T(8,128)S(1)} %collective-permute-done.20), channel_id=1, source_target_pairs={{0,8},{8,16},{16,24},{24,28},{4,0},{12,4},{20,12},{28,20},{1,9},{9... | collective-permute-start | bytes 294920 | tf_op jit(solution)/shard_map/ppermute | solution.py:363
  59.4 5.5 %shard_map.62 = (f32[96,2048]{1,0:T(8,128)}, f32[96,2048]{1,0:T(8,128)S(1)}, f32[96,1024]{1,0:T(8,128)S(1)}, f32[96,96]{1,0:T(8,128)S(1)}) custom-call(s32[1,5,1,16]{3,2,1,0:T(1,128)S(1)} %bitcast.5, s32[1,1]{1,0:T(1,128)S(6)} %copy.6.counts, f32[96,256]{1,0:T(8,128)S(1)} %collective-permute-done.16.refs_0_.r0, ...), custom_call_target="tpu_custom_call" | custom-call | tf_op jit(solution)/shard_map/pallas_call | solution.py:416
  64.9 1.0 %shard_map.63 = f32[96,96]{1,0:T(8,128)S(1)} custom-call(f32[96,256]{1,0:T(8,128)S(1)} %collective-permute-done.21.r0, f32[96,256]{1,0:T(8,128)S(1)} %collective-permute-done.22.r1, f32[96,256]{1,0:T(8,128)S(1)} %collective-permute-done.23.r2, f32[96,256]{1,0:T(8,128)S(1)} %collective-permute-done.24.r3, f32[96,1024]{1,0:T(8,128)S(1)} %get-tuple-element.70.edge_local, ...), custom_call_target="tpu_custom_call" | custom-call | tf_op jit(solution)/shard_map/pallas_call | solution.py:425
  65.9 0.1 collective-permute-start.25
  66.0 1.2 %collective-permute-done.25 = f32[96,96]{1,0:T(8,128)S(1)} collective-permute-done((f32[96,96]{1,0:T(8,128)S(1)}, f32[96,96]{1,0:T(8,128)S(1)}, u32[]{:S(2)}, u32[]{:S(2)}) %collective-permute-start.25) | collective-permute-done | bytes 36896 | tf_op jit(solution)/shard_map/ppermute | solution.py:344
  67.2 0.6 collective-permute-start.26
  67.8 3.6 %collective-permute-done.26 = f32[96,96]{1,0:T(8,128)S(1)} collective-permute-done((f32[96,96]{1,0:T(8,128)S(1)}, f32[96,96]{1,0:T(8,128)S(1)}, u32[]{:S(2)}, u32[]{:S(2)}) %collective-permute-start.26) | collective-permute-done | bytes 36896 | tf_op jit(solution)/shard_map/ppermute | solution.py:344
  71.4 1.6 %collective-permute-start.27 = (f32[96,96]{1,0:T(8,128)S(1)}, f32[96,96]{1,0:T(8,128)S(1)}, u32[]{:S(2)}, u32[]{:S(2)}) collective-permute-start(f32[96,96]{1,0:T(8,128)S(1)} %add.13), channel_id=1, source_target_pairs={{0,16},{4,20},{8,24},{12,28},{16,0},{20,4},{24,8},{28,12},{1,17},{... | collective-permute-start | bytes 110600 | tf_op jit(solution)/shard_map/ppermute | solution.py:344
  73.0 3.9 %collective-permute-done.27 = f32[96,96]{1,0:T(8,128)S(1)} collective-permute-done((f32[96,96]{1,0:T(8,128)S(1)}, f32[96,96]{1,0:T(8,128)S(1)}, u32[]{:S(2)}, u32[]{:S(2)}) %collective-permute-start.27) | collective-permute-done | bytes 36896 | tf_op jit(solution)/shard_map/ppermute | solution.py:344
  76.9 1.5 %collective-permute-start.28 = (f32[96,96]{1,0:T(8,128)S(1)}, f32[96,96]{1,0:T(8,128)S(1)}, u32[]{:S(2)}, u32[]{:S(2)}) collective-permute-start(f32[96,96]{1,0:T(8,128)S(1)} %add.14), channel_id=1, source_target_pairs={{0,1},{1,0},{2,3},{3,2},{4,5},{5,4},{6,7},{7,6},{8,9},{9,8},{10,11... | collective-permute-start | bytes 110600 | tf_op jit(solution)/shard_map/ppermute | solution.py:344
  78.5 2.6 %collective-permute-done.28 = f32[96,96]{1,0:T(8,128)S(1)} collective-permute-done((f32[96,96]{1,0:T(8,128)S(1)}, f32[96,96]{1,0:T(8,128)S(1)}, u32[]{:S(2)}, u32[]{:S(2)}) %collective-permute-start.28) | collective-permute-done | bytes 36896 | tf_op jit(solution)/shard_map/ppermute | solution.py:344
  81.1 1.6 %collective-permute-start.29 = (f32[96,96]{1,0:T(8,128)S(1)}, f32[96,96]{1,0:T(8,128)S(1)}, u32[]{:S(2)}, u32[]{:S(2)}) collective-permute-start(f32[96,96]{1,0:T(8,128)S(1)} %add.15.first), channel_id=1, source_target_pairs={{0,2},{1,3},{2,0},{3,1},{4,6},{5,7},{6,4},{7,5},{8,10},{9,11},{10,... | collective-permute-start | bytes 110600 | tf_op jit(solution)/shard_map/ppermute | solution.py:428
  82.6 1.6 %shard_map.64.values = bf16[288,2048]{1,0:T(8,128)(2,1)S(1)} custom-call(f32[96,256]{1,0:T(8,128)S(1)} %collective-permute-done.21.r0, f32[96,256]{1,0:T(8,128)S(1)} %collective-permute-done.22.r1, f32[96,256]{1,0:T(8,128)S(1)} %collective-permute-done.23.r2, f32[96,256]{1,0:T(8,128)S(1)} %collective-permute-done.24.r3, ...), custom_call_target="tpu_custom_call" | custom-call | tf_op jit(solution)/shard_map/pallas_call | solution.py:429
  84.2 1.0 %collective-permute-done.29.second = f32[96,96]{1,0:T(8,128)S(1)} collective-permute-done((f32[96,96]{1,0:T(8,128)S(1)}, f32[96,96]{1,0:T(8,128)S(1)}, u32[]{:S(2)}, u32[]{:S(2)}) %collective-permute-start.29) | collective-permute-done | bytes 36896 | tf_op jit(solution)/shard_map/ppermute | solution.py:428
  85.2 4.9 %shard_map.65 = f32[1,1,96,2048]{3,2,1,0:T(8,128)} custom-call(f32[96,96]{1,0:T(8,128)S(1)} %add.15.first, f32[96,96]{1,0:T(8,128)S(1)} %collective-permute-done.29.second, bf16[288,2048]{1,0:T(8,128)(2,1)S(1)} %shard_map.64.values), custom_call_target="tpu_custom_call" | custom-call | tf_op jit(solution)/shard_map/pallas_call | solution.py:431
  (36 shorter events, 0.1 us)
Async XLA Ops:
  0.7 0.7 copy-start
  9.1 4.6 %collective-permute-start = (f32[96,256]{1,0:T(8,128)S(1)}, f32[96,256]{1,0:T(8,128)S(1)}, u32[]{:S(2)}, u32[]{:S(2)}) collective-permute-start(f32[96,256]{1,0:T(8,128)S(1)} %get-tuple-element.39.refs_8_), channel_id=1, source_target_pairs={{0,4},{4,0},{8,12},{12,8},{16,20},{20,16},{24,28},{28,24},{1,5},{5... | collective-permute-start | bytes 294920 | tf_op jit(solution)/shard_map/ppermute | solution.py:360
  9.6 9.2 %collective-permute-start.2 = (f32[96,256]{1,0:T(8,128)S(1)}, f32[96,256]{1,0:T(8,128)S(1)}, u32[]{:S(2)}, u32[]{:S(2)}) collective-permute-start(f32[96,256]{1,0:T(8,128)S(1)} %get-tuple-element.40.refs_9_), channel_id=1, source_target_pairs={{0,3},{1,2},{2,1},{3,0},{4,7},{5,6},{6,5},{7,4},{8,11},{9,10},{10,... | collective-permute-start | bytes 294920 | tf_op jit(solution)/shard_map/ppermute | solution.py:361
  13.1 5.7 %collective-permute-start.3 = (f32[96,256]{1,0:T(8,128)S(1)}, f32[96,256]{1,0:T(8,128)S(1)}, u32[]{:S(2)}, u32[]{:S(2)}) collective-permute-start(f32[96,256]{1,0:T(8,128)S(1)} %get-tuple-element.41.refs_10_), channel_id=1, source_target_pairs={{0,1},{1,0},{2,3},{3,2},{4,5},{5,4},{6,7},{7,6},{8,9},{9,8},{10,11... | collective-permute-start | bytes 294920 | tf_op jit(solution)/shard_map/ppermute | solution.py:362
  13.7 5.2 %collective-permute-start.4 = (f32[96,256]{1,0:T(8,128)S(1)}, f32[96,256]{1,0:T(8,128)S(1)}, u32[]{:S(2)}, u32[]{:S(2)}) collective-permute-start(f32[96,256]{1,0:T(8,128)S(1)} %get-tuple-element.42.refs_11_), channel_id=1, source_target_pairs={{0,4},{4,0},{8,12},{12,8},{16,20},{20,16},{24,28},{28,24},{1,5},{5... | collective-permute-start | bytes 294920 | tf_op jit(solution)/shard_map/ppermute | solution.py:364
  13.7 5.2 %collective-permute-start.1 = (f32[96,256]{1,0:T(8,128)S(1)}, f32[96,256]{1,0:T(8,128)S(1)}, u32[]{:S(2)}, u32[]{:S(2)}) collective-permute-start(f32[96,256]{1,0:T(8,128)S(1)} %collective-permute-done), channel_id=1, source_target_pairs={{0,8},{8,16},{16,24},{24,28},{4,0},{12,4},{20,12},{28,20},{1,9},{9... | collective-permute-start | bytes 294920 | tf_op jit(solution)/shard_map/ppermute | solution.py:363
  15.2 24.5 %copy-start.1 = (s32[1,1,16,5]{2,1,3,0:T(1,128)S(1)}, s32[1,1,16,5]{2,1,3,0:T(1,128)}, u32[]{:S(2)}) copy-start(s32[1,1,16,5]{2,1,3,0:T(1,128)} %param.7) | copy-start | bytes 964
  19.5 2.1 %collective-permute-start.5 = (f32[96,256]{1,0:T(8,128)S(1)}, f32[96,256]{1,0:T(8,128)S(1)}, u32[]{:S(2)}, u32[]{:S(2)}) collective-permute-start(f32[96,256]{1,0:T(8,128)S(1)} %get-tuple-element.51.refs_12_), channel_id=1, source_target_pairs={{0,4},{4,0},{8,12},{12,8},{16,20},{20,16},{24,28},{28,24},{1,5},{5... | collective-permute-start | bytes 294920 | tf_op jit(solution)/shard_map/ppermute | solution.py:360
  19.6 24.8 %collective-permute-start.7 = (f32[96,256]{1,0:T(8,128)S(1)}, f32[96,256]{1,0:T(8,128)S(1)}, u32[]{:S(2)}, u32[]{:S(2)}) collective-permute-start(f32[96,256]{1,0:T(8,128)S(1)} %get-tuple-element.52.refs_13_), channel_id=1, source_target_pairs={{0,3},{1,2},{2,1},{3,0},{4,7},{5,6},{6,5},{7,4},{8,11},{9,10},{10,... | collective-permute-start | bytes 294920 | tf_op jit(solution)/shard_map/ppermute | solution.py:361
  21.1 23.3 %collective-permute-start.8 = (f32[96,256]{1,0:T(8,128)S(1)}, f32[96,256]{1,0:T(8,128)S(1)}, u32[]{:S(2)}, u32[]{:S(2)}) collective-permute-start(f32[96,256]{1,0:T(8,128)S(1)} %get-tuple-element.53.refs_14_), channel_id=1, source_target_pairs={{0,1},{1,0},{2,3},{3,2},{4,5},{5,4},{6,7},{7,6},{8,9},{9,8},{10,11... | collective-permute-start | bytes 294920 | tf_op jit(solution)/shard_map/ppermute | solution.py:362
  21.6 22.8 %collective-permute-start.9 = (f32[96,256]{1,0:T(8,128)S(1)}, f32[96,256]{1,0:T(8,128)S(1)}, u32[]{:S(2)}, u32[]{:S(2)}) collective-permute-start(f32[96,256]{1,0:T(8,128)S(1)} %get-tuple-element.54.refs_15_), channel_id=1, source_target_pairs={{0,4},{4,0},{8,12},{12,8},{16,20},{20,16},{24,28},{28,24},{1,5},{5... | collective-permute-start | bytes 294920 | tf_op jit(solution)/shard_map/ppermute | solution.py:364
  21.6 22.8 %collective-permute-start.6 = (f32[96,256]{1,0:T(8,128)S(1)}, f32[96,256]{1,0:T(8,128)S(1)}, u32[]{:S(2)}, u32[]{:S(2)}) collective-permute-start(f32[96,256]{1,0:T(8,128)S(1)} %collective-permute-done.5), channel_id=1, source_target_pairs={{0,8},{8,16},{16,24},{24,28},{4,0},{12,4},{20,12},{28,20},{1,9},{9... | collective-permute-start | bytes 294920 | tf_op jit(solution)/shard_map/ppermute | solution.py:363
  23.2 1.2 %collective-permute-start.10 = (f32[8,128]{1,0:T(8,128)S(1)}, f32[8,128]{1,0:T(8,128)S(1)}, u32[]{:S(2)}, u32[]{:S(2)}) collective-permute-start(f32[8,128]{1,0:T(8,128)S(1)} %get-tuple-element.50.refs_6_.refs_7_.own.peak), channel_id=1, source_target_pairs={{0,4},{4,0},{8,12},{12,8},{16,20},{20,16},{24,28},{28,24},{1,5},{5... | collective-permute-start | bytes 12296 | tf_op jit(solution)/shard_map/ppermute | solution.py:344
  24.4 3.6 %collective-permute-start.11 = (f32[8,128]{1,0:T(8,128)S(1)}, f32[8,128]{1,0:T(8,128)S(1)}, u32[]{:S(2)}, u32[]{:S(2)}) collective-permute-start(f32[8,128]{1,0:T(8,128)S(1)} %max.15), channel_id=1, source_target_pairs={{0,8},{4,12},{8,0},{12,4},{16,24},{20,28},{24,16},{28,20},{1,9},{5... | collective-permute-start | bytes 12296 | tf_op jit(solution)/shard_map/ppermute | solution.py:344
  28.0 4.5 %collective-permute-start.12 = (f32[8,128]{1,0:T(8,128)S(1)}, f32[8,128]{1,0:T(8,128)S(1)}, u32[]{:S(2)}, u32[]{:S(2)}) collective-permute-start(f32[8,128]{1,0:T(8,128)S(1)} %max.16), channel_id=1, source_target_pairs={{0,16},{4,20},{8,24},{12,28},{16,0},{20,4},{24,8},{28,12},{1,17},{... | collective-permute-start | bytes 12296 | tf_op jit(solution)/shard_map/ppermute | solution.py:344
  32.5 3.6 %collective-permute-start.13 = (f32[8,128]{1,0:T(8,128)S(1)}, f32[8,128]{1,0:T(8,128)S(1)}, u32[]{:S(2)}, u32[]{:S(2)}) collective-permute-start(f32[8,128]{1,0:T(8,128)S(1)} %max.17), channel_id=1, source_target_pairs={{0,1},{1,0},{2,3},{3,2},{4,5},{5,4},{6,7},{7,6},{8,9},{9,8},{10,11... | collective-permute-start | bytes 12296 | tf_op jit(solution)/shard_map/ppermute | solution.py:344
  36.1 3.6 %collective-permute-start.14 = (f32[8,128]{1,0:T(8,128)S(1)}, f32[8,128]{1,0:T(8,128)S(1)}, u32[]{:S(2)}, u32[]{:S(2)}) collective-permute-start(f32[8,128]{1,0:T(8,128)S(1)} %max.18), channel_id=1, source_target_pairs={{0,2},{1,3},{2,0},{3,1},{4,6},{5,7},{6,4},{7,5},{8,10},{9,11},{10,... | collective-permute-start | bytes 12296 | tf_op jit(solution)/shard_map/ppermute | solution.py:344
  45.1 3.2 %collective-permute-start.15 = (f32[96,256]{1,0:T(8,128)S(1)}, f32[96,256]{1,0:T(8,128)S(1)}, u32[]{:S(2)}, u32[]{:S(2)}) collective-permute-start(f32[96,256]{1,0:T(8,128)S(1)} %get-tuple-element.57), channel_id=1, source_target_pairs={{0,4},{4,0},{8,12},{12,8},{16,20},{20,16},{24,28},{28,24},{1,5},{5... | collective-permute-start | bytes 294920 | tf_op jit(solution)/shard_map/ppermute | solution.py:360
  45.2 9.9 %collective-permute-start.17 = (f32[96,256]{1,0:T(8,128)S(1)}, f32[96,256]{1,0:T(8,128)S(1)}, u32[]{:S(2)}, u32[]{:S(2)}) collective-permute-start(f32[96,256]{1,0:T(8,128)S(1)} %get-tuple-element.58), channel_id=1, source_target_pairs={{0,3},{1,2},{2,1},{3,0},{4,7},{5,6},{6,5},{7,4},{8,11},{9,10},{10,... | collective-permute-start | bytes 294920 | tf_op jit(solution)/shard_map/ppermute | solution.py:361
  47.7 7.4 %collective-permute-start.18 = (f32[96,256]{1,0:T(8,128)S(1)}, f32[96,256]{1,0:T(8,128)S(1)}, u32[]{:S(2)}, u32[]{:S(2)}) collective-permute-start(f32[96,256]{1,0:T(8,128)S(1)} %get-tuple-element.59), channel_id=1, source_target_pairs={{0,1},{1,0},{2,3},{3,2},{4,5},{5,4},{6,7},{7,6},{8,9},{9,8},{10,11... | collective-permute-start | bytes 294920 | tf_op jit(solution)/shard_map/ppermute | solution.py:362
  48.2 6.8 %collective-permute-start.19 = (f32[96,256]{1,0:T(8,128)S(1)}, f32[96,256]{1,0:T(8,128)S(1)}, u32[]{:S(2)}, u32[]{:S(2)}) collective-permute-start(f32[96,256]{1,0:T(8,128)S(1)} %get-tuple-element.60), channel_id=1, source_target_pairs={{0,4},{4,0},{8,12},{12,8},{16,20},{20,16},{24,28},{28,24},{1,5},{5... | collective-permute-start | bytes 294920 | tf_op jit(solution)/shard_map/ppermute | solution.py:364
  48.2 6.8 %collective-permute-start.16 = (f32[96,256]{1,0:T(8,128)S(1)}, f32[96,256]{1,0:T(8,128)S(1)}, u32[]{:S(2)}, u32[]{:S(2)}) collective-permute-start(f32[96,256]{1,0:T(8,128)S(1)} %collective-permute-done.15), channel_id=1, source_target_pairs={{0,8},{8,16},{16,24},{24,28},{4,0},{12,4},{20,12},{28,20},{1,9},{9... | collective-permute-start | bytes 294920 | tf_op jit(solution)/shard_map/ppermute | solution.py:363
  55.7 2.1 %collective-permute-start.20 = (f32[96,256]{1,0:T(8,128)S(1)}, f32[96,256]{1,0:T(8,128)S(1)}, u32[]{:S(2)}, u32[]{:S(2)}) collective-permute-start(f32[96,256]{1,0:T(8,128)S(1)} %get-tuple-element.64), channel_id=1, source_target_pairs={{0,4},{4,0},{8,12},{12,8},{16,20},{20,16},{24,28},{28,24},{1,5},{5... | collective-permute-start | bytes 294920 | tf_op jit(solution)/shard_map/ppermute | solution.py:360
  55.8 9.1 %collective-permute-start.22 = (f32[96,256]{1,0:T(8,128)S(1)}, f32[96,256]{1,0:T(8,128)S(1)}, u32[]{:S(2)}, u32[]{:S(2)}) collective-permute-start(f32[96,256]{1,0:T(8,128)S(1)} %get-tuple-element.65), channel_id=1, source_target_pairs={{0,3},{1,2},{2,1},{3,0},{4,7},{5,6},{6,5},{7,4},{8,11},{9,10},{10,... | collective-permute-start | bytes 294920 | tf_op jit(solution)/shard_map/ppermute | solution.py:361
  57.2 7.6 %collective-permute-start.23 = (f32[96,256]{1,0:T(8,128)S(1)}, f32[96,256]{1,0:T(8,128)S(1)}, u32[]{:S(2)}, u32[]{:S(2)}) collective-permute-start(f32[96,256]{1,0:T(8,128)S(1)} %get-tuple-element.66), channel_id=1, source_target_pairs={{0,1},{1,0},{2,3},{3,2},{4,5},{5,4},{6,7},{7,6},{8,9},{9,8},{10,11... | collective-permute-start | bytes 294920 | tf_op jit(solution)/shard_map/ppermute | solution.py:362
  57.8 7.1 %collective-permute-start.24 = (f32[96,256]{1,0:T(8,128)S(1)}, f32[96,256]{1,0:T(8,128)S(1)}, u32[]{:S(2)}, u32[]{:S(2)}) collective-permute-start(f32[96,256]{1,0:T(8,128)S(1)} %get-tuple-element.67), channel_id=1, source_target_pairs={{0,4},{4,0},{8,12},{12,8},{16,20},{20,16},{24,28},{28,24},{1,5},{5... | collective-permute-start | bytes 294920 | tf_op jit(solution)/shard_map/ppermute | solution.py:364
  57.8 7.1 %collective-permute-start.21 = (f32[96,256]{1,0:T(8,128)S(1)}, f32[96,256]{1,0:T(8,128)S(1)}, u32[]{:S(2)}, u32[]{:S(2)}) collective-permute-start(f32[96,256]{1,0:T(8,128)S(1)} %collective-permute-done.20), channel_id=1, source_target_pairs={{0,8},{8,16},{16,24},{24,28},{4,0},{12,4},{20,12},{28,20},{1,9},{9... | collective-permute-start | bytes 294920 | tf_op jit(solution)/shard_map/ppermute | solution.py:363
  65.9 1.3 %collective-permute-start.25 = (f32[96,96]{1,0:T(8,128)S(1)}, f32[96,96]{1,0:T(8,128)S(1)}, u32[]{:S(2)}, u32[]{:S(2)}) collective-permute-start(f32[96,96]{1,0:T(8,128)S(1)} %shard_map.63), channel_id=1, source_target_pairs={{0,4},{4,0},{8,12},{12,8},{16,20},{20,16},{24,28},{28,24},{1,5},{5... | collective-permute-start | bytes 110600 | tf_op jit(solution)/shard_map/ppermute | solution.py:344
  67.2 4.2 %collective-permute-start.26 = (f32[96,96]{1,0:T(8,128)S(1)}, f32[96,96]{1,0:T(8,128)S(1)}, u32[]{:S(2)}, u32[]{:S(2)}) collective-permute-start(f32[96,96]{1,0:T(8,128)S(1)} %add.12), channel_id=1, source_target_pairs={{0,8},{4,12},{8,0},{12,4},{16,24},{20,28},{24,16},{28,20},{1,9},{5... | collective-permute-start | bytes 110600 | tf_op jit(solution)/shard_map/ppermute | solution.py:344
  71.4 5.5 %collective-permute-start.27 = (f32[96,96]{1,0:T(8,128)S(1)}, f32[96,96]{1,0:T(8,128)S(1)}, u32[]{:S(2)}, u32[]{:S(2)}) collective-permute-start(f32[96,96]{1,0:T(8,128)S(1)} %add.13), channel_id=1, source_target_pairs={{0,16},{4,20},{8,24},{12,28},{16,0},{20,4},{24,8},{28,12},{1,17},{... | collective-permute-start | bytes 110600 | tf_op jit(solution)/shard_map/ppermute | solution.py:344
  76.9 4.2 %collective-permute-start.28 = (f32[96,96]{1,0:T(8,128)S(1)}, f32[96,96]{1,0:T(8,128)S(1)}, u32[]{:S(2)}, u32[]{:S(2)}) collective-permute-start(f32[96,96]{1,0:T(8,128)S(1)} %add.14), channel_id=1, source_target_pairs={{0,1},{1,0},{2,3},{3,2},{4,5},{5,4},{6,7},{7,6},{8,9},{9,8},{10,11... | collective-permute-start | bytes 110600 | tf_op jit(solution)/shard_map/ppermute | solution.py:344
  81.1 4.2 %collective-permute-start.29 = (f32[96,96]{1,0:T(8,128)S(1)}, f32[96,96]{1,0:T(8,128)S(1)}, u32[]{:S(2)}, u32[]{:S(2)}) collective-permute-start(f32[96,96]{1,0:T(8,128)S(1)} %add.15.first), channel_id=1, source_target_pairs={{0,2},{1,3},{2,0},{3,1},{4,6},{5,7},{6,4},{7,5},{8,10},{9,11},{10,... | collective-permute-start | bytes 110600 | tf_op jit(solution)/shard_map/ppermute | solution.py:428
where the time goes:
time: 90.4 us; the launch traced here: 90.2 us
  Pallas kernels  35.9 us (40%)
  starting transfers between devices  30.9 us (34%)
  waiting for transfers between devices  21.7 us (24%)
    ppermute x9, waiting for transfers between devices, spread(): value = combine(value, lax.ppermute(value, axis, pairs))  20.6 us
    pallas_call x3, Pallas kernels, per_device(): call(functools.partial(field_kernel, number), [field, field, edge_field]...  15.3 us
    ppermute x9, starting transfers between devices, spread(): value = combine(value, lax.ppermute(value, axis, pairs))  11 us
    ppermute x4, starting transfers between devices, exchange(): y_far = lax.ppermute(y_far, 'gy', far_pairs(sizes[1]))  9 us
    pallas_call x1, Pallas kernels, per_device(): call(functools.partial(first_kernel, sizes), [shape(cells, 4 * edges, dty...  7.7 us
    ppermute x4, starting transfers between devices, exchange(): x_far = lax.ppermute(x_far, 'gx', turn_pairs(sizes[0]))  6.37 us
    pallas_call x1, Pallas kernels, per_device(): call(functools.partial(encode_kernel, root), shape(1, 1, vecs, cells), [V...  4.94 us
    pallas_call x1, Pallas kernels, per_device(): call(open_kernel, [field, edge_field, shape(4 * edges, 4 * edges, dtype=B...  3.56 us
  transfers between devices with their start and end apart: 30, of which 10 were waited for; matrix products, arithmetic and copies ran while one was open for 0% of the time, Pallas kernels for 23%

commit v1 on v0

--- a/solution.py
+++ b/solution.py
@@ -51,6 +51,13 @@
     return product[:, :half] + product[:, half:]
 
 
+def total(terms):
+    terms = list(terms)
+    while len(terms) > 1:
+        terms = [a + b for a, b in zip(terms[::2], terms[1::2])] + terms[len(terms) & ~1 :]
+    return terms[0]
+
+
 def near_pairs(size):
     return [(i, i ^ 1) for i in range(size)]
 
@@ -93,7 +100,7 @@
 def first_kernel(sizes, cols, counts, lists_any, basis_any, weights_any, *refs):
     place, stored, begin, degree, peak, marks = refs[:6]
     outs = refs[6:10]
-    lists, basis, weights, sems = refs[10:]
+    lists, basis, weights, hits, sems = refs[10:]
     blocks, slots = weights.shape[:2]
     cells, edges = place.shape
     width = edges // len(outs)
@@ -104,11 +111,14 @@
     blocks_in = [
         pltpu.make_async_copy(weights_any.at[0, 0, m], weights.at[m], sems.at[m]) for m in range(blocks)
     ]
-    for load in loads + blocks_in:
+    for load in loads:
         load.start()
     count = counts[...]
     degree[...] = jnp.zeros_like(degree)
-    loads[0].wait()
+    for load in loads:
+        load.wait()
+    for load in blocks_in:
+        load.start()
     order = []
     for axis, shift in SIDES:
         dim = ("gx", "gy").index(axis)
@@ -121,38 +131,39 @@
     marks[...] = jnp.broadcast_to(targets, marks.shape)
     for start in range(0, cells, CHUNK):
         spot = lax.broadcasted_iota(jnp.int32, (CHUNK, edges), 0) + start
-        place[start : start + CHUNK] = (spot == targets).astype(F32).astype(BF16)
-    loads[1].wait()
+        equal = (spot == targets).astype(F32)
+        place[start : start + CHUNK] = equal.astype(BF16)
+        hits[start : start + CHUNK] = total(
+            equal[:, other : other + LANES] for other in range(0, edges, LANES)
+        ).astype(BF16)
     begin[...] = jnp.where(live_lanes(count, 0, cells), basis[...], 0.0)
     picked = folded(dot(stacked(begin[...]), place[...]))
     for i, out in enumerate(outs):
         out[...] = picked[:, i * width : (i + 1) * width]
-    joined = dot_nt(jnp.ones((16, edges), BF16), place[...])[:8]
+    joined = dot_nt(jnp.ones((16, LANES), BF16), hits[...])[:8]
+    rows = lax.broadcasted_iota(jnp.int32, (LANES, LANES), 0)
     for m in range(blocks):
         blocks_in[m].wait()
+        live = rows + m * LANES < count
         for j in range(slots):
-            hi, lo = split(weights[m, j])
+            value = weights[m, j]
+            hi, lo = split(value)
             stored[m, 0:LANES, j * LANES : (j + 1) * LANES] = hi
             stored[m, LANES : 2 * LANES, j * LANES : (j + 1) * LANES] = lo
-        live = live_lanes(count, m * LANES, LANES)
-        ones = jnp.broadcast_to(live.astype(F32), (16, LANES)).astype(BF16)
-        sums = dot(jnp.concatenate([ones, ones], axis=1), stored[m])[:8]
-        for j in range(slots):
+            kept = jnp.where(live, value, 0.0)
             spot = pl.ds(pl.multiple_of(cols[0, j, 0, m] * LANES, LANES), LANES)
-            degree[:, spot] += sums[:, j * LANES : (j + 1) * LANES]
-    value = jnp.where(live_lanes(count, 0, cells), degree[...] + joined, 0.0)
+            degree[:, spot] += total(kept[i : i + 8] for i in range(0, LANES, 8))
+    value = jnp.sum(degree[...], axis=0, keepdims=True) + joined
+    value = jnp.where(live_lanes(count, 0, cells), value, 0.0)
     degree[...] = value
     peak[...] = jnp.full(peak.shape, jnp.max(value), F32)
 
 
-def multiply(cols, values, stored, inside):
-    blocks, _, width = stored.shape
-    inside[...] = jnp.zeros_like(inside)
-    for m in range(blocks):
-        product = folded(dot(left_rows(values[:, m * LANES : (m + 1) * LANES]), stored[m]))
-        for j in range(width // LANES):
-            spot = pl.ds(pl.multiple_of(cols[0, j, 0, m] * LANES, LANES), LANES)
-            inside[:, spot] += product[:, j * LANES : (j + 1) * LANES]
+def multiply(cols, m, value, stored, inside):
+    product = folded(dot(left_rows(value), stored[m]))
+    for j in range(stored.shape[2] // LANES):
+        spot = pl.ds(pl.multiple_of(cols[0, j, 0, m] * LANES, LANES), LANES)
+        inside[:, spot] += product[:, j * LANES : (j + 1) * LANES]
 
 
 def gather(values, place):
@@ -167,7 +178,7 @@
     return [slice(start, start + CHUNK) for start in range(0, cells, CHUNK)]
 
 
-def open_kernel(cols, counts, begin, stored, degree, place, marks, local, edge_local, same, inside):
+def open_kernel(cols, counts, begin, stored, degree, place, marks, local, edge_local, same, back, inside):
     cells, edges = place.shape
     targets = marks[0:1]
     for start in range(0, edges, LANES):
@@ -177,7 +188,13 @@
         for other in range(0, edges, LANES):
             equal = down == targets[:, other : other + LANES]
             same[start : start + LANES, other : other + LANES] = equal.astype(F32).astype(BF16)
-    multiply(cols, begin, stored, inside)
+        lane = lax.broadcasted_iota(jnp.int32, (LANES, LANES), 1)
+        for other in range(0, cells, LANES):
+            equal = down == lane + other
+            back[start : start + LANES, other : other + LANES] = equal.astype(F32).astype(BF16)
+    inside[...] = jnp.zeros_like(inside)
+    for m in range(cells // LANES):
+        multiply(cols, m, begin[:, m * LANES : (m + 1) * LANES], stored, inside)
     for part in chunks(cells):
         live = live_lanes(counts[...], part.start, CHUNK)
         local[:, part] = degree[0:1, part] * begin[:, part] - jnp.where(live, inside[:, part], 0.0)
@@ -209,26 +226,32 @@
     return first, second
 
 
-def field_kernel(number, cols, counts, r0, r1, r2, r3, local, stored, degree, place, own, peak, begin, once, *refs):
+def field_kernel(
+    number, cols, counts, r0, r1, r2, r3, local, stored, degree, place, back, own, peak, begin, once, *refs
+):
     field, later, edge_local = refs[:3]
     inside = refs[-1]
     cells = place.shape[0]
     top = own[0:1, 0:1]
     centre, half = scalars(peak)
     arrived = stacked(joined_up((r0, r1, r2, r3)))
+    inside[...] = jnp.zeros_like(inside)
     for part in chunks(cells):
-        crossed = folded(dot_nt(arrived, place[part]))
+        crossed = folded(dot(arrived, back[:, part]))
         if number == 0:
-            field[:, part] = (local[:, part] - crossed) / top
+            value = (local[:, part] - crossed) / top
         elif number == 1:
-            first, field[:, part] = second_field(
+            first, value = second_field(
                 centre, half, top, local[:, part] - crossed / top, once[:, part] * top, begin[:, part]
             )
             later[:, part] = first
         else:
-            field[:, part] = local[:, part] - (2.0 / half) * crossed
+            value = local[:, part] - (2.0 / half) * crossed
             later[:, part] = begin[:, part]
-    multiply(cols, field, stored, inside)
+        field[:, part] = value
+        for start in range(0, CHUNK, LANES):
+            block = (part.start + start) // LANES
+            multiply(cols, block, value[:, start : start + LANES], stored, inside)
     for part in chunks(cells):
         live = live_lanes(counts[...], part.start, CHUNK)
         kept = jnp.where(live, inside[:, part], 0.0)
@@ -251,11 +274,11 @@
     gram[...] = base[...] - mixed - mixed.T
 
 
-def last_kernel(r0, r1, r2, r3, local, place, peak, terms):
+def last_kernel(r0, r1, r2, r3, local, back, peak, terms):
     _, half = scalars(peak)
     arrived = stacked(joined_up((r0, r1, r2, r3)))
-    for part in chunks(place.shape[0]):
-        hi, lo = split(local[:, part] - (2.0 / half) * folded(dot_nt(arrived, place[part])))
+    for part in chunks(back.shape[1]):
+        hi, lo = split(local[:, part] - (2.0 / half) * folded(dot(arrived, back[:, part])))
         terms[:, part] = jnp.concatenate([hi, lo, hi], axis=0)
 
 
@@ -280,13 +303,6 @@
     return [
         [far[i][j] * near[i] for j in range(i)] + [near[i]] for i in range(size)
     ]
-
-
-def total(terms):
-    terms = list(terms)
-    while len(terms) > 1:
-        terms = [a + b for a, b in zip(terms[::2], terms[1::2])] + terms[len(terms) & ~1 :]
-    return terms[0]
 
 
 def encode_kernel(root, first, second, values, out):
@@ -381,6 +397,7 @@
             pltpu.VMEM((4, edges), jnp.int32),
             pltpu.VMEM((vecs, cells), F32),
             pltpu.VMEM((blocks, slots, block, block), F32),
+            pltpu.VMEM((cells, LANES), BF16),
             pltpu.SemaphoreType.DMA((blocks + 2,)),
         ],
     )(
@@ -393,9 +410,14 @@
     ]
     arrived = exchange(outgoing)
     peak = spread(own, jnp.maximum, stages)
-    local, edge_local, same = call(
+    local, edge_local, same, back = call(
         open_kernel,
-        [field, edge_field, shape(4 * edges, 4 * edges, dtype=BF16)],
+        [
+            field,
+            edge_field,
+            shape(4 * edges, 4 * edges, dtype=BF16),
+            shape(4 * edges, cells, dtype=BF16),
+        ],
         [SM] + [VM] * 6,
         scratch_shapes=scratch,
     )(cols, live_counts, begin, stored, degree, place, marks)
@@ -416,9 +438,9 @@
         now, local, edge_local, *base = call(
             functools.partial(field_kernel, number),
             [field, field, edge_field] + [shape(vecs, vecs)] * (number == 2),
-            [SM] + [VM] * 13,
+            [SM] + [VM] * 14,
             scratch_shapes=scratch,
-        )(cols, live_counts, *arrived, local, stored, degree, place, own, bound, *earlier)
+        )(cols, live_counts, *arrived, local, stored, degree, place, back, own, bound, *earlier)
         earlier = [begin, now] if number == 0 else [now, now]
         arrived = coming
 
@@ -426,7 +448,7 @@
     gram = spread(gram, jnp.add, stages[:-1])
     axis, bit = stages[-1]
     other = lax.ppermute(gram, axis, xor_pairs(lax.axis_size(axis), bit))
-    now = call(last_kernel, shape(3 * vecs, cells, dtype=BF16), [VM] * 7)(*arrived, local, place, peak)
+    now = call(last_kernel, shape(3 * vecs, cells, dtype=BF16), [VM] * 7)(*arrived, local, back, peak)
     root = math.sqrt(cells * sizes[0] * sizes[1])
     return call(functools.partial(encode_kernel, root), shape(1, 1, vecs, cells), [VM] * 3)(gram, other, now)
 

time: 90.4 us -> 89.4 us (0.989)
  starting transfers between devices: 30.9 us -> 29.9 us
    pallas_call x1, Pallas kernels: 7.7 us -> 6.05 us  [per_device(): call(functools.partial(first_kernel, sizes), [shape(cells, 4 * edges, dty...]
    pallas_call x1, Pallas kernels: 3.56 us -> 4.64 us  [per_device(): call(open_kernel, [field, edge_field, shape(4 * edges, 4 * edges, dtype=B...]
    ppermute x4, starting transfers between devices: 6.37 us -> 5.35 us  [exchange(): x_far = lax.ppermute(x_far, 'gx', turn_pairs(sizes[0]))]
    pallas_call x3, Pallas kernels: 15.3 us -> 16.3 us  [per_device(): call(functools.partial(field_kernel, number), [field, field, edge_field]...]
  transfers between devices with their start and end apart: 30 -> 30, of which waited for: 10 -> 10; matrix products, arithmetic and copies ran while one was open for 0% -> 0% of each run, Pallas kernels for 23% -> 25%
where the time goes in v1:
time: 89.4 us; the launch traced here: 89.2 us
  Pallas kernels  36 us (40%)
  starting transfers between devices  29.9 us (33%)
  waiting for transfers between devices  21.6 us (24%)
  between operations  0.92 us (1%)
    ppermute x9, waiting for transfers between devices, spread(): value = combine(value, lax.ppermute(value, axis, pairs))  20.1 us
    pallas_call x3, Pallas kernels, per_device(): call(functools.partial(field_kernel, number), [field, field, edge_field]...  16.3 us
    ppermute x9, starting transfers between devices, spread(): value = combine(value, lax.ppermute(value, axis, pairs))  11 us
    ppermute x4, starting transfers between devices, exchange(): y_far = lax.ppermute(y_far, 'gy', far_pairs(sizes[1]))  8.97 us
    pallas_call x1, Pallas kernels, per_device(): call(functools.partial(first_kernel, sizes), [shape(cells, 4 * edges, dty...  6.05 us
    ppermute x4, starting transfers between devices, exchange(): x_far = lax.ppermute(x_far, 'gx', turn_pairs(sizes[0]))  5.35 us
    pallas_call x1, Pallas kernels, per_device(): call(functools.partial(encode_kernel, root), shape(1, 1, vecs, cells), [V...  4.94 us
    pallas_call x1, Pallas kernels, per_device(): call(open_kernel, [field, edge_field, shape(4 * edges, 4 * edges, dtype=B...  4.64 us
  transfers between devices with their start and end apart: 30, of which 10 were waited for; matrix products, arithmetic and copies ran while one was open for 0% of the time, Pallas kernels for 25%

profile of v1, /device:TPU:0, one launch (start us, length us, event | category | flops | bytes accessed | tf_op | source)
XLA Modules:
  0.0 89.2 jit_solution(12220560611418153335)
XLA Ops:
  0.7 0.7 copy-done
  1.3 6.1 %shard_map.55 = (bf16[2048,1024]{1,0:T(8,128)(2,1)S(1)}, bf16[16,256,640]{2,1,0:T(8,128)(2,1)S(1)}, f32[96,2048]{1,0:T(8,128)S(1)}, f32[8,2048]{1,0:T(8,128)S(1)...) custom-call(s32[1,5,1,16]{3,2,1,0:T(1,128)S(1)} %bitcast.1, ...), custom_call_target="tpu_custom_call" | custom-call | tf_op jit(solution)/shard_map/pallas_call | solution.py:384
  7.4 0.6 collective-permute-start
  8.0 3.5 %collective-permute-start.2 = (f32[96,256]{1,0:T(8,128)S(1)}, f32[96,256]{1,0:T(8,128)S(1)}, u32[]{:S(2)}, u32[]{:S(2)}) collective-permute-start(f32[96,256]{1,0:T(8,128)S(1)} %get-tuple-element.41.refs_9_), channel_id=1, source_target_pairs={{0,3},{1,2},{2,1},{3,0},{4,7},{5,6},{6,5},{7,4},{8,11},{9,10},{10,... | collective-permute-start | bytes 294920 | tf_op jit(solution)/shard_map/ppermute | solution.py:377
  11.5 0.5 collective-permute-start.3
  12.0 0.0 collective-permute-start.4
  12.0 1.6 %collective-permute-start.1 = (f32[96,256]{1,0:T(8,128)S(1)}, f32[96,256]{1,0:T(8,128)S(1)}, u32[]{:S(2)}, u32[]{:S(2)}) collective-permute-start(f32[96,256]{1,0:T(8,128)S(1)} %collective-permute-done), channel_id=1, source_target_pairs={{0,8},{8,16},{16,24},{24,28},{4,0},{12,4},{20,12},{28,20},{1,9},{9... | collective-permute-start | bytes 294920 | tf_op jit(solution)/shard_map/ppermute | solution.py:379
  13.6 4.6 %shard_map.56 = (f32[96,2048]{1,0:T(8,128)S(1)}, f32[96,1024]{1,0:T(8,128)S(1)}, bf16[1024,1024]{1,0:T(8,128)(2,1)S(1)}, bf16[1024,2048]{1,0:T(8,128)(2,1)S(1)}) custom-call(s32[1,5,1,16]{3,2,1,0:T(1,128)S(1)} %bitcast.2, s32[1,1]{1,0:T(1,128)S(6)} %copy.6.counts, f32[96,2048]{1,0:T(8,128)S(1)} %get-tuple-element.44.begin.once, ...), custom_call_target="tpu_custom_call" | custom-call | tf_op jit(solution)/shard_map/pallas_call | solution.py:413
  18.3 0.6 shard_map.57
  18.9 0.1 collective-permute-start.5
  19.0 1.5 %collective-permute-start.7 = (f32[96,256]{1,0:T(8,128)S(1)}, f32[96,256]{1,0:T(8,128)S(1)}, u32[]{:S(2)}, u32[]{:S(2)}) collective-permute-start(f32[96,256]{1,0:T(8,128)S(1)} %get-tuple-element.53.refs_13_), channel_id=1, source_target_pairs={{0,3},{1,2},{2,1},{3,0},{4,7},{5,6},{6,5},{7,4},{8,11},{9,10},{10,... | collective-permute-start | bytes 294920 | tf_op jit(solution)/shard_map/ppermute | solution.py:377
  20.5 0.5 collective-permute-start.8
  21.0 1.6 %collective-permute-start.6 = (f32[96,256]{1,0:T(8,128)S(1)}, f32[96,256]{1,0:T(8,128)S(1)}, u32[]{:S(2)}, u32[]{:S(2)}) collective-permute-start(f32[96,256]{1,0:T(8,128)S(1)} %collective-permute-done.5), channel_id=1, source_target_pairs={{0,8},{8,16},{16,24},{24,28},{4,0},{12,4},{20,12},{28,20},{1,9},{9... | collective-permute-start | bytes 294920 | tf_op jit(solution)/shard_map/ppermute | solution.py:379
  22.6 1.2 %collective-permute-done.10 = f32[8,128]{1,0:T(8,128)S(1)} collective-permute-done((f32[8,128]{1,0:T(8,128)S(1)}, f32[8,128]{1,0:T(8,128)S(1)}, u32[]{:S(2)}, u32[]{:S(2)}) %collective-permute-start.10) | collective-permute-done | bytes 4128 | tf_op jit(solution)/shard_map/ppermute | solution.py:360
  23.8 1.5 %collective-permute-start.11 = (f32[8,128]{1,0:T(8,128)S(1)}, f32[8,128]{1,0:T(8,128)S(1)}, u32[]{:S(2)}, u32[]{:S(2)}) collective-permute-start(f32[8,128]{1,0:T(8,128)S(1)} %max.15), channel_id=1, source_target_pairs={{0,8},{4,12},{8,0},{12,4},{16,24},{20,28},{24,16},{28,20},{1,9},{5... | collective-permute-start | bytes 12296 | tf_op jit(solution)/shard_map/ppermute | solution.py:360
  25.3 2.1 %collective-permute-done.11 = f32[8,128]{1,0:T(8,128)S(1)} collective-permute-done((f32[8,128]{1,0:T(8,128)S(1)}, f32[8,128]{1,0:T(8,128)S(1)}, u32[]{:S(2)}, u32[]{:S(2)}) %collective-permute-start.11) | collective-permute-done | bytes 4128 | tf_op jit(solution)/shard_map/ppermute | solution.py:360
  27.4 1.6 %collective-permute-start.12 = (f32[8,128]{1,0:T(8,128)S(1)}, f32[8,128]{1,0:T(8,128)S(1)}, u32[]{:S(2)}, u32[]{:S(2)}) collective-permute-start(f32[8,128]{1,0:T(8,128)S(1)} %max.16), channel_id=1, source_target_pairs={{0,16},{4,20},{8,24},{12,28},{16,0},{20,4},{24,8},{28,12},{1,17},{... | collective-permute-start | bytes 12296 | tf_op jit(solution)/shard_map/ppermute | solution.py:360
  29.0 2.9 %collective-permute-done.12 = f32[8,128]{1,0:T(8,128)S(1)} collective-permute-done((f32[8,128]{1,0:T(8,128)S(1)}, f32[8,128]{1,0:T(8,128)S(1)}, u32[]{:S(2)}, u32[]{:S(2)}) %collective-permute-start.12) | collective-permute-done | bytes 4128 | tf_op jit(solution)/shard_map/ppermute | solution.py:360
  31.9 1.5 %collective-permute-start.13 = (f32[8,128]{1,0:T(8,128)S(1)}, f32[8,128]{1,0:T(8,128)S(1)}, u32[]{:S(2)}, u32[]{:S(2)}) collective-permute-start(f32[8,128]{1,0:T(8,128)S(1)} %max.17), channel_id=1, source_target_pairs={{0,1},{1,0},{2,3},{3,2},{4,5},{5,4},{6,7},{7,6},{8,9},{9,8},{10,11... | collective-permute-start | bytes 12296 | tf_op jit(solution)/shard_map/ppermute | solution.py:360
  33.4 2.1 %collective-permute-done.13 = f32[8,128]{1,0:T(8,128)S(1)} collective-permute-done((f32[8,128]{1,0:T(8,128)S(1)}, f32[8,128]{1,0:T(8,128)S(1)}, u32[]{:S(2)}, u32[]{:S(2)}) %collective-permute-start.13) | collective-permute-done | bytes 4128 | tf_op jit(solution)/shard_map/ppermute | solution.py:360
  35.5 1.5 %collective-permute-start.14 = (f32[8,128]{1,0:T(8,128)S(1)}, f32[8,128]{1,0:T(8,128)S(1)}, u32[]{:S(2)}, u32[]{:S(2)}) collective-permute-start(f32[8,128]{1,0:T(8,128)S(1)} %max.18), channel_id=1, source_target_pairs={{0,2},{1,3},{2,0},{3,1},{4,6},{5,7},{6,4},{7,5},{8,10},{9,11},{10,... | collective-permute-start | bytes 12296 | tf_op jit(solution)/shard_map/ppermute | solution.py:360
  37.0 2.1 %collective-permute-done.14 = f32[8,128]{1,0:T(8,128)S(1)} collective-permute-done((f32[8,128]{1,0:T(8,128)S(1)}, f32[8,128]{1,0:T(8,128)S(1)}, u32[]{:S(2)}, u32[]{:S(2)}) %collective-permute-start.14) | collective-permute-done | bytes 4128 | tf_op jit(solution)/shard_map/ppermute | solution.py:360
  39.1 5.1 %shard_map.58 = (f32[96,2048]{1,0:T(8,128)S(1)}, f32[96,2048]{1,0:T(8,128)S(1)}, f32[96,1024]{1,0:T(8,128)S(1)}) custom-call(s32[1,5,1,16]{3,2,1,0:T(1,128)S(1)} %bitcast.3, s32[1,1]{1,0:T(1,128)S(6)} %copy.6.counts, f32[96,256]{1,0:T(8,128)S(1)} %collective-permute-done.1.refs_0_.r0, f32[96,256]{1,0:T(8,128)S(1)} %collective-permute-done.2.refs_1_.r1, ...), custom_call_target="tpu_custom_call" | custom-call | tf_op jit(solution)/shard_map/pallas_call | solution.py:438
  44.3 0.8 shard_map.59
  45.1 0.1 collective-permute-start.15
  45.2 2.5 %collective-permute-start.17 = (f32[96,256]{1,0:T(8,128)S(1)}, f32[96,256]{1,0:T(8,128)S(1)}, u32[]{:S(2)}, u32[]{:S(2)}) collective-permute-start(f32[96,256]{1,0:T(8,128)S(1)} %get-tuple-element.60), channel_id=1, source_target_pairs={{0,3},{1,2},{2,1},{3,0},{4,7},{5,6},{6,5},{7,4},{8,11},{9,10},{10,... | collective-permute-start | bytes 294920 | tf_op jit(solution)/shard_map/ppermute | solution.py:377
  47.7 0.5 collective-permute-start.18
  48.2 1.6 %collective-permute-start.16 = (f32[96,256]{1,0:T(8,128)S(1)}, f32[96,256]{1,0:T(8,128)S(1)}, u32[]{:S(2)}, u32[]{:S(2)}) collective-permute-start(f32[96,256]{1,0:T(8,128)S(1)} %collective-permute-done.15), channel_id=1, source_target_pairs={{0,8},{8,16},{16,24},{24,28},{4,0},{12,4},{20,12},{28,20},{1,9},{9... | collective-permute-start | bytes 294920 | tf_op jit(solution)/shard_map/ppermute | solution.py:379
  49.8 5.5 %shard_map.60 = (f32[96,2048]{1,0:T(8,128)S(1)}, f32[96,2048]{1,0:T(8,128)S(1)}, f32[96,1024]{1,0:T(8,128)S(1)}) custom-call(s32[1,5,1,16]{3,2,1,0:T(1,128)S(1)} %bitcast.4, s32[1,1]{1,0:T(1,128)S(6)} %copy.6.counts, f32[96,256]{1,0:T(8,128)S(1)} %collective-permute-done.6.refs_0_.r0, f32[96,256]{1,0:T(8,128)S(1)} %collective-permute-done.7.refs_1_.r1, ...), custom_call_target="tpu_custom_call" | custom-call | tf_op jit(solution)/shard_map/pallas_call | solution.py:438
  55.3 0.6 shard_map.61
  56.0 0.1 collective-permute-start.20
  56.1 1.5 %collective-permute-start.22 = (f32[96,256]{1,0:T(8,128)S(1)}, f32[96,256]{1,0:T(8,128)S(1)}, u32[]{:S(2)}, u32[]{:S(2)}) collective-permute-start(f32[96,256]{1,0:T(8,128)S(1)} %get-tuple-element.67), channel_id=1, source_target_pairs={{0,3},{1,2},{2,1},{3,0},{4,7},{5,6},{6,5},{7,4},{8,11},{9,10},{10,... | collective-permute-start | bytes 294920 | tf_op jit(solution)/shard_map/ppermute | solution.py:377
  57.5 0.5 collective-permute-start.23
  58.1 0.6 collective-permute-start.21
  58.7 5.7 %shard_map.62 = (f32[96,2048]{1,0:T(8,128)}, f32[96,2048]{1,0:T(8,128)S(1)}, f32[96,1024]{1,0:T(8,128)S(1)}, f32[96,96]{1,0:T(8,128)S(1)}) custom-call(s32[1,5,1,16]{3,2,1,0:T(1,128)S(1)} %bitcast.5, s32[1,1]{1,0:T(1,128)S(6)} %copy.6.counts, f32[96,256]{1,0:T(8,128)S(1)} %collective-permute-done.16.refs_0_.r0, ...), custom_call_target="tpu_custom_call" | custom-call | tf_op jit(solution)/shard_map/pallas_call | solution.py:438
  64.4 1.0 %shard_map.63 = f32[96,96]{1,0:T(8,128)S(1)} custom-call(f32[96,256]{1,0:T(8,128)S(1)} %collective-permute-done.21.r0, f32[96,256]{1,0:T(8,128)S(1)} %collective-permute-done.22.r1, f32[96,256]{1,0:T(8,128)S(1)} %collective-permute-done.23.r2, f32[96,256]{1,0:T(8,128)S(1)} %collective-permute-done.24.r3, f32[96,1024]{1,0:T(8,128)S(1)} %get-tuple-element.72.edge_local, ...), custom_call_target="tpu_custom_call" | custom-call | tf_op jit(solution)/shard_map/pallas_call | solution.py:447
  65.4 0.1 collective-permute-start.25
  65.5 1.2 %collective-permute-done.25 = f32[96,96]{1,0:T(8,128)S(1)} collective-permute-done((f32[96,96]{1,0:T(8,128)S(1)}, f32[96,96]{1,0:T(8,128)S(1)}, u32[]{:S(2)}, u32[]{:S(2)}) %collective-permute-start.25) | collective-permute-done | bytes 36896 | tf_op jit(solution)/shard_map/ppermute | solution.py:360
  66.7 1.6 %collective-permute-start.26 = (f32[96,96]{1,0:T(8,128)S(1)}, f32[96,96]{1,0:T(8,128)S(1)}, u32[]{:S(2)}, u32[]{:S(2)}) collective-permute-start(f32[96,96]{1,0:T(8,128)S(1)} %add.12), channel_id=1, source_target_pairs={{0,8},{4,12},{8,0},{12,4},{16,24},{20,28},{24,16},{28,20},{1,9},{5... | collective-permute-start | bytes 110600 | tf_op jit(solution)/shard_map/ppermute | solution.py:360
  68.3 2.6 %collective-permute-done.26 = f32[96,96]{1,0:T(8,128)S(1)} collective-permute-done((f32[96,96]{1,0:T(8,128)S(1)}, f32[96,96]{1,0:T(8,128)S(1)}, u32[]{:S(2)}, u32[]{:S(2)}) %collective-permute-start.26) | collective-permute-done | bytes 36896 | tf_op jit(solution)/shard_map/ppermute | solution.py:360
  70.9 1.7 %collective-permute-start.27 = (f32[96,96]{1,0:T(8,128)S(1)}, f32[96,96]{1,0:T(8,128)S(1)}, u32[]{:S(2)}, u32[]{:S(2)}) collective-permute-start(f32[96,96]{1,0:T(8,128)S(1)} %add.13), channel_id=1, source_target_pairs={{0,16},{4,20},{8,24},{12,28},{16,0},{20,4},{24,8},{28,12},{1,17},{... | collective-permute-start | bytes 110600 | tf_op jit(solution)/shard_map/ppermute | solution.py:360
  72.5 3.4 %collective-permute-done.27 = f32[96,96]{1,0:T(8,128)S(1)} collective-permute-done((f32[96,96]{1,0:T(8,128)S(1)}, f32[96,96]{1,0:T(8,128)S(1)}, u32[]{:S(2)}, u32[]{:S(2)}) %collective-permute-start.27) | collective-permute-done | bytes 36896 | tf_op jit(solution)/shard_map/ppermute | solution.py:360
  75.9 1.5 %collective-permute-start.28 = (f32[96,96]{1,0:T(8,128)S(1)}, f32[96,96]{1,0:T(8,128)S(1)}, u32[]{:S(2)}, u32[]{:S(2)}) collective-permute-start(f32[96,96]{1,0:T(8,128)S(1)} %add.14), channel_id=1, source_target_pairs={{0,1},{1,0},{2,3},{3,2},{4,5},{5,4},{6,7},{7,6},{8,9},{9,8},{10,11... | collective-permute-start | bytes 110600 | tf_op jit(solution)/shard_map/ppermute | solution.py:360
  77.5 2.6 %collective-permute-done.28 = f32[96,96]{1,0:T(8,128)S(1)} collective-permute-done((f32[96,96]{1,0:T(8,128)S(1)}, f32[96,96]{1,0:T(8,128)S(1)}, u32[]{:S(2)}, u32[]{:S(2)}) %collective-permute-start.28) | collective-permute-done | bytes 36896 | tf_op jit(solution)/shard_map/ppermute | solution.py:360
  80.1 1.6 %collective-permute-start.29 = (f32[96,96]{1,0:T(8,128)S(1)}, f32[96,96]{1,0:T(8,128)S(1)}, u32[]{:S(2)}, u32[]{:S(2)}) collective-permute-start(f32[96,96]{1,0:T(8,128)S(1)} %add.15.first), channel_id=1, source_target_pairs={{0,2},{1,3},{2,0},{3,1},{4,6},{5,7},{6,4},{7,5},{8,10},{9,11},{10,... | collective-permute-start | bytes 110600 | tf_op jit(solution)/shard_map/ppermute | solution.py:450
  81.7 1.1 %shard_map.64.values = bf16[288,2048]{1,0:T(8,128)(2,1)S(1)} custom-call(f32[96,256]{1,0:T(8,128)S(1)} %collective-permute-done.21.r0, f32[96,256]{1,0:T(8,128)S(1)} %collective-permute-done.22.r1, f32[96,256]{1,0:T(8,128)S(1)} %collective-permute-done.23.r2, f32[96,256]{1,0:T(8,128)S(1)} %collective-permute-done.24.r3, ...), custom_call_target="tpu_custom_call" | custom-call | tf_op jit(solution)/shard_map/pallas_call | solution.py:451
  82.8 1.4 %collective-permute-done.29.second = f32[96,96]{1,0:T(8,128)S(1)} collective-permute-done((f32[96,96]{1,0:T(8,128)S(1)}, f32[96,96]{1,0:T(8,128)S(1)}, u32[]{:S(2)}, u32[]{:S(2)}) %collective-permute-start.29) | collective-permute-done | bytes 36896 | tf_op jit(solution)/shard_map/ppermute | solution.py:450
  84.2 4.9 %shard_map.65 = f32[1,1,96,2048]{3,2,1,0:T(8,128)} custom-call(f32[96,96]{1,0:T(8,128)S(1)} %add.15.first, f32[96,96]{1,0:T(8,128)S(1)} %collective-permute-done.29.second, bf16[288,2048]{1,0:T(8,128)(2,1)S(1)} %shard_map.64.values), custom_call_target="tpu_custom_call" | custom-call | tf_op jit(solution)/shard_map/pallas_call | solution.py:453
  (34 shorter events, 0.1 us)
Async XLA Ops:
  0.7 0.7 copy-start
  7.4 4.6 %collective-permute-start = (f32[96,256]{1,0:T(8,128)S(1)}, f32[96,256]{1,0:T(8,128)S(1)}, u32[]{:S(2)}, u32[]{:S(2)}) collective-permute-start(f32[96,256]{1,0:T(8,128)S(1)} %get-tuple-element.40.refs_8_), channel_id=1, source_target_pairs={{0,4},{4,0},{8,12},{12,8},{16,20},{20,16},{24,28},{28,24},{1,5},{5... | collective-permute-start | bytes 294920 | tf_op jit(solution)/shard_map/ppermute | solution.py:376
  8.0 10.3 %collective-permute-start.2 = (f32[96,256]{1,0:T(8,128)S(1)}, f32[96,256]{1,0:T(8,128)S(1)}, u32[]{:S(2)}, u32[]{:S(2)}) collective-permute-start(f32[96,256]{1,0:T(8,128)S(1)} %get-tuple-element.41.refs_9_), channel_id=1, source_target_pairs={{0,3},{1,2},{2,1},{3,0},{4,7},{5,6},{6,5},{7,4},{8,11},{9,10},{10,... | collective-permute-start | bytes 294920 | tf_op jit(solution)/shard_map/ppermute | solution.py:377
  11.5 6.8 %collective-permute-start.3 = (f32[96,256]{1,0:T(8,128)S(1)}, f32[96,256]{1,0:T(8,128)S(1)}, u32[]{:S(2)}, u32[]{:S(2)}) collective-permute-start(f32[96,256]{1,0:T(8,128)S(1)} %get-tuple-element.42.refs_10_), channel_id=1, source_target_pairs={{0,1},{1,0},{2,3},{3,2},{4,5},{5,4},{6,7},{7,6},{8,9},{9,8},{10,11... | collective-permute-start | bytes 294920 | tf_op jit(solution)/shard_map/ppermute | solution.py:378
  12.0 6.3 %collective-permute-start.4 = (f32[96,256]{1,0:T(8,128)S(1)}, f32[96,256]{1,0:T(8,128)S(1)}, u32[]{:S(2)}, u32[]{:S(2)}) collective-permute-start(f32[96,256]{1,0:T(8,128)S(1)} %get-tuple-element.43.refs_11_), channel_id=1, source_target_pairs={{0,4},{4,0},{8,12},{12,8},{16,20},{20,16},{24,28},{28,24},{1,5},{5... | collective-permute-start | bytes 294920 | tf_op jit(solution)/shard_map/ppermute | solution.py:380
  12.0 6.3 %collective-permute-start.1 = (f32[96,256]{1,0:T(8,128)S(1)}, f32[96,256]{1,0:T(8,128)S(1)}, u32[]{:S(2)}, u32[]{:S(2)}) collective-permute-start(f32[96,256]{1,0:T(8,128)S(1)} %collective-permute-done), channel_id=1, source_target_pairs={{0,8},{8,16},{16,24},{24,28},{4,0},{12,4},{20,12},{28,20},{1,9},{9... | collective-permute-start | bytes 294920 | tf_op jit(solution)/shard_map/ppermute | solution.py:379
  18.9 2.2 %collective-permute-start.5 = (f32[96,256]{1,0:T(8,128)S(1)}, f32[96,256]{1,0:T(8,128)S(1)}, u32[]{:S(2)}, u32[]{:S(2)}) collective-permute-start(f32[96,256]{1,0:T(8,128)S(1)} %get-tuple-element.52.refs_12_), channel_id=1, source_target_pairs={{0,4},{4,0},{8,12},{12,8},{16,20},{20,16},{24,28},{28,24},{1,5},{5... | collective-permute-start | bytes 294920 | tf_op jit(solution)/shard_map/ppermute | solution.py:376
  19.0 25.3 %collective-permute-start.7 = (f32[96,256]{1,0:T(8,128)S(1)}, f32[96,256]{1,0:T(8,128)S(1)}, u32[]{:S(2)}, u32[]{:S(2)}) collective-permute-start(f32[96,256]{1,0:T(8,128)S(1)} %get-tuple-element.53.refs_13_), channel_id=1, source_target_pairs={{0,3},{1,2},{2,1},{3,0},{4,7},{5,6},{6,5},{7,4},{8,11},{9,10},{10,... | collective-permute-start | bytes 294920 | tf_op jit(solution)/shard_map/ppermute | solution.py:377
  20.5 23.8 %collective-permute-start.8 = (f32[96,256]{1,0:T(8,128)S(1)}, f32[96,256]{1,0:T(8,128)S(1)}, u32[]{:S(2)}, u32[]{:S(2)}) collective-permute-start(f32[96,256]{1,0:T(8,128)S(1)} %get-tuple-element.54.refs_14_), channel_id=1, source_target_pairs={{0,1},{1,0},{2,3},{3,2},{4,5},{5,4},{6,7},{7,6},{8,9},{9,8},{10,11... | collective-permute-start | bytes 294920 | tf_op jit(solution)/shard_map/ppermute | solution.py:378
  21.0 23.2 %collective-permute-start.9 = (f32[96,256]{1,0:T(8,128)S(1)}, f32[96,256]{1,0:T(8,128)S(1)}, u32[]{:S(2)}, u32[]{:S(2)}) collective-permute-start(f32[96,256]{1,0:T(8,128)S(1)} %get-tuple-element.55.refs_15_), channel_id=1, source_target_pairs={{0,4},{4,0},{8,12},{12,8},{16,20},{20,16},{24,28},{28,24},{1,5},{5... | collective-permute-start | bytes 294920 | tf_op jit(solution)/shard_map/ppermute | solution.py:380
  21.0 23.2 %collective-permute-start.6 = (f32[96,256]{1,0:T(8,128)S(1)}, f32[96,256]{1,0:T(8,128)S(1)}, u32[]{:S(2)}, u32[]{:S(2)}) collective-permute-start(f32[96,256]{1,0:T(8,128)S(1)} %collective-permute-done.5), channel_id=1, source_target_pairs={{0,8},{8,16},{16,24},{24,28},{4,0},{12,4},{20,12},{28,20},{1,9},{9... | collective-permute-start | bytes 294920 | tf_op jit(solution)/shard_map/ppermute | solution.py:379
  22.6 1.2 %collective-permute-start.10 = (f32[8,128]{1,0:T(8,128)S(1)}, f32[8,128]{1,0:T(8,128)S(1)}, u32[]{:S(2)}, u32[]{:S(2)}) collective-permute-start(f32[8,128]{1,0:T(8,128)S(1)} %get-tuple-element.51.refs_6_.refs_7_.own.peak), channel_id=1, source_target_pairs={{0,4},{4,0},{8,12},{12,8},{16,20},{20,16},{24,28},{28,24},{1,5},{5... | collective-permute-start | bytes 12296 | tf_op jit(solution)/shard_map/ppermute | solution.py:360
  23.8 3.6 %collective-permute-start.11 = (f32[8,128]{1,0:T(8,128)S(1)}, f32[8,128]{1,0:T(8,128)S(1)}, u32[]{:S(2)}, u32[]{:S(2)}) collective-permute-start(f32[8,128]{1,0:T(8,128)S(1)} %max.15), channel_id=1, source_target_pairs={{0,8},{4,12},{8,0},{12,4},{16,24},{20,28},{24,16},{28,20},{1,9},{5... | collective-permute-start | bytes 12296 | tf_op jit(solution)/shard_map/ppermute | solution.py:360
  27.4 4.5 %collective-permute-start.12 = (f32[8,128]{1,0:T(8,128)S(1)}, f32[8,128]{1,0:T(8,128)S(1)}, u32[]{:S(2)}, u32[]{:S(2)}) collective-permute-start(f32[8,128]{1,0:T(8,128)S(1)} %max.16), channel_id=1, source_target_pairs={{0,16},{4,20},{8,24},{12,28},{16,0},{20,4},{24,8},{28,12},{1,17},{... | collective-permute-start | bytes 12296 | tf_op jit(solution)/shard_map/ppermute | solution.py:360
  31.9 3.6 %collective-permute-start.13 = (f32[8,128]{1,0:T(8,128)S(1)}, f32[8,128]{1,0:T(8,128)S(1)}, u32[]{:S(2)}, u32[]{:S(2)}) collective-permute-start(f32[8,128]{1,0:T(8,128)S(1)} %max.17), channel_id=1, source_target_pairs={{0,1},{1,0},{2,3},{3,2},{4,5},{5,4},{6,7},{7,6},{8,9},{9,8},{10,11... | collective-permute-start | bytes 12296 | tf_op jit(solution)/shard_map/ppermute | solution.py:360
  35.5 3.6 %collective-permute-start.14 = (f32[8,128]{1,0:T(8,128)S(1)}, f32[8,128]{1,0:T(8,128)S(1)}, u32[]{:S(2)}, u32[]{:S(2)}) collective-permute-start(f32[8,128]{1,0:T(8,128)S(1)} %max.18), channel_id=1, source_target_pairs={{0,2},{1,3},{2,0},{3,1},{4,6},{5,7},{6,4},{7,5},{8,10},{9,11},{10,... | collective-permute-start | bytes 12296 | tf_op jit(solution)/shard_map/ppermute | solution.py:360
  45.1 3.1 %collective-permute-start.15 = (f32[96,256]{1,0:T(8,128)S(1)}, f32[96,256]{1,0:T(8,128)S(1)}, u32[]{:S(2)}, u32[]{:S(2)}) collective-permute-start(f32[96,256]{1,0:T(8,128)S(1)} %get-tuple-element.59), channel_id=1, source_target_pairs={{0,4},{4,0},{8,12},{12,8},{16,20},{20,16},{24,28},{28,24},{1,5},{5... | collective-permute-start | bytes 294920 | tf_op jit(solution)/shard_map/ppermute | solution.py:376
  45.2 10.1 %collective-permute-start.17 = (f32[96,256]{1,0:T(8,128)S(1)}, f32[96,256]{1,0:T(8,128)S(1)}, u32[]{:S(2)}, u32[]{:S(2)}) collective-permute-start(f32[96,256]{1,0:T(8,128)S(1)} %get-tuple-element.60), channel_id=1, source_target_pairs={{0,3},{1,2},{2,1},{3,0},{4,7},{5,6},{6,5},{7,4},{8,11},{9,10},{10,... | collective-permute-start | bytes 294920 | tf_op jit(solution)/shard_map/ppermute | solution.py:377
  47.7 7.6 %collective-permute-start.18 = (f32[96,256]{1,0:T(8,128)S(1)}, f32[96,256]{1,0:T(8,128)S(1)}, u32[]{:S(2)}, u32[]{:S(2)}) collective-permute-start(f32[96,256]{1,0:T(8,128)S(1)} %get-tuple-element.61), channel_id=1, source_target_pairs={{0,1},{1,0},{2,3},{3,2},{4,5},{5,4},{6,7},{7,6},{8,9},{9,8},{10,11... | collective-permute-start | bytes 294920 | tf_op jit(solution)/shard_map/ppermute | solution.py:378
  48.2 7.1 %collective-permute-start.19 = (f32[96,256]{1,0:T(8,128)S(1)}, f32[96,256]{1,0:T(8,128)S(1)}, u32[]{:S(2)}, u32[]{:S(2)}) collective-permute-start(f32[96,256]{1,0:T(8,128)S(1)} %get-tuple-element.62), channel_id=1, source_target_pairs={{0,4},{4,0},{8,12},{12,8},{16,20},{20,16},{24,28},{28,24},{1,5},{5... | collective-permute-start | bytes 294920 | tf_op jit(solution)/shard_map/ppermute | solution.py:380
  48.2 7.1 %collective-permute-start.16 = (f32[96,256]{1,0:T(8,128)S(1)}, f32[96,256]{1,0:T(8,128)S(1)}, u32[]{:S(2)}, u32[]{:S(2)}) collective-permute-start(f32[96,256]{1,0:T(8,128)S(1)} %collective-permute-done.15), channel_id=1, source_target_pairs={{0,8},{8,16},{16,24},{24,28},{4,0},{12,4},{20,12},{28,20},{1,9},{9... | collective-permute-start | bytes 294920 | tf_op jit(solution)/shard_map/ppermute | solution.py:379
  56.0 2.1 %collective-permute-start.20 = (f32[96,256]{1,0:T(8,128)S(1)}, f32[96,256]{1,0:T(8,128)S(1)}, u32[]{:S(2)}, u32[]{:S(2)}) collective-permute-start(f32[96,256]{1,0:T(8,128)S(1)} %get-tuple-element.66), channel_id=1, source_target_pairs={{0,4},{4,0},{8,12},{12,8},{16,20},{20,16},{24,28},{28,24},{1,5},{5... | collective-permute-start | bytes 294920 | tf_op jit(solution)/shard_map/ppermute | solution.py:376
  56.1 8.3 %collective-permute-start.22 = (f32[96,256]{1,0:T(8,128)S(1)}, f32[96,256]{1,0:T(8,128)S(1)}, u32[]{:S(2)}, u32[]{:S(2)}) collective-permute-start(f32[96,256]{1,0:T(8,128)S(1)} %get-tuple-element.67), channel_id=1, source_target_pairs={{0,3},{1,2},{2,1},{3,0},{4,7},{5,6},{6,5},{7,4},{8,11},{9,10},{10,... | collective-permute-start | bytes 294920 | tf_op jit(solution)/shard_map/ppermute | solution.py:377
  57.5 6.9 %collective-permute-start.23 = (f32[96,256]{1,0:T(8,128)S(1)}, f32[96,256]{1,0:T(8,128)S(1)}, u32[]{:S(2)}, u32[]{:S(2)}) collective-permute-start(f32[96,256]{1,0:T(8,128)S(1)} %get-tuple-element.68), channel_id=1, source_target_pairs={{0,1},{1,0},{2,3},{3,2},{4,5},{5,4},{6,7},{7,6},{8,9},{9,8},{10,11... | collective-permute-start | bytes 294920 | tf_op jit(solution)/shard_map/ppermute | solution.py:378
  58.0 6.3 %collective-permute-start.24 = (f32[96,256]{1,0:T(8,128)S(1)}, f32[96,256]{1,0:T(8,128)S(1)}, u32[]{:S(2)}, u32[]{:S(2)}) collective-permute-start(f32[96,256]{1,0:T(8,128)S(1)} %get-tuple-element.69), channel_id=1, source_target_pairs={{0,4},{4,0},{8,12},{12,8},{16,20},{20,16},{24,28},{28,24},{1,5},{5... | collective-permute-start | bytes 294920 | tf_op jit(solution)/shard_map/ppermute | solution.py:380
  58.1 6.3 %collective-permute-start.21 = (f32[96,256]{1,0:T(8,128)S(1)}, f32[96,256]{1,0:T(8,128)S(1)}, u32[]{:S(2)}, u32[]{:S(2)}) collective-permute-start(f32[96,256]{1,0:T(8,128)S(1)} %collective-permute-done.20), channel_id=1, source_target_pairs={{0,8},{8,16},{16,24},{24,28},{4,0},{12,4},{20,12},{28,20},{1,9},{9... | collective-permute-start | bytes 294920 | tf_op jit(solution)/shard_map/ppermute | solution.py:379
  65.4 1.3 %collective-permute-start.25 = (f32[96,96]{1,0:T(8,128)S(1)}, f32[96,96]{1,0:T(8,128)S(1)}, u32[]{:S(2)}, u32[]{:S(2)}) collective-permute-start(f32[96,96]{1,0:T(8,128)S(1)} %shard_map.63), channel_id=1, source_target_pairs={{0,4},{4,0},{8,12},{12,8},{16,20},{20,16},{24,28},{28,24},{1,5},{5... | collective-permute-start | bytes 110600 | tf_op jit(solution)/shard_map/ppermute | solution.py:360
  66.7 4.2 %collective-permute-start.26 = (f32[96,96]{1,0:T(8,128)S(1)}, f32[96,96]{1,0:T(8,128)S(1)}, u32[]{:S(2)}, u32[]{:S(2)}) collective-permute-start(f32[96,96]{1,0:T(8,128)S(1)} %add.12), channel_id=1, source_target_pairs={{0,8},{4,12},{8,0},{12,4},{16,24},{20,28},{24,16},{28,20},{1,9},{5... | collective-permute-start | bytes 110600 | tf_op jit(solution)/shard_map/ppermute | solution.py:360
  70.9 5.0 %collective-permute-start.27 = (f32[96,96]{1,0:T(8,128)S(1)}, f32[96,96]{1,0:T(8,128)S(1)}, u32[]{:S(2)}, u32[]{:S(2)}) collective-permute-start(f32[96,96]{1,0:T(8,128)S(1)} %add.13), channel_id=1, source_target_pairs={{0,16},{4,20},{8,24},{12,28},{16,0},{20,4},{24,8},{28,12},{1,17},{... | collective-permute-start | bytes 110600 | tf_op jit(solution)/shard_map/ppermute | solution.py:360
  75.9 4.2 %collective-permute-start.28 = (f32[96,96]{1,0:T(8,128)S(1)}, f32[96,96]{1,0:T(8,128)S(1)}, u32[]{:S(2)}, u32[]{:S(2)}) collective-permute-start(f32[96,96]{1,0:T(8,128)S(1)} %add.14), channel_id=1, source_target_pairs={{0,1},{1,0},{2,3},{3,2},{4,5},{5,4},{6,7},{7,6},{8,9},{9,8},{10,11... | collective-permute-start | bytes 110600 | tf_op jit(solution)/shard_map/ppermute | solution.py:360
  80.1 4.2 %collective-permute-start.29 = (f32[96,96]{1,0:T(8,128)S(1)}, f32[96,96]{1,0:T(8,128)S(1)}, u32[]{:S(2)}, u32[]{:S(2)}) collective-permute-start(f32[96,96]{1,0:T(8,128)S(1)} %add.15.first), channel_id=1, source_target_pairs={{0,2},{1,3},{2,0},{3,1},{4,6},{5,7},{6,4},{7,5},{8,10},{9,11},{10,... | collective-permute-start | bytes 110600 | tf_op jit(solution)/shard_map/ppermute | solution.py:450

commit v2 on v1

--- a/solution.py
+++ b/solution.py
@@ -11,6 +11,7 @@
 
 LOWER_FRACTION = 0.125
 LANES = 128
+SHIFT = 7
 CHUNK = 256
 F32 = jnp.float32
 BF16 = jnp.bfloat16
@@ -129,13 +130,15 @@
         order.append(jnp.where(upward, high, low))
     targets = jnp.concatenate(order, axis=1)
     marks[...] = jnp.broadcast_to(targets, marks.shape)
-    for start in range(0, cells, CHUNK):
-        spot = lax.broadcasted_iota(jnp.int32, (CHUNK, edges), 0) + start
-        equal = (spot == targets).astype(F32)
-        place[start : start + CHUNK] = equal.astype(BF16)
-        hits[start : start + CHUNK] = total(
+    spot = lax.broadcasted_iota(jnp.int32, (LANES, edges), 0)
+    within = (spot == (targets & (LANES - 1))).astype(F32).astype(BF16)
+    block = jnp.broadcast_to((targets >> SHIFT).astype(F32).astype(BF16), within.shape)
+    for m in range(blocks):
+        equal = jnp.where(block == BF16(m), within, jnp.zeros_like(within))
+        place[m * LANES : (m + 1) * LANES] = equal
+        hits[m * LANES : (m + 1) * LANES] = total(
             equal[:, other : other + LANES] for other in range(0, edges, LANES)
-        ).astype(BF16)
+        )
     begin[...] = jnp.where(live_lanes(count, 0, cells), basis[...], 0.0)
     picked = folded(dot(stacked(begin[...]), place[...]))
     for i, out in enumerate(outs):
@@ -159,11 +162,14 @@
     peak[...] = jnp.full(peak.shape, jnp.max(value), F32)
 
 
-def multiply(cols, m, value, stored, inside):
-    product = folded(dot(left_rows(value), stored[m]))
-    for j in range(stored.shape[2] // LANES):
-        spot = pl.ds(pl.multiple_of(cols[0, j, 0, m] * LANES, LANES), LANES)
-        inside[:, spot] += product[:, j * LANES : (j + 1) * LANES]
+def multiply(cols, values, stored, inside):
+    blocks, _, width = stored.shape
+    inside[...] = jnp.zeros_like(inside)
+    for m in range(blocks):
+        product = folded(dot(left_rows(values[:, m * LANES : (m + 1) * LANES]), stored[m]))
+        for j in range(width // LANES):
+            spot = pl.ds(pl.multiple_of(cols[0, j, 0, m] * LANES, LANES), LANES)
+            inside[:, spot] += product[:, j * LANES : (j + 1) * LANES]
 
 
 def gather(values, place):
@@ -189,12 +195,12 @@
             equal = down == targets[:, other : other + LANES]
             same[start : start + LANES, other : other + LANES] = equal.astype(F32).astype(BF16)
         lane = lax.broadcasted_iota(jnp.int32, (LANES, LANES), 1)
-        for other in range(0, cells, LANES):
-            equal = down == lane + other
-            back[start : start + LANES, other : other + LANES] = equal.astype(F32).astype(BF16)
-    inside[...] = jnp.zeros_like(inside)
-    for m in range(cells // LANES):
-        multiply(cols, m, begin[:, m * LANES : (m + 1) * LANES], stored, inside)
+        within = ((down & (LANES - 1)) == lane).astype(F32).astype(BF16)
+        block = (down >> SHIFT).astype(F32).astype(BF16)
+        for m in range(cells // LANES):
+            equal = jnp.where(block == BF16(m), within, jnp.zeros_like(within))
+            back[start : start + LANES, m * LANES : (m + 1) * LANES] = equal
+    multiply(cols, begin, stored, inside)
     for part in chunks(cells):
         live = live_lanes(counts[...], part.start, CHUNK)
         local[:, part] = degree[0:1, part] * begin[:, part] - jnp.where(live, inside[:, part], 0.0)
@@ -235,7 +241,6 @@
     top = own[0:1, 0:1]
     centre, half = scalars(peak)
     arrived = stacked(joined_up((r0, r1, r2, r3)))
-    inside[...] = jnp.zeros_like(inside)
     for part in chunks(cells):
         crossed = folded(dot(arrived, back[:, part]))
         if number == 0:
@@ -249,9 +254,7 @@
             value = local[:, part] - (2.0 / half) * crossed
             later[:, part] = begin[:, part]
         field[:, part] = value
-        for start in range(0, CHUNK, LANES):
-            block = (part.start + start) // LANES
-            multiply(cols, block, value[:, start : start + LANES], stored, inside)
+    multiply(cols, field, stored, inside)
     for part in chunks(cells):
         live = live_lanes(counts[...], part.start, CHUNK)
         kept = jnp.where(live, inside[:, part], 0.0)
@@ -265,13 +268,43 @@
         refs[3][...] = product_nt(later[...], later[...])
 
 
+def places(size):
+    row = lax.broadcasted_iota(jnp.int32, (size, size), 0)
+    return row, lax.broadcasted_iota(jnp.int32, (size, size), 1)
+
+
+def packed(gram):
+    size = gram.shape[0] // 2
+    row, col = places(size)
+    low, high = gram[:size, :size], gram[size:, size:]
+    diagonal = jnp.sum(jnp.where(row == col, high, 0.0), axis=1, keepdims=True)
+    width = LANES - 2 * size
+    return jnp.concatenate(
+        [jnp.where(col <= row, low, high), gram[:size, size:], jnp.broadcast_to(diagonal, (size, width))],
+        axis=1,
+    )
+
+
+def unpacked(value):
+    size = value.shape[0]
+    row, col = places(size)
+    mixed, cross = value[:, :size], value[:, size : 2 * size]
+    below, above = jnp.where(col < row, mixed, 0.0), jnp.where(col > row, mixed, 0.0)
+    diagonal = jnp.where(row == col, value[:, 2 * size : 2 * size + 1], 0.0)
+    low = jnp.where(row == col, mixed, below) + below.T
+    high = above + above.T + diagonal
+    return jnp.concatenate(
+        [jnp.concatenate([low, cross], axis=1), jnp.concatenate([cross.T, high], axis=1)], axis=0
+    )
+
+
 def gram_kernel(r0, r1, r2, r3, edge_local, same, peak, base, gram):
     _, half = scalars(peak)
     scale = 2.0 / half
     arrived = joined_up((r0, r1, r2, r3))
     crossed = folded(dot(stacked(arrived), same[...]))
     mixed = product_nt(scale * (edge_local[...] - (0.5 * scale) * crossed), arrived)
-    gram[...] = base[...] - mixed - mixed.T
+    gram[...] = packed(base[...] - mixed - mixed.T)
 
 
 def last_kernel(r0, r1, r2, r3, local, back, peak, terms):
@@ -305,8 +338,9 @@
     ]
 
 
-def encode_kernel(root, first, second, values, out):
-    gram = first[...] + second[...]
+def encode_kernel(root, *refs):
+    *parts, values, out = refs
+    gram = unpacked(total(part[...] for part in parts))
     vecs = gram.shape[0]
     size = 8
     lane = lax.broadcasted_iota(jnp.int32, (size, vecs), 1)
@@ -444,13 +478,17 @@
         earlier = [begin, now] if number == 0 else [now, now]
         arrived = coming
 
-    gram = call(gram_kernel, shape(vecs, vecs), [VM] * 8)(*arrived, edge_local, same, peak, *base)
-    gram = spread(gram, jnp.add, stages[:-1])
-    axis, bit = stages[-1]
-    other = lax.ppermute(gram, axis, xor_pairs(lax.axis_size(axis), bit))
+    gram = call(gram_kernel, shape(vecs // 2, LANES), [VM] * 8)(*arrived, edge_local, same, peak, *base)
+    direct = sizes[1] == 4
+    gram = spread(gram, jnp.add, [stage for stage in stages if not (direct and stage[0] == "gy")])
+    parts = [gram]
+    if direct:
+        parts += [lax.ppermute(gram, "gy", xor_pairs(4, bit)) for bit in (3, 2, 1)]
     now = call(last_kernel, shape(3 * vecs, cells, dtype=BF16), [VM] * 7)(*arrived, local, back, peak)
     root = math.sqrt(cells * sizes[0] * sizes[1])
-    return call(functools.partial(encode_kernel, root), shape(1, 1, vecs, cells), [VM] * 3)(gram, other, now)
+    return call(functools.partial(encode_kernel, root), shape(1, 1, vecs, cells), [VM] * (len(parts) + 1))(
+        *parts, now
+    )
 
 
 def solution(mesh):
@@ -463,6 +501,4 @@
     )
     out_specs = P("gx", "gy", None, None)
 
-    return jax.shard_map(
-        per_device, mesh=mesh, in_specs=in_specs, out_specs=out_specs, check_vma=False
-    )
+    return jax.shard_map(per_device, mesh=mesh, in_specs=in_specs, out_specs=out_specs, check_vma=False)

time: 89.4 us -> 84.4 us (0.944)
  Pallas kernels: 36 us -> 32.9 us
  waiting for transfers between devices: 21.6 us -> 19.2 us
    ppermute x9 -> x8, waiting for transfers between devices: 20.1 us -> 17 us  [spread(): value = combine(value, lax.ppermute(value, axis, pairs))]
    pallas_call x3, Pallas kernels: 16.3 us -> 13.7 us  [per_device(): call(functools.partial(field_kernel, number), [field, field, edge_field]...]
    ppermute x1 -> x3, starting transfers between devices: 1.64 us -> 3.49 us  [per_device(): parts += [lax.ppermute(gram, 'gy', xor_pairs(4, bit)) for bit in (3, 2, 1)]]
    ppermute x9 -> x8, starting transfers between devices: 11 us -> 9.34 us  [spread(): value = combine(value, lax.ppermute(value, axis, pairs))]
    ppermute x1 -> x3, waiting for transfers between devices: 1.42 us -> 2.21 us  [per_device(): parts += [lax.ppermute(gram, 'gy', xor_pairs(4, bit)) for bit in (3, 2, 1)]]
  transfers between devices with their start and end apart: 30 -> 31, of which waited for: 10 -> 11; matrix products, arithmetic and copies ran while one was open for 0% -> 0% of each run, Pallas kernels for 25% -> 23%
where the time goes in v2:
time: 84.4 us; the launch traced here: 84.2 us
  Pallas kernels  32.9 us (39%)
  starting transfers between devices  30.4 us (36%)
  waiting for transfers between devices  19.2 us (23%)
  between operations  0.92 us (1%)
    ppermute x8, waiting for transfers between devices, spread(): value = combine(value, lax.ppermute(value, axis, pairs))  17 us
    pallas_call x3, Pallas kernels, per_device(): call(functools.partial(field_kernel, number), [field, field, edge_field]...  13.7 us
    ppermute x8, starting transfers between devices, spread(): value = combine(value, lax.ppermute(value, axis, pairs))  9.34 us
    ppermute x4, starting transfers between devices, exchange(): y_far = lax.ppermute(y_far, 'gy', far_pairs(sizes[1]))  9.06 us
    pallas_call x1, Pallas kernels, per_device(): call(functools.partial(first_kernel, sizes), [shape(cells, 4 * edges, dty...  5.67 us
    ppermute x4, starting transfers between devices, exchange(): x_far = lax.ppermute(x_far, 'gx', turn_pairs(sizes[0]))  5.65 us
    pallas_call x1, Pallas kernels, per_device(): call(functools.partial(encode_kernel, root), shape(1, 1, vecs, cells), [V...  5.15 us
    pallas_call x1, Pallas kernels, per_device(): call(open_kernel, [field, edge_field, shape(4 * edges, 4 * edges, dtype=B...  4.27 us
  transfers between devices with their start and end apart: 31, of which 11 were waited for; matrix products, arithmetic and copies ran while one was open for 0% of the time, Pallas kernels for 23%

profile of v2, /device:TPU:0, one launch (start us, length us, event | category | flops | bytes accessed | tf_op | source)
XLA Modules:
  0.0 84.2 jit_solution(1791372077297332034)
XLA Ops:
  0.7 0.7 copy-done
  1.3 5.7 %shard_map.55 = (bf16[2048,1024]{1,0:T(8,128)(2,1)S(1)}, bf16[16,256,640]{2,1,0:T(8,128)(2,1)S(1)}, f32[96,2048]{1,0:T(8,128)S(1)}, f32[8,2048]{1,0:T(8,128)S(1)...) custom-call(s32[1,5,1,16]{3,2,1,0:T(1,128)S(1)} %bitcast.1, ...), custom_call_target="tpu_custom_call" | custom-call | tf_op jit(solution)/shard_map/pallas_call | solution.py:418
  7.0 0.6 collective-permute-start
  7.6 3.5 %collective-permute-start.2 = (f32[96,256]{1,0:T(8,128)S(1)}, f32[96,256]{1,0:T(8,128)S(1)}, u32[]{:S(2)}, u32[]{:S(2)}) collective-permute-start(f32[96,256]{1,0:T(8,128)S(1)} %get-tuple-element.41.refs_9_), channel_id=1, source_target_pairs={{0,3},{1,2},{2,1},{3,0},{4,7},{5,6},{6,5},{7,4},{8,11},{9,10},{10,... | collective-permute-start | bytes 294920 | tf_op jit(solution)/shard_map/ppermute | solution.py:411
  11.1 0.5 collective-permute-start.3
  11.6 1.6 %collective-permute-start.1 = (f32[96,256]{1,0:T(8,128)S(1)}, f32[96,256]{1,0:T(8,128)S(1)}, u32[]{:S(2)}, u32[]{:S(2)}) collective-permute-start(f32[96,256]{1,0:T(8,128)S(1)} %collective-permute-done), channel_id=1, source_target_pairs={{0,8},{8,16},{16,24},{24,28},{4,0},{12,4},{20,12},{28,20},{1,9},{9... | collective-permute-start | bytes 294920 | tf_op jit(solution)/shard_map/ppermute | solution.py:413
  13.2 4.3 %shard_map.56 = (f32[96,2048]{1,0:T(8,128)S(1)}, f32[96,1024]{1,0:T(8,128)S(1)}, bf16[1024,1024]{1,0:T(8,128)(2,1)S(1)}, bf16[1024,2048]{1,0:T(8,128)(2,1)S(1)}) custom-call(s32[1,5,1,16]{3,2,1,0:T(1,128)S(1)} %bitcast.2, s32[1,1]{1,0:T(1,128)S(6)} %copy.6.counts, f32[96,2048]{1,0:T(8,128)S(1)} %get-tuple-element.44.begin.once, ...), custom_call_target="tpu_custom_call" | custom-call | tf_op jit(solution)/shard_map/pallas_call | solution.py:447
  17.5 0.6 shard_map.57
  18.1 0.1 collective-permute-start.5
  18.2 1.5 %collective-permute-start.7 = (f32[96,256]{1,0:T(8,128)S(1)}, f32[96,256]{1,0:T(8,128)S(1)}, u32[]{:S(2)}, u32[]{:S(2)}) collective-permute-start(f32[96,256]{1,0:T(8,128)S(1)} %get-tuple-element.53.refs_13_), channel_id=1, source_target_pairs={{0,3},{1,2},{2,1},{3,0},{4,7},{5,6},{6,5},{7,4},{8,11},{9,10},{10,... | collective-permute-start | bytes 294920 | tf_op jit(solution)/shard_map/ppermute | solution.py:411
  19.7 0.6 collective-permute-start.8
  20.3 1.6 %collective-permute-start.6 = (f32[96,256]{1,0:T(8,128)S(1)}, f32[96,256]{1,0:T(8,128)S(1)}, u32[]{:S(2)}, u32[]{:S(2)}) collective-permute-start(f32[96,256]{1,0:T(8,128)S(1)} %collective-permute-done.5), channel_id=1, source_target_pairs={{0,8},{8,16},{16,24},{24,28},{4,0},{12,4},{20,12},{28,20},{1,9},{9... | collective-permute-start | bytes 294920 | tf_op jit(solution)/shard_map/ppermute | solution.py:413
  21.8 1.2 %collective-permute-done.10 = f32[8,128]{1,0:T(8,128)S(1)} collective-permute-done((f32[8,128]{1,0:T(8,128)S(1)}, f32[8,128]{1,0:T(8,128)S(1)}, u32[]{:S(2)}, u32[]{:S(2)}) %collective-permute-start.10) | collective-permute-done | bytes 4128 | tf_op jit(solution)/shard_map/ppermute | solution.py:394
  23.0 1.6 %collective-permute-start.11 = (f32[8,128]{1,0:T(8,128)S(1)}, f32[8,128]{1,0:T(8,128)S(1)}, u32[]{:S(2)}, u32[]{:S(2)}) collective-permute-start(f32[8,128]{1,0:T(8,128)S(1)} %max.15), channel_id=1, source_target_pairs={{0,8},{4,12},{8,0},{12,4},{16,24},{20,28},{24,16},{28,20},{1,9},{5... | collective-permute-start | bytes 12296 | tf_op jit(solution)/shard_map/ppermute | solution.py:394
  24.6 2.0 %collective-permute-done.11 = f32[8,128]{1,0:T(8,128)S(1)} collective-permute-done((f32[8,128]{1,0:T(8,128)S(1)}, f32[8,128]{1,0:T(8,128)S(1)}, u32[]{:S(2)}, u32[]{:S(2)}) %collective-permute-start.11) | collective-permute-done | bytes 4128 | tf_op jit(solution)/shard_map/ppermute | solution.py:394
  26.6 1.9 %collective-permute-start.12 = (f32[8,128]{1,0:T(8,128)S(1)}, f32[8,128]{1,0:T(8,128)S(1)}, u32[]{:S(2)}, u32[]{:S(2)}) collective-permute-start(f32[8,128]{1,0:T(8,128)S(1)} %max.16), channel_id=1, source_target_pairs={{0,16},{4,20},{8,24},{12,28},{16,0},{20,4},{24,8},{28,12},{1,17},{... | collective-permute-start | bytes 12296 | tf_op jit(solution)/shard_map/ppermute | solution.py:394
  28.5 2.6 %collective-permute-done.12 = f32[8,128]{1,0:T(8,128)S(1)} collective-permute-done((f32[8,128]{1,0:T(8,128)S(1)}, f32[8,128]{1,0:T(8,128)S(1)}, u32[]{:S(2)}, u32[]{:S(2)}) %collective-permute-start.12) | collective-permute-done | bytes 4128 | tf_op jit(solution)/shard_map/ppermute | solution.py:394
  31.1 1.5 %collective-permute-start.13 = (f32[8,128]{1,0:T(8,128)S(1)}, f32[8,128]{1,0:T(8,128)S(1)}, u32[]{:S(2)}, u32[]{:S(2)}) collective-permute-start(f32[8,128]{1,0:T(8,128)S(1)} %max.17), channel_id=1, source_target_pairs={{0,1},{1,0},{2,3},{3,2},{4,5},{5,4},{6,7},{7,6},{8,9},{9,8},{10,11... | collective-permute-start | bytes 12296 | tf_op jit(solution)/shard_map/ppermute | solution.py:394
  32.6 2.1 %collective-permute-done.13 = f32[8,128]{1,0:T(8,128)S(1)} collective-permute-done((f32[8,128]{1,0:T(8,128)S(1)}, f32[8,128]{1,0:T(8,128)S(1)}, u32[]{:S(2)}, u32[]{:S(2)}) %collective-permute-start.13) | collective-permute-done | bytes 4128 | tf_op jit(solution)/shard_map/ppermute | solution.py:394
  34.8 1.5 %collective-permute-start.14 = (f32[8,128]{1,0:T(8,128)S(1)}, f32[8,128]{1,0:T(8,128)S(1)}, u32[]{:S(2)}, u32[]{:S(2)}) collective-permute-start(f32[8,128]{1,0:T(8,128)S(1)} %max.18), channel_id=1, source_target_pairs={{0,2},{1,3},{2,0},{3,1},{4,6},{5,7},{6,4},{7,5},{8,10},{9,11},{10,... | collective-permute-start | bytes 12296 | tf_op jit(solution)/shard_map/ppermute | solution.py:394
  36.3 2.1 %collective-permute-done.14 = f32[8,128]{1,0:T(8,128)S(1)} collective-permute-done((f32[8,128]{1,0:T(8,128)S(1)}, f32[8,128]{1,0:T(8,128)S(1)}, u32[]{:S(2)}, u32[]{:S(2)}) %collective-permute-start.14) | collective-permute-done | bytes 4128 | tf_op jit(solution)/shard_map/ppermute | solution.py:394
  38.4 4.1 %shard_map.58 = (f32[96,2048]{1,0:T(8,128)S(1)}, f32[96,2048]{1,0:T(8,128)S(1)}, f32[96,1024]{1,0:T(8,128)S(1)}) custom-call(s32[1,5,1,16]{3,2,1,0:T(1,128)S(1)} %bitcast.3, s32[1,1]{1,0:T(1,128)S(6)} %copy.6.counts, f32[96,256]{1,0:T(8,128)S(1)} %collective-permute-done.1.refs_0_.r0, f32[96,256]{1,0:T(8,128)S(1)} %collective-permute-done.2.refs_1_.r1, ...), custom_call_target="tpu_custom_call" | custom-call | tf_op jit(solution)/shard_map/pallas_call | solution.py:472
  42.5 0.7 shard_map.59
  43.2 0.1 collective-permute-start.15
  43.3 2.5 %collective-permute-start.17 = (f32[96,256]{1,0:T(8,128)S(1)}, f32[96,256]{1,0:T(8,128)S(1)}, u32[]{:S(2)}, u32[]{:S(2)}) collective-permute-start(f32[96,256]{1,0:T(8,128)S(1)} %get-tuple-element.60), channel_id=1, source_target_pairs={{0,3},{1,2},{2,1},{3,0},{4,7},{5,6},{6,5},{7,4},{8,11},{9,10},{10,... | collective-permute-start | bytes 294920 | tf_op jit(solution)/shard_map/ppermute | solution.py:411
  45.8 0.5 collective-permute-start.18
  46.4 1.6 %collective-permute-start.16 = (f32[96,256]{1,0:T(8,128)S(1)}, f32[96,256]{1,0:T(8,128)S(1)}, u32[]{:S(2)}, u32[]{:S(2)}) collective-permute-start(f32[96,256]{1,0:T(8,128)S(1)} %collective-permute-done.15), channel_id=1, source_target_pairs={{0,8},{8,16},{16,24},{24,28},{4,0},{12,4},{20,12},{28,20},{1,9},{9... | collective-permute-start | bytes 294920 | tf_op jit(solution)/shard_map/ppermute | solution.py:413
  48.0 4.6 %shard_map.60 = (f32[96,2048]{1,0:T(8,128)S(1)}, f32[96,2048]{1,0:T(8,128)S(1)}, f32[96,1024]{1,0:T(8,128)S(1)}) custom-call(s32[1,5,1,16]{3,2,1,0:T(1,128)S(1)} %bitcast.4, s32[1,1]{1,0:T(1,128)S(6)} %copy.6.counts, f32[96,256]{1,0:T(8,128)S(1)} %collective-permute-done.6.refs_0_.r0, f32[96,256]{1,0:T(8,128)S(1)} %collective-permute-done.7.refs_1_.r1, ...), custom_call_target="tpu_custom_call" | custom-call | tf_op jit(solution)/shard_map/pallas_call | solution.py:472
  52.7 0.6 shard_map.61
  53.3 0.1 collective-permute-start.20
  53.4 1.5 %collective-permute-start.22 = (f32[96,256]{1,0:T(8,128)S(1)}, f32[96,256]{1,0:T(8,128)S(1)}, u32[]{:S(2)}, u32[]{:S(2)}) collective-permute-start(f32[96,256]{1,0:T(8,128)S(1)} %get-tuple-element.67), channel_id=1, source_target_pairs={{0,3},{1,2},{2,1},{3,0},{4,7},{5,6},{6,5},{7,4},{8,11},{9,10},{10,... | collective-permute-start | bytes 294920 | tf_op jit(solution)/shard_map/ppermute | solution.py:411
  54.9 0.5 collective-permute-start.23
  55.4 0.9 %collective-permute-start.21 = (f32[96,256]{1,0:T(8,128)S(1)}, f32[96,256]{1,0:T(8,128)S(1)}, u32[]{:S(2)}, u32[]{:S(2)}) collective-permute-start(f32[96,256]{1,0:T(8,128)S(1)} %collective-permute-done.20), channel_id=1, source_target_pairs={{0,8},{8,16},{16,24},{24,28},{4,0},{12,4},{20,12},{28,20},{1,9},{9... | collective-permute-start | bytes 294920 | tf_op jit(solution)/shard_map/ppermute | solution.py:413
  56.3 5.0 %shard_map.62 = (f32[96,2048]{1,0:T(8,128)}, f32[96,2048]{1,0:T(8,128)S(1)}, f32[96,1024]{1,0:T(8,128)S(1)}, f32[96,96]{1,0:T(8,128)S(1)}) custom-call(s32[1,5,1,16]{3,2,1,0:T(1,128)S(1)} %bitcast.5, s32[1,1]{1,0:T(1,128)S(6)} %copy.6.counts, f32[96,256]{1,0:T(8,128)S(1)} %collective-permute-done.16.refs_0_.r0, ...), custom_call_target="tpu_custom_call" | custom-call | tf_op jit(solution)/shard_map/pallas_call | solution.py:472
  61.3 1.1 %shard_map.63 = f32[48,128]{1,0:T(8,128)S(1)} custom-call(f32[96,256]{1,0:T(8,128)S(1)} %collective-permute-done.21.r0, f32[96,256]{1,0:T(8,128)S(1)} %collective-permute-done.22.r1, f32[96,256]{1,0:T(8,128)S(1)} %collective-permute-done.23.r2, f32[96,256]{1,0:T(8,128)S(1)} %collective-permute-done.24.r3, f32[96,1024]{1,0:T(8,128)S(1)} %get-tuple-element.72.edge_local, ...), custom_call_target="tpu_custom_call" | custom-call | tf_op jit(solution)/shard_map/pallas_call | solution.py:481
  62.5 1.2 %collective-permute-done.25 = f32[48,128]{1,0:T(8,128)S(1)} collective-permute-done((f32[48,128]{1,0:T(8,128)S(1)}, f32[48,128]{1,0:T(8,128)S(1)}, u32[]{:S(2)}, u32[]{:S(2)}) %collective-permute-start.25) | collective-permute-done | bytes 24608 | tf_op jit(solution)/shard_map/ppermute | solution.py:394
  63.7 1.2 %collective-permute-start.26 = (f32[48,128]{1,0:T(8,128)S(1)}, f32[48,128]{1,0:T(8,128)S(1)}, u32[]{:S(2)}, u32[]{:S(2)}) collective-permute-start(f32[48,128]{1,0:T(8,128)S(1)} %add.9), channel_id=1, source_target_pairs={{0,8},{4,12},{8,0},{12,4},{16,24},{20,28},{24,16},{28,20},{1,9},{5... | collective-permute-start | bytes 73736 | tf_op jit(solution)/shard_map/ppermute | solution.py:394
  65.0 2.6 %collective-permute-done.26 = f32[48,128]{1,0:T(8,128)S(1)} collective-permute-done((f32[48,128]{1,0:T(8,128)S(1)}, f32[48,128]{1,0:T(8,128)S(1)}, u32[]{:S(2)}, u32[]{:S(2)}) %collective-permute-start.26) | collective-permute-done | bytes 24608 | tf_op jit(solution)/shard_map/ppermute | solution.py:394
  67.6 1.6 %collective-permute-start.27 = (f32[48,128]{1,0:T(8,128)S(1)}, f32[48,128]{1,0:T(8,128)S(1)}, u32[]{:S(2)}, u32[]{:S(2)}) collective-permute-start(f32[48,128]{1,0:T(8,128)S(1)} %add.10), channel_id=1, source_target_pairs={{0,16},{4,20},{8,24},{12,28},{16,0},{20,4},{24,8},{28,12},{1,17},{... | collective-permute-start | bytes 73736 | tf_op jit(solution)/shard_map/ppermute | solution.py:394
  69.1 3.1 %collective-permute-done.27 = f32[48,128]{1,0:T(8,128)S(1)} collective-permute-done((f32[48,128]{1,0:T(8,128)S(1)}, f32[48,128]{1,0:T(8,128)S(1)}, u32[]{:S(2)}, u32[]{:S(2)}) %collective-permute-start.27) | collective-permute-done | bytes 24608 | tf_op jit(solution)/shard_map/ppermute | solution.py:394
  72.3 2.4 %collective-permute-start.28 = (f32[48,128]{1,0:T(8,128)S(1)}, f32[48,128]{1,0:T(8,128)S(1)}, u32[]{:S(2)}, u32[]{:S(2)}) collective-permute-start(f32[48,128]{1,0:T(8,128)S(1)} %add.11.refs_0_), channel_id=1, source_target_pairs={{0,3},{1,2},{2,1},{3,0},{4,7},{5,6},{6,5},{7,4},{8,11},{9,10},{10,... | collective-permute-start | bytes 73736 | tf_op jit(solution)/shard_map/ppermute | solution.py:486
  74.7 0.6 collective-permute-start.29
  75.3 0.5 collective-permute-start.30
  75.8 1.1 %shard_map.64.refs_4_ = bf16[288,2048]{1,0:T(8,128)(2,1)S(1)} custom-call(f32[96,256]{1,0:T(8,128)S(1)} %collective-permute-done.21.r0, f32[96,256]{1,0:T(8,128)S(1)} %collective-permute-done.22.r1, f32[96,256]{1,0:T(8,128)S(1)} %collective-permute-done.23.r2, f32[96,256]{1,0:T(8,128)S(1)} %collective-permute-done.24.r3, ...), custom_call_target="tpu_custom_call" | custom-call | tf_op jit(solution)/shard_map/pallas_call | solution.py:487
  76.9 0.2 collective-permute-done.28.refs_1_
  77.0 1.5 %collective-permute-done.29.refs_2_ = f32[48,128]{1,0:T(8,128)S(1)} collective-permute-done((f32[48,128]{1,0:T(8,128)S(1)}, f32[48,128]{1,0:T(8,128)S(1)}, u32[]{:S(2)}, u32[]{:S(2)}) %collective-permute-start.29) | collective-permute-done | bytes 24608 | tf_op jit(solution)/shard_map/ppermute | solution.py:486
  78.5 0.6 collective-permute-done.30.refs_3_
  79.1 5.1 %shard_map.65 = f32[1,1,96,2048]{3,2,1,0:T(8,128)} custom-call(f32[48,128]{1,0:T(8,128)S(1)} %add.11.refs_0_, f32[48,128]{1,0:T(8,128)S(1)} %collective-permute-done.28.refs_1_, f32[48,128]{1,0:T(8,128)S(1)} %collective-permute-done.29.refs_2_, f32[48,128]{1,0:T(8,128)S(1)} %collective-permute-done.30.refs_3_, bf16[288,2048]{1,0:T(8,128)(2,1)S(1)} %shard_map.64.refs_4_), custom_call_target="tpu_custom_call" | custom-call | tf_op jit(solution)/shard_map/pallas_call | solution.py:489
  (35 shorter events, 0.2 us)
Async XLA Ops:
  0.7 0.7 copy-start
  7.0 4.6 %collective-permute-start = (f32[96,256]{1,0:T(8,128)S(1)}, f32[96,256]{1,0:T(8,128)S(1)}, u32[]{:S(2)}, u32[]{:S(2)}) collective-permute-start(f32[96,256]{1,0:T(8,128)S(1)} %get-tuple-element.40.refs_8_), channel_id=1, source_target_pairs={{0,4},{4,0},{8,12},{12,8},{16,20},{20,16},{24,28},{28,24},{1,5},{5... | collective-permute-start | bytes 294920 | tf_op jit(solution)/shard_map/ppermute | solution.py:410
  7.6 9.9 %collective-permute-start.2 = (f32[96,256]{1,0:T(8,128)S(1)}, f32[96,256]{1,0:T(8,128)S(1)}, u32[]{:S(2)}, u32[]{:S(2)}) collective-permute-start(f32[96,256]{1,0:T(8,128)S(1)} %get-tuple-element.41.refs_9_), channel_id=1, source_target_pairs={{0,3},{1,2},{2,1},{3,0},{4,7},{5,6},{6,5},{7,4},{8,11},{9,10},{10,... | collective-permute-start | bytes 294920 | tf_op jit(solution)/shard_map/ppermute | solution.py:411
  11.1 6.4 %collective-permute-start.3 = (f32[96,256]{1,0:T(8,128)S(1)}, f32[96,256]{1,0:T(8,128)S(1)}, u32[]{:S(2)}, u32[]{:S(2)}) collective-permute-start(f32[96,256]{1,0:T(8,128)S(1)} %get-tuple-element.42.refs_10_), channel_id=1, source_target_pairs={{0,1},{1,0},{2,3},{3,2},{4,5},{5,4},{6,7},{7,6},{8,9},{9,8},{10,11... | collective-permute-start | bytes 294920 | tf_op jit(solution)/shard_map/ppermute | solution.py:412
  11.6 5.9 %collective-permute-start.4 = (f32[96,256]{1,0:T(8,128)S(1)}, f32[96,256]{1,0:T(8,128)S(1)}, u32[]{:S(2)}, u32[]{:S(2)}) collective-permute-start(f32[96,256]{1,0:T(8,128)S(1)} %get-tuple-element.43.refs_11_), channel_id=1, source_target_pairs={{0,4},{4,0},{8,12},{12,8},{16,20},{20,16},{24,28},{28,24},{1,5},{5... | collective-permute-start | bytes 294920 | tf_op jit(solution)/shard_map/ppermute | solution.py:414
  11.6 5.9 %collective-permute-start.1 = (f32[96,256]{1,0:T(8,128)S(1)}, f32[96,256]{1,0:T(8,128)S(1)}, u32[]{:S(2)}, u32[]{:S(2)}) collective-permute-start(f32[96,256]{1,0:T(8,128)S(1)} %collective-permute-done), channel_id=1, source_target_pairs={{0,8},{8,16},{16,24},{24,28},{4,0},{12,4},{20,12},{28,20},{1,9},{9... | collective-permute-start | bytes 294920 | tf_op jit(solution)/shard_map/ppermute | solution.py:413
  18.1 2.2 %collective-permute-start.5 = (f32[96,256]{1,0:T(8,128)S(1)}, f32[96,256]{1,0:T(8,128)S(1)}, u32[]{:S(2)}, u32[]{:S(2)}) collective-permute-start(f32[96,256]{1,0:T(8,128)S(1)} %get-tuple-element.52.refs_12_), channel_id=1, source_target_pairs={{0,4},{4,0},{8,12},{12,8},{16,20},{20,16},{24,28},{28,24},{1,5},{5... | collective-permute-start | bytes 294920 | tf_op jit(solution)/shard_map/ppermute | solution.py:410
  18.2 24.3 %collective-permute-start.7 = (f32[96,256]{1,0:T(8,128)S(1)}, f32[96,256]{1,0:T(8,128)S(1)}, u32[]{:S(2)}, u32[]{:S(2)}) collective-permute-start(f32[96,256]{1,0:T(8,128)S(1)} %get-tuple-element.53.refs_13_), channel_id=1, source_target_pairs={{0,3},{1,2},{2,1},{3,0},{4,7},{5,6},{6,5},{7,4},{8,11},{9,10},{10,... | collective-permute-start | bytes 294920 | tf_op jit(solution)/shard_map/ppermute | solution.py:411
  19.7 22.8 %collective-permute-start.8 = (f32[96,256]{1,0:T(8,128)S(1)}, f32[96,256]{1,0:T(8,128)S(1)}, u32[]{:S(2)}, u32[]{:S(2)}) collective-permute-start(f32[96,256]{1,0:T(8,128)S(1)} %get-tuple-element.54.refs_14_), channel_id=1, source_target_pairs={{0,1},{1,0},{2,3},{3,2},{4,5},{5,4},{6,7},{7,6},{8,9},{9,8},{10,11... | collective-permute-start | bytes 294920 | tf_op jit(solution)/shard_map/ppermute | solution.py:412
  20.3 22.2 %collective-permute-start.9 = (f32[96,256]{1,0:T(8,128)S(1)}, f32[96,256]{1,0:T(8,128)S(1)}, u32[]{:S(2)}, u32[]{:S(2)}) collective-permute-start(f32[96,256]{1,0:T(8,128)S(1)} %get-tuple-element.55.refs_15_), channel_id=1, source_target_pairs={{0,4},{4,0},{8,12},{12,8},{16,20},{20,16},{24,28},{28,24},{1,5},{5... | collective-permute-start | bytes 294920 | tf_op jit(solution)/shard_map/ppermute | solution.py:414
  20.3 22.2 %collective-permute-start.6 = (f32[96,256]{1,0:T(8,128)S(1)}, f32[96,256]{1,0:T(8,128)S(1)}, u32[]{:S(2)}, u32[]{:S(2)}) collective-permute-start(f32[96,256]{1,0:T(8,128)S(1)} %collective-permute-done.5), channel_id=1, source_target_pairs={{0,8},{8,16},{16,24},{24,28},{4,0},{12,4},{20,12},{28,20},{1,9},{9... | collective-permute-start | bytes 294920 | tf_op jit(solution)/shard_map/ppermute | solution.py:413
  21.8 1.2 %collective-permute-start.10 = (f32[8,128]{1,0:T(8,128)S(1)}, f32[8,128]{1,0:T(8,128)S(1)}, u32[]{:S(2)}, u32[]{:S(2)}) collective-permute-start(f32[8,128]{1,0:T(8,128)S(1)} %get-tuple-element.51.refs_6_.refs_7_.own.peak), channel_id=1, source_target_pairs={{0,4},{4,0},{8,12},{12,8},{16,20},{20,16},{24,28},{28,24},{1,5},{5... | collective-permute-start | bytes 12296 | tf_op jit(solution)/shard_map/ppermute | solution.py:394
  23.0 3.6 %collective-permute-start.11 = (f32[8,128]{1,0:T(8,128)S(1)}, f32[8,128]{1,0:T(8,128)S(1)}, u32[]{:S(2)}, u32[]{:S(2)}) collective-permute-start(f32[8,128]{1,0:T(8,128)S(1)} %max.15), channel_id=1, source_target_pairs={{0,8},{4,12},{8,0},{12,4},{16,24},{20,28},{24,16},{28,20},{1,9},{5... | collective-permute-start | bytes 12296 | tf_op jit(solution)/shard_map/ppermute | solution.py:394
  26.6 4.5 %collective-permute-start.12 = (f32[8,128]{1,0:T(8,128)S(1)}, f32[8,128]{1,0:T(8,128)S(1)}, u32[]{:S(2)}, u32[]{:S(2)}) collective-permute-start(f32[8,128]{1,0:T(8,128)S(1)} %max.16), channel_id=1, source_target_pairs={{0,16},{4,20},{8,24},{12,28},{16,0},{20,4},{24,8},{28,12},{1,17},{... | collective-permute-start | bytes 12296 | tf_op jit(solution)/shard_map/ppermute | solution.py:394
  31.1 3.6 %collective-permute-start.13 = (f32[8,128]{1,0:T(8,128)S(1)}, f32[8,128]{1,0:T(8,128)S(1)}, u32[]{:S(2)}, u32[]{:S(2)}) collective-permute-start(f32[8,128]{1,0:T(8,128)S(1)} %max.17), channel_id=1, source_target_pairs={{0,1},{1,0},{2,3},{3,2},{4,5},{5,4},{6,7},{7,6},{8,9},{9,8},{10,11... | collective-permute-start | bytes 12296 | tf_op jit(solution)/shard_map/ppermute | solution.py:394
  34.8 3.6 %collective-permute-start.14 = (f32[8,128]{1,0:T(8,128)S(1)}, f32[8,128]{1,0:T(8,128)S(1)}, u32[]{:S(2)}, u32[]{:S(2)}) collective-permute-start(f32[8,128]{1,0:T(8,128)S(1)} %max.18), channel_id=1, source_target_pairs={{0,2},{1,3},{2,0},{3,1},{4,6},{5,7},{6,4},{7,5},{8,10},{9,11},{10,... | collective-permute-start | bytes 12296 | tf_op jit(solution)/shard_map/ppermute | solution.py:394
  43.2 3.1 %collective-permute-start.15 = (f32[96,256]{1,0:T(8,128)S(1)}, f32[96,256]{1,0:T(8,128)S(1)}, u32[]{:S(2)}, u32[]{:S(2)}) collective-permute-start(f32[96,256]{1,0:T(8,128)S(1)} %get-tuple-element.59), channel_id=1, source_target_pairs={{0,4},{4,0},{8,12},{12,8},{16,20},{20,16},{24,28},{28,24},{1,5},{5... | collective-permute-start | bytes 294920 | tf_op jit(solution)/shard_map/ppermute | solution.py:410
  43.3 9.3 %collective-permute-start.17 = (f32[96,256]{1,0:T(8,128)S(1)}, f32[96,256]{1,0:T(8,128)S(1)}, u32[]{:S(2)}, u32[]{:S(2)}) collective-permute-start(f32[96,256]{1,0:T(8,128)S(1)} %get-tuple-element.60), channel_id=1, source_target_pairs={{0,3},{1,2},{2,1},{3,0},{4,7},{5,6},{6,5},{7,4},{8,11},{9,10},{10,... | collective-permute-start | bytes 294920 | tf_op jit(solution)/shard_map/ppermute | solution.py:411
  45.8 6.8 %collective-permute-start.18 = (f32[96,256]{1,0:T(8,128)S(1)}, f32[96,256]{1,0:T(8,128)S(1)}, u32[]{:S(2)}, u32[]{:S(2)}) collective-permute-start(f32[96,256]{1,0:T(8,128)S(1)} %get-tuple-element.61), channel_id=1, source_target_pairs={{0,1},{1,0},{2,3},{3,2},{4,5},{5,4},{6,7},{7,6},{8,9},{9,8},{10,11... | collective-permute-start | bytes 294920 | tf_op jit(solution)/shard_map/ppermute | solution.py:412
  46.4 6.3 %collective-permute-start.19 = (f32[96,256]{1,0:T(8,128)S(1)}, f32[96,256]{1,0:T(8,128)S(1)}, u32[]{:S(2)}, u32[]{:S(2)}) collective-permute-start(f32[96,256]{1,0:T(8,128)S(1)} %get-tuple-element.62), channel_id=1, source_target_pairs={{0,4},{4,0},{8,12},{12,8},{16,20},{20,16},{24,28},{28,24},{1,5},{5... | collective-permute-start | bytes 294920 | tf_op jit(solution)/shard_map/ppermute | solution.py:414
  46.4 6.3 %collective-permute-start.16 = (f32[96,256]{1,0:T(8,128)S(1)}, f32[96,256]{1,0:T(8,128)S(1)}, u32[]{:S(2)}, u32[]{:S(2)}) collective-permute-start(f32[96,256]{1,0:T(8,128)S(1)} %collective-permute-done.15), channel_id=1, source_target_pairs={{0,8},{8,16},{16,24},{24,28},{4,0},{12,4},{20,12},{28,20},{1,9},{9... | collective-permute-start | bytes 294920 | tf_op jit(solution)/shard_map/ppermute | solution.py:413
  53.3 2.1 %collective-permute-start.20 = (f32[96,256]{1,0:T(8,128)S(1)}, f32[96,256]{1,0:T(8,128)S(1)}, u32[]{:S(2)}, u32[]{:S(2)}) collective-permute-start(f32[96,256]{1,0:T(8,128)S(1)} %get-tuple-element.66), channel_id=1, source_target_pairs={{0,4},{4,0},{8,12},{12,8},{16,20},{20,16},{24,28},{28,24},{1,5},{5... | collective-permute-start | bytes 294920 | tf_op jit(solution)/shard_map/ppermute | solution.py:410
  53.4 7.9 %collective-permute-start.22 = (f32[96,256]{1,0:T(8,128)S(1)}, f32[96,256]{1,0:T(8,128)S(1)}, u32[]{:S(2)}, u32[]{:S(2)}) collective-permute-start(f32[96,256]{1,0:T(8,128)S(1)} %get-tuple-element.67), channel_id=1, source_target_pairs={{0,3},{1,2},{2,1},{3,0},{4,7},{5,6},{6,5},{7,4},{8,11},{9,10},{10,... | collective-permute-start | bytes 294920 | tf_op jit(solution)/shard_map/ppermute | solution.py:411
  54.9 6.4 %collective-permute-start.23 = (f32[96,256]{1,0:T(8,128)S(1)}, f32[96,256]{1,0:T(8,128)S(1)}, u32[]{:S(2)}, u32[]{:S(2)}) collective-permute-start(f32[96,256]{1,0:T(8,128)S(1)} %get-tuple-element.68), channel_id=1, source_target_pairs={{0,1},{1,0},{2,3},{3,2},{4,5},{5,4},{6,7},{7,6},{8,9},{9,8},{10,11... | collective-permute-start | bytes 294920 | tf_op jit(solution)/shard_map/ppermute | solution.py:412
  55.4 5.9 %collective-permute-start.24 = (f32[96,256]{1,0:T(8,128)S(1)}, f32[96,256]{1,0:T(8,128)S(1)}, u32[]{:S(2)}, u32[]{:S(2)}) collective-permute-start(f32[96,256]{1,0:T(8,128)S(1)} %get-tuple-element.69), channel_id=1, source_target_pairs={{0,4},{4,0},{8,12},{12,8},{16,20},{20,16},{24,28},{28,24},{1,5},{5... | collective-permute-start | bytes 294920 | tf_op jit(solution)/shard_map/ppermute | solution.py:414
  55.4 5.9 %collective-permute-start.21 = (f32[96,256]{1,0:T(8,128)S(1)}, f32[96,256]{1,0:T(8,128)S(1)}, u32[]{:S(2)}, u32[]{:S(2)}) collective-permute-start(f32[96,256]{1,0:T(8,128)S(1)} %collective-permute-done.20), channel_id=1, source_target_pairs={{0,8},{8,16},{16,24},{24,28},{4,0},{12,4},{20,12},{28,20},{1,9},{9... | collective-permute-start | bytes 294920 | tf_op jit(solution)/shard_map/ppermute | solution.py:413
  62.5 1.3 %collective-permute-start.25 = (f32[48,128]{1,0:T(8,128)S(1)}, f32[48,128]{1,0:T(8,128)S(1)}, u32[]{:S(2)}, u32[]{:S(2)}) collective-permute-start(f32[48,128]{1,0:T(8,128)S(1)} %shard_map.63), channel_id=1, source_target_pairs={{0,4},{4,0},{8,12},{12,8},{16,20},{20,16},{24,28},{28,24},{1,5},{5... | collective-permute-start | bytes 73736 | tf_op jit(solution)/shard_map/ppermute | solution.py:394
  63.7 3.8 %collective-permute-start.26 = (f32[48,128]{1,0:T(8,128)S(1)}, f32[48,128]{1,0:T(8,128)S(1)}, u32[]{:S(2)}, u32[]{:S(2)}) collective-permute-start(f32[48,128]{1,0:T(8,128)S(1)} %add.9), channel_id=1, source_target_pairs={{0,8},{4,12},{8,0},{12,4},{16,24},{20,28},{24,16},{28,20},{1,9},{5... | collective-permute-start | bytes 73736 | tf_op jit(solution)/shard_map/ppermute | solution.py:394
  67.6 4.7 %collective-permute-start.27 = (f32[48,128]{1,0:T(8,128)S(1)}, f32[48,128]{1,0:T(8,128)S(1)}, u32[]{:S(2)}, u32[]{:S(2)}) collective-permute-start(f32[48,128]{1,0:T(8,128)S(1)} %add.10), channel_id=1, source_target_pairs={{0,16},{4,20},{8,24},{12,28},{16,0},{20,4},{24,8},{28,12},{1,17},{... | collective-permute-start | bytes 73736 | tf_op jit(solution)/shard_map/ppermute | solution.py:394
  72.3 4.7 %collective-permute-start.28 = (f32[48,128]{1,0:T(8,128)S(1)}, f32[48,128]{1,0:T(8,128)S(1)}, u32[]{:S(2)}, u32[]{:S(2)}) collective-permute-start(f32[48,128]{1,0:T(8,128)S(1)} %add.11.refs_0_), channel_id=1, source_target_pairs={{0,3},{1,2},{2,1},{3,0},{4,7},{5,6},{6,5},{7,4},{8,11},{9,10},{10,... | collective-permute-start | bytes 73736 | tf_op jit(solution)/shard_map/ppermute | solution.py:486
  74.7 3.8 %collective-permute-start.29 = (f32[48,128]{1,0:T(8,128)S(1)}, f32[48,128]{1,0:T(8,128)S(1)}, u32[]{:S(2)}, u32[]{:S(2)}) collective-permute-start(f32[48,128]{1,0:T(8,128)S(1)} %add.11.refs_0_), channel_id=1, source_target_pairs={{0,2},{1,3},{2,0},{3,1},{4,6},{5,7},{6,4},{7,5},{8,10},{9,11},{10,... | collective-permute-start | bytes 73736 | tf_op jit(solution)/shard_map/ppermute | solution.py:486
  75.3 3.8 %collective-permute-start.30 = (f32[48,128]{1,0:T(8,128)S(1)}, f32[48,128]{1,0:T(8,128)S(1)}, u32[]{:S(2)}, u32[]{:S(2)}) collective-permute-start(f32[48,128]{1,0:T(8,128)S(1)} %add.11.refs_0_), channel_id=1, source_target_pairs={{0,1},{1,0},{2,3},{3,2},{4,5},{5,4},{6,7},{7,6},{8,9},{9,8},{10,11... | collective-permute-start | bytes 73736 | tf_op jit(solution)/shard_map/ppermute | solution.py:486

commit v3 on v2

--- a/solution.py
+++ b/solution.py
@@ -315,27 +315,27 @@
         terms[:, part] = jnp.concatenate([hi, lo, hi], axis=0)
 
 
-def small_inverse(rows, start, size, width):
+def eliminate(block, start, right):
+    size, width = block.shape
     near = [
-        [jnp.broadcast_to(rows[i : i + 1, start + j : start + j + 1], (size, width)) for j in range(i + 1)]
+        [jnp.broadcast_to(block[i : i + 1, start + j : start + j + 1], (size, width)) for j in range(i + 1)]
         for i in range(size)
     ]
-    far = [[None] * size for _ in range(size)]
+    rows, factors, inverses = list(right), [[] for _ in range(size)], []
     for k in range(size):
-        pivot = near[k][k]
-        inverse = 1.0 / pivot
+        inverses.append(1.0 / near[k][k])
         for i in range(k + 1, size):
-            factor = near[i][k] * inverse
+            factor = near[i][k] * inverses[k]
+            factors[i].append(factor)
             for j in range(k + 1, i + 1):
                 near[i][j] = near[i][j] - factor * near[j][k]
-            for j in range(k):
-                far[i][j] = far[i][j] - factor * far[k][j]
-            far[i][k] = -factor
-        root = lax.rsqrt(pivot)
-        near[k] = root
-    return [
-        [far[i][j] * near[i] for j in range(i)] + [near[i]] for i in range(size)
-    ]
+            rows[i] = rows[i] - factor * rows[k]
+    half = [lax.rsqrt(near[i][i]) * rows[i] for i in range(size)]
+    whole = [rows[i] * inverses[i] for i in range(size)]
+    for i in reversed(range(size)):
+        for j in range(i):
+            whole[j] = whole[j] - factors[i][j] * whole[i]
+    return half, whole
 
 
 def encode_kernel(root, *refs):
@@ -349,15 +349,9 @@
     for g in range(vecs // size):
         start = g * size
         inside = jnp.logical_and(lane >= start, lane < start + size)
-        small = small_inverse(rows[g], start, size, vecs)
         unit = jnp.where(inside, (lane - start == sub).astype(F32), rows[g])
         spread_rows = [jnp.broadcast_to(unit[j : j + 1], (size, vecs)) for j in range(size)]
-        half = [
-            total(small[i][j] * spread_rows[j] for j in range(i + 1)) for i in range(size)
-        ]
-        whole = [
-            total(small[i][j] * half[i] for i in range(j, size)) for j in range(size)
-        ]
+        half, whole = eliminate(rows[g], start, spread_rows)
         for i in range(g + 1, vecs // size):
             kept = jnp.where(inside, 0.0, rows[i])
             rows[i] = kept - total(
@@ -393,6 +387,11 @@
         pairs = xor_pairs(lax.axis_size(axis), bit)
         value = combine(value, lax.ppermute(value, axis, pairs))
     return value
+
+
+def all_of(value, axis, bits):
+    size = lax.axis_size(axis)
+    return [value] + [lax.ppermute(value, axis, xor_pairs(size, bit)) for bit in bits]
 
 
 def per_device(basis, block_vals, block_cols, edge_rows, live_counts):
@@ -479,11 +478,11 @@
         arrived = coming
 
     gram = call(gram_kernel, shape(vecs // 2, LANES), [VM] * 8)(*arrived, edge_local, same, peak, *base)
-    direct = sizes[1] == 4
-    gram = spread(gram, jnp.add, [stage for stage in stages if not (direct and stage[0] == "gy")])
-    parts = [gram]
-    if direct:
-        parts += [lax.ppermute(gram, "gy", xor_pairs(4, bit)) for bit in (3, 2, 1)]
+    gram = spread(gram, jnp.add, stages[:1])
+    if sizes == (8, 4):
+        parts = all_of(total(all_of(gram, "gx", (4, 6, 2))), "gy", (3, 2, 1))
+    else:
+        parts = [spread(gram, jnp.add, stages[1:])]
     now = call(last_kernel, shape(3 * vecs, cells, dtype=BF16), [VM] * 7)(*arrived, local, back, peak)
     root = math.sqrt(cells * sizes[0] * sizes[1])
     return call(functools.partial(encode_kernel, root), shape(1, 1, vecs, cells), [VM] * (len(parts) + 1))(

time: 84.4 us -> 82.8 us (0.981)
  waiting for transfers between devices: 19.2 us -> 16 us
  starting transfers between devices: 30.4 us -> 32.1 us
    ppermute x8 -> x6, waiting for transfers between devices: 17 us -> 11.2 us  [spread(): value = combine(value, lax.ppermute(value, axis, pairs))]
    ppermute x3 -> x6, starting transfers between devices: 3.49 us -> 7.94 us  [all_of(): lax.ppermute(value, axis, xor_pairs(size, bit))]
    ppermute x8 -> x6, starting transfers between devices: 9.34 us -> 6.52 us  [spread(): value = combine(value, lax.ppermute(value, axis, pairs))]
    ppermute x3 -> x6, waiting for transfers between devices: 2.21 us -> 4.7 us  [all_of(): lax.ppermute(value, axis, xor_pairs(size, bit))]
  transfers between devices with their start and end apart: 31 -> 32, of which waited for: 11 -> 12; matrix products, arithmetic and copies ran while one was open for 0% -> 0% of each run, Pallas kernels for 23% -> 23%
where the time goes in v3:
time: 82.8 us; the launch traced here: 82.6 us
  Pallas kernels  32.9 us (40%)
  starting transfers between devices  32.1 us (39%)
  waiting for transfers between devices  16 us (19%)
  between operations  0.92 us (1%)
    pallas_call x3, Pallas kernels, per_device(): call(functools.partial(field_kernel, number), [field, field, edge_field]...  13.7 us
    ppermute x6, waiting for transfers between devices, spread(): value = combine(value, lax.ppermute(value, axis, pairs))  11.2 us
    ppermute x4, starting transfers between devices, exchange(): y_far = lax.ppermute(y_far, 'gy', far_pairs(sizes[1]))  9.06 us
    ppermute x6, starting transfers between devices, all_of(): lax.ppermute(value, axis, xor_pairs(size, bit))  7.94 us
    ppermute x6, starting transfers between devices, spread(): value = combine(value, lax.ppermute(value, axis, pairs))  6.52 us
    pallas_call x1, Pallas kernels, per_device(): call(functools.partial(first_kernel, sizes), [shape(cells, 4 * edges, dty...  5.67 us
    ppermute x4, starting transfers between devices, exchange(): x_far = lax.ppermute(x_far, 'gx', turn_pairs(sizes[0]))  5.65 us
    pallas_call x1, Pallas kernels, per_device(): call(functools.partial(encode_kernel, root), shape(1, 1, vecs, cells), [V...  5.09 us
  transfers between devices with their start and end apart: 32, of which 12 were waited for; matrix products, arithmetic and copies ran while one was open for 0% of the time, Pallas kernels for 23%

profile of v3, /device:TPU:0, one launch (start us, length us, event | category | flops | bytes accessed | tf_op | source)
XLA Modules:
  0.0 82.6 jit_solution(12858042889834080609)
XLA Ops:
  0.7 0.7 copy-done
  1.3 5.7 %shard_map.55 = (bf16[2048,1024]{1,0:T(8,128)(2,1)S(1)}, bf16[16,256,640]{2,1,0:T(8,128)(2,1)S(1)}, f32[96,2048]{1,0:T(8,128)S(1)}, f32[8,2048]{1,0:T(8,128)S(1)...) custom-call(s32[1,5,1,16]{3,2,1,0:T(1,128)S(1)} %bitcast.1, ...), custom_call_target="tpu_custom_call" | custom-call | tf_op jit(solution)/shard_map/pallas_call | solution.py:417
  7.0 0.6 collective-permute-start
  7.6 3.5 %collective-permute-start.2 = (f32[96,256]{1,0:T(8,128)S(1)}, f32[96,256]{1,0:T(8,128)S(1)}, u32[]{:S(2)}, u32[]{:S(2)}) collective-permute-start(f32[96,256]{1,0:T(8,128)S(1)} %get-tuple-element.41.refs_9_), channel_id=1, source_target_pairs={{0,3},{1,2},{2,1},{3,0},{4,7},{5,6},{6,5},{7,4},{8,11},{9,10},{10,... | collective-permute-start | bytes 294920 | tf_op jit(solution)/shard_map/ppermute | solution.py:410
  11.1 0.5 collective-permute-start.3
  11.6 1.6 %collective-permute-start.1 = (f32[96,256]{1,0:T(8,128)S(1)}, f32[96,256]{1,0:T(8,128)S(1)}, u32[]{:S(2)}, u32[]{:S(2)}) collective-permute-start(f32[96,256]{1,0:T(8,128)S(1)} %collective-permute-done), channel_id=1, source_target_pairs={{0,8},{8,16},{16,24},{24,28},{4,0},{12,4},{20,12},{28,20},{1,9},{9... | collective-permute-start | bytes 294920 | tf_op jit(solution)/shard_map/ppermute | solution.py:412
  13.2 4.3 %shard_map.56 = (f32[96,2048]{1,0:T(8,128)S(1)}, f32[96,1024]{1,0:T(8,128)S(1)}, bf16[1024,1024]{1,0:T(8,128)(2,1)S(1)}, bf16[1024,2048]{1,0:T(8,128)(2,1)S(1)}) custom-call(s32[1,5,1,16]{3,2,1,0:T(1,128)S(1)} %bitcast.2, s32[1,1]{1,0:T(1,128)S(6)} %copy.6.counts, f32[96,2048]{1,0:T(8,128)S(1)} %get-tuple-element.44.begin.once, ...), custom_call_target="tpu_custom_call" | custom-call | tf_op jit(solution)/shard_map/pallas_call | solution.py:446
  17.5 0.6 shard_map.57
  18.1 0.1 collective-permute-start.5
  18.2 1.5 %collective-permute-start.7 = (f32[96,256]{1,0:T(8,128)S(1)}, f32[96,256]{1,0:T(8,128)S(1)}, u32[]{:S(2)}, u32[]{:S(2)}) collective-permute-start(f32[96,256]{1,0:T(8,128)S(1)} %get-tuple-element.53.refs_13_), channel_id=1, source_target_pairs={{0,3},{1,2},{2,1},{3,0},{4,7},{5,6},{6,5},{7,4},{8,11},{9,10},{10,... | collective-permute-start | bytes 294920 | tf_op jit(solution)/shard_map/ppermute | solution.py:410
  19.7 0.6 collective-permute-start.8
  20.3 1.6 %collective-permute-start.6 = (f32[96,256]{1,0:T(8,128)S(1)}, f32[96,256]{1,0:T(8,128)S(1)}, u32[]{:S(2)}, u32[]{:S(2)}) collective-permute-start(f32[96,256]{1,0:T(8,128)S(1)} %collective-permute-done.5), channel_id=1, source_target_pairs={{0,8},{8,16},{16,24},{24,28},{4,0},{12,4},{20,12},{28,20},{1,9},{9... | collective-permute-start | bytes 294920 | tf_op jit(solution)/shard_map/ppermute | solution.py:412
  21.8 1.2 %collective-permute-done.10 = f32[8,128]{1,0:T(8,128)S(1)} collective-permute-done((f32[8,128]{1,0:T(8,128)S(1)}, f32[8,128]{1,0:T(8,128)S(1)}, u32[]{:S(2)}, u32[]{:S(2)}) %collective-permute-start.10) | collective-permute-done | bytes 4128 | tf_op jit(solution)/shard_map/ppermute | solution.py:388
  23.0 1.6 %collective-permute-start.11 = (f32[8,128]{1,0:T(8,128)S(1)}, f32[8,128]{1,0:T(8,128)S(1)}, u32[]{:S(2)}, u32[]{:S(2)}) collective-permute-start(f32[8,128]{1,0:T(8,128)S(1)} %max.15), channel_id=1, source_target_pairs={{0,8},{4,12},{8,0},{12,4},{16,24},{20,28},{24,16},{28,20},{1,9},{5... | collective-permute-start | bytes 12296 | tf_op jit(solution)/shard_map/ppermute | solution.py:388
  24.6 2.0 %collective-permute-done.11 = f32[8,128]{1,0:T(8,128)S(1)} collective-permute-done((f32[8,128]{1,0:T(8,128)S(1)}, f32[8,128]{1,0:T(8,128)S(1)}, u32[]{:S(2)}, u32[]{:S(2)}) %collective-permute-start.11) | collective-permute-done | bytes 4128 | tf_op jit(solution)/shard_map/ppermute | solution.py:388
  26.6 1.9 %collective-permute-start.12 = (f32[8,128]{1,0:T(8,128)S(1)}, f32[8,128]{1,0:T(8,128)S(1)}, u32[]{:S(2)}, u32[]{:S(2)}) collective-permute-start(f32[8,128]{1,0:T(8,128)S(1)} %max.16), channel_id=1, source_target_pairs={{0,16},{4,20},{8,24},{12,28},{16,0},{20,4},{24,8},{28,12},{1,17},{... | collective-permute-start | bytes 12296 | tf_op jit(solution)/shard_map/ppermute | solution.py:388
  28.5 2.6 %collective-permute-done.12 = f32[8,128]{1,0:T(8,128)S(1)} collective-permute-done((f32[8,128]{1,0:T(8,128)S(1)}, f32[8,128]{1,0:T(8,128)S(1)}, u32[]{:S(2)}, u32[]{:S(2)}) %collective-permute-start.12) | collective-permute-done | bytes 4128 | tf_op jit(solution)/shard_map/ppermute | solution.py:388
  31.1 1.5 %collective-permute-start.13 = (f32[8,128]{1,0:T(8,128)S(1)}, f32[8,128]{1,0:T(8,128)S(1)}, u32[]{:S(2)}, u32[]{:S(2)}) collective-permute-start(f32[8,128]{1,0:T(8,128)S(1)} %max.17), channel_id=1, source_target_pairs={{0,1},{1,0},{2,3},{3,2},{4,5},{5,4},{6,7},{7,6},{8,9},{9,8},{10,11... | collective-permute-start | bytes 12296 | tf_op jit(solution)/shard_map/ppermute | solution.py:388
  32.6 2.1 %collective-permute-done.13 = f32[8,128]{1,0:T(8,128)S(1)} collective-permute-done((f32[8,128]{1,0:T(8,128)S(1)}, f32[8,128]{1,0:T(8,128)S(1)}, u32[]{:S(2)}, u32[]{:S(2)}) %collective-permute-start.13) | collective-permute-done | bytes 4128 | tf_op jit(solution)/shard_map/ppermute | solution.py:388
  34.8 1.5 %collective-permute-start.14 = (f32[8,128]{1,0:T(8,128)S(1)}, f32[8,128]{1,0:T(8,128)S(1)}, u32[]{:S(2)}, u32[]{:S(2)}) collective-permute-start(f32[8,128]{1,0:T(8,128)S(1)} %max.18), channel_id=1, source_target_pairs={{0,2},{1,3},{2,0},{3,1},{4,6},{5,7},{6,4},{7,5},{8,10},{9,11},{10,... | collective-permute-start | bytes 12296 | tf_op jit(solution)/shard_map/ppermute | solution.py:388
  36.3 2.1 %collective-permute-done.14 = f32[8,128]{1,0:T(8,128)S(1)} collective-permute-done((f32[8,128]{1,0:T(8,128)S(1)}, f32[8,128]{1,0:T(8,128)S(1)}, u32[]{:S(2)}, u32[]{:S(2)}) %collective-permute-start.14) | collective-permute-done | bytes 4128 | tf_op jit(solution)/shard_map/ppermute | solution.py:388
  38.4 4.1 %shard_map.58 = (f32[96,2048]{1,0:T(8,128)S(1)}, f32[96,2048]{1,0:T(8,128)S(1)}, f32[96,1024]{1,0:T(8,128)S(1)}) custom-call(s32[1,5,1,16]{3,2,1,0:T(1,128)S(1)} %bitcast.3, s32[1,1]{1,0:T(1,128)S(6)} %copy.6.counts, f32[96,256]{1,0:T(8,128)S(1)} %collective-permute-done.1.refs_0_.r0, f32[96,256]{1,0:T(8,128)S(1)} %collective-permute-done.2.refs_1_.r1, ...), custom_call_target="tpu_custom_call" | custom-call | tf_op jit(solution)/shard_map/pallas_call | solution.py:471
  42.5 0.7 shard_map.59
  43.3 2.5 %collective-permute-start.17 = (f32[96,256]{1,0:T(8,128)S(1)}, f32[96,256]{1,0:T(8,128)S(1)}, u32[]{:S(2)}, u32[]{:S(2)}) collective-permute-start(f32[96,256]{1,0:T(8,128)S(1)} %get-tuple-element.60), channel_id=1, source_target_pairs={{0,3},{1,2},{2,1},{3,0},{4,7},{5,6},{6,5},{7,4},{8,11},{9,10},{10,... | collective-permute-start | bytes 294920 | tf_op jit(solution)/shard_map/ppermute | solution.py:410
  45.8 0.5 collective-permute-start.18
  46.4 1.6 %collective-permute-start.16 = (f32[96,256]{1,0:T(8,128)S(1)}, f32[96,256]{1,0:T(8,128)S(1)}, u32[]{:S(2)}, u32[]{:S(2)}) collective-permute-start(f32[96,256]{1,0:T(8,128)S(1)} %collective-permute-done.15), channel_id=1, source_target_pairs={{0,8},{8,16},{16,24},{24,28},{4,0},{12,4},{20,12},{28,20},{1,9},{9... | collective-permute-start | bytes 294920 | tf_op jit(solution)/shard_map/ppermute | solution.py:412
  48.0 4.6 %shard_map.60 = (f32[96,2048]{1,0:T(8,128)S(1)}, f32[96,2048]{1,0:T(8,128)S(1)}, f32[96,1024]{1,0:T(8,128)S(1)}) custom-call(s32[1,5,1,16]{3,2,1,0:T(1,128)S(1)} %bitcast.4, s32[1,1]{1,0:T(1,128)S(6)} %copy.6.counts, f32[96,256]{1,0:T(8,128)S(1)} %collective-permute-done.6.refs_0_.r0, f32[96,256]{1,0:T(8,128)S(1)} %collective-permute-done.7.refs_1_.r1, ...), custom_call_target="tpu_custom_call" | custom-call | tf_op jit(solution)/shard_map/pallas_call | solution.py:471
  52.7 0.6 shard_map.61
  53.4 1.5 %collective-permute-start.22 = (f32[96,256]{1,0:T(8,128)S(1)}, f32[96,256]{1,0:T(8,128)S(1)}, u32[]{:S(2)}, u32[]{:S(2)}) collective-permute-start(f32[96,256]{1,0:T(8,128)S(1)} %get-tuple-element.67), channel_id=1, source_target_pairs={{0,3},{1,2},{2,1},{3,0},{4,7},{5,6},{6,5},{7,4},{8,11},{9,10},{10,... | collective-permute-start | bytes 294920 | tf_op jit(solution)/shard_map/ppermute | solution.py:410
  54.9 0.5 collective-permute-start.23
  55.4 0.9 %collective-permute-start.21 = (f32[96,256]{1,0:T(8,128)S(1)}, f32[96,256]{1,0:T(8,128)S(1)}, u32[]{:S(2)}, u32[]{:S(2)}) collective-permute-start(f32[96,256]{1,0:T(8,128)S(1)} %collective-permute-done.20), channel_id=1, source_target_pairs={{0,8},{8,16},{16,24},{24,28},{4,0},{12,4},{20,12},{28,20},{1,9},{9... | collective-permute-start | bytes 294920 | tf_op jit(solution)/shard_map/ppermute | solution.py:412
  56.3 5.0 %shard_map.62 = (f32[96,2048]{1,0:T(8,128)}, f32[96,2048]{1,0:T(8,128)S(1)}, f32[96,1024]{1,0:T(8,128)S(1)}, f32[96,96]{1,0:T(8,128)S(1)}) custom-call(s32[1,5,1,16]{3,2,1,0:T(1,128)S(1)} %bitcast.5, s32[1,1]{1,0:T(1,128)S(6)} %copy.6.counts, f32[96,256]{1,0:T(8,128)S(1)} %collective-permute-done.16.refs_0_.r0, ...), custom_call_target="tpu_custom_call" | custom-call | tf_op jit(solution)/shard_map/pallas_call | solution.py:471
  61.3 1.1 %shard_map.63 = f32[48,128]{1,0:T(8,128)S(1)} custom-call(f32[96,256]{1,0:T(8,128)S(1)} %collective-permute-done.21.r0, f32[96,256]{1,0:T(8,128)S(1)} %collective-permute-done.22.r1, f32[96,256]{1,0:T(8,128)S(1)} %collective-permute-done.23.r2, f32[96,256]{1,0:T(8,128)S(1)} %collective-permute-done.24.r3, f32[96,1024]{1,0:T(8,128)S(1)} %get-tuple-element.72.edge_local, ...), custom_call_target="tpu_custom_call" | custom-call | tf_op jit(solution)/shard_map/pallas_call | solution.py:480
  62.5 1.2 %collective-permute-done.25 = f32[48,128]{1,0:T(8,128)S(1)} collective-permute-done((f32[48,128]{1,0:T(8,128)S(1)}, f32[48,128]{1,0:T(8,128)S(1)}, u32[]{:S(2)}, u32[]{:S(2)}) %collective-permute-start.25) | collective-permute-done | bytes 24608 | tf_op jit(solution)/shard_map/ppermute | solution.py:388
  63.7 2.0 %collective-permute-start.27 = (f32[48,128]{1,0:T(8,128)S(1)}, f32[48,128]{1,0:T(8,128)S(1)}, u32[]{:S(2)}, u32[]{:S(2)}) collective-permute-start(f32[48,128]{1,0:T(8,128)S(1)} %add.12), channel_id=1, source_target_pairs={{0,24},{4,28},{8,16},{12,20},{16,8},{20,12},{24,0},{28,4},{1,25},{... | collective-permute-start | bytes 73736 | tf_op jit(solution)/shard_map/ppermute | solution.py:394
  65.8 0.1 collective-permute-start.28
  65.9 2.2 %collective-permute-start.26 = (f32[48,128]{1,0:T(8,128)S(1)}, f32[48,128]{1,0:T(8,128)S(1)}, u32[]{:S(2)}, u32[]{:S(2)}) collective-permute-start(f32[48,128]{1,0:T(8,128)S(1)} %add.12), channel_id=1, source_target_pairs={{0,16},{4,20},{8,24},{12,28},{16,0},{20,4},{24,8},{28,12},{1,17},{... | collective-permute-start | bytes 73736 | tf_op jit(solution)/shard_map/ppermute | solution.py:394
  68.1 1.2 %collective-permute-done.27 = f32[48,128]{1,0:T(8,128)S(1)} collective-permute-done((f32[48,128]{1,0:T(8,128)S(1)}, f32[48,128]{1,0:T(8,128)S(1)}, u32[]{:S(2)}, u32[]{:S(2)}) %collective-permute-start.27) | collective-permute-done | bytes 24608 | tf_op jit(solution)/shard_map/ppermute | solution.py:394
  69.4 0.5 collective-permute-done.28
  69.9 0.7 collective-permute-done.26
  70.6 2.5 %collective-permute-start.29 = (f32[48,128]{1,0:T(8,128)S(1)}, f32[48,128]{1,0:T(8,128)S(1)}, u32[]{:S(2)}, u32[]{:S(2)}) collective-permute-start(f32[48,128]{1,0:T(8,128)S(1)} %add_add_fusion.refs_0_), channel_id=1, source_target_pairs={{0,3},{1,2},{2,1},{3,0},{4,7},{5,6},{6,5},{7,4},{8,11},{9,10},{10,... | collective-permute-start | bytes 73736 | tf_op jit(solution)/shard_map/ppermute | solution.py:394
  73.1 0.5 collective-permute-start.30
  73.7 0.5 collective-permute-start.31
  74.2 1.1 %shard_map.64.refs_4_ = bf16[288,2048]{1,0:T(8,128)(2,1)S(1)} custom-call(f32[96,256]{1,0:T(8,128)S(1)} %collective-permute-done.21.r0, f32[96,256]{1,0:T(8,128)S(1)} %collective-permute-done.22.r1, f32[96,256]{1,0:T(8,128)S(1)} %collective-permute-done.23.r2, f32[96,256]{1,0:T(8,128)S(1)} %collective-permute-done.24.r3, ...), custom_call_target="tpu_custom_call" | custom-call | tf_op jit(solution)/shard_map/pallas_call | solution.py:486
  75.3 0.2 collective-permute-done.29.refs_1_
  75.4 1.6 %collective-permute-done.30.refs_2_ = f32[48,128]{1,0:T(8,128)S(1)} collective-permute-done((f32[48,128]{1,0:T(8,128)S(1)}, f32[48,128]{1,0:T(8,128)S(1)}, u32[]{:S(2)}, u32[]{:S(2)}) %collective-permute-start.30) | collective-permute-done | bytes 24608 | tf_op jit(solution)/shard_map/ppermute | solution.py:394
  77.0 0.5 collective-permute-done.31.refs_3_
  77.5 5.1 %shard_map.65 = f32[1,1,96,2048]{3,2,1,0:T(8,128)} custom-call(f32[48,128]{1,0:T(8,128)S(1)} %add_add_fusion.refs_0_, f32[48,128]{1,0:T(8,128)S(1)} %collective-permute-done.29.refs_1_, f32[48,128]{1,0:T(8,128)S(1)} %collective-permute-done.30.refs_2_, f32[48,128]{1,0:T(8,128)S(1)} %collective-permute-done.31.refs_3_, bf16[288,2048]{1,0:T(8,128)(2,1)S(1)} %shard_map.64.refs_4_), custom_call_target="tpu_custom_call" | custom-call | tf_op jit(solution)/shard_map/pallas_call | solution.py:488
  (36 shorter events, 0.3 us)
Async XLA Ops:
  0.7 0.7 copy-start
  7.0 4.6 %collective-permute-start = (f32[96,256]{1,0:T(8,128)S(1)}, f32[96,256]{1,0:T(8,128)S(1)}, u32[]{:S(2)}, u32[]{:S(2)}) collective-permute-start(f32[96,256]{1,0:T(8,128)S(1)} %get-tuple-element.40.refs_8_), channel_id=1, source_target_pairs={{0,4},{4,0},{8,12},{12,8},{16,20},{20,16},{24,28},{28,24},{1,5},{5... | collective-permute-start | bytes 294920 | tf_op jit(solution)/shard_map/ppermute | solution.py:409
  7.6 9.9 %collective-permute-start.2 = (f32[96,256]{1,0:T(8,128)S(1)}, f32[96,256]{1,0:T(8,128)S(1)}, u32[]{:S(2)}, u32[]{:S(2)}) collective-permute-start(f32[96,256]{1,0:T(8,128)S(1)} %get-tuple-element.41.refs_9_), channel_id=1, source_target_pairs={{0,3},{1,2},{2,1},{3,0},{4,7},{5,6},{6,5},{7,4},{8,11},{9,10},{10,... | collective-permute-start | bytes 294920 | tf_op jit(solution)/shard_map/ppermute | solution.py:410
  11.1 6.4 %collective-permute-start.3 = (f32[96,256]{1,0:T(8,128)S(1)}, f32[96,256]{1,0:T(8,128)S(1)}, u32[]{:S(2)}, u32[]{:S(2)}) collective-permute-start(f32[96,256]{1,0:T(8,128)S(1)} %get-tuple-element.42.refs_10_), channel_id=1, source_target_pairs={{0,1},{1,0},{2,3},{3,2},{4,5},{5,4},{6,7},{7,6},{8,9},{9,8},{10,11... | collective-permute-start | bytes 294920 | tf_op jit(solution)/shard_map/ppermute | solution.py:411
  11.6 5.9 %collective-permute-start.4 = (f32[96,256]{1,0:T(8,128)S(1)}, f32[96,256]{1,0:T(8,128)S(1)}, u32[]{:S(2)}, u32[]{:S(2)}) collective-permute-start(f32[96,256]{1,0:T(8,128)S(1)} %get-tuple-element.43.refs_11_), channel_id=1, source_target_pairs={{0,4},{4,0},{8,12},{12,8},{16,20},{20,16},{24,28},{28,24},{1,5},{5... | collective-permute-start | bytes 294920 | tf_op jit(solution)/shard_map/ppermute | solution.py:413
  11.6 5.9 %collective-permute-start.1 = (f32[96,256]{1,0:T(8,128)S(1)}, f32[96,256]{1,0:T(8,128)S(1)}, u32[]{:S(2)}, u32[]{:S(2)}) collective-permute-start(f32[96,256]{1,0:T(8,128)S(1)} %collective-permute-done), channel_id=1, source_target_pairs={{0,8},{8,16},{16,24},{24,28},{4,0},{12,4},{20,12},{28,20},{1,9},{9... | collective-permute-start | bytes 294920 | tf_op jit(solution)/shard_map/ppermute | solution.py:412
  18.1 2.2 %collective-permute-start.5 = (f32[96,256]{1,0:T(8,128)S(1)}, f32[96,256]{1,0:T(8,128)S(1)}, u32[]{:S(2)}, u32[]{:S(2)}) collective-permute-start(f32[96,256]{1,0:T(8,128)S(1)} %get-tuple-element.52.refs_12_), channel_id=1, source_target_pairs={{0,4},{4,0},{8,12},{12,8},{16,20},{20,16},{24,28},{28,24},{1,5},{5... | collective-permute-start | bytes 294920 | tf_op jit(solution)/shard_map/ppermute | solution.py:409
  18.2 24.3 %collective-permute-start.7 = (f32[96,256]{1,0:T(8,128)S(1)}, f32[96,256]{1,0:T(8,128)S(1)}, u32[]{:S(2)}, u32[]{:S(2)}) collective-permute-start(f32[96,256]{1,0:T(8,128)S(1)} %get-tuple-element.53.refs_13_), channel_id=1, source_target_pairs={{0,3},{1,2},{2,1},{3,0},{4,7},{5,6},{6,5},{7,4},{8,11},{9,10},{10,... | collective-permute-start | bytes 294920 | tf_op jit(solution)/shard_map/ppermute | solution.py:410
  19.7 22.8 %collective-permute-start.8 = (f32[96,256]{1,0:T(8,128)S(1)}, f32[96,256]{1,0:T(8,128)S(1)}, u32[]{:S(2)}, u32[]{:S(2)}) collective-permute-start(f32[96,256]{1,0:T(8,128)S(1)} %get-tuple-element.54.refs_14_), channel_id=1, source_target_pairs={{0,1},{1,0},{2,3},{3,2},{4,5},{5,4},{6,7},{7,6},{8,9},{9,8},{10,11... | collective-permute-start | bytes 294920 | tf_op jit(solution)/shard_map/ppermute | solution.py:411
  20.3 22.2 %collective-permute-start.9 = (f32[96,256]{1,0:T(8,128)S(1)}, f32[96,256]{1,0:T(8,128)S(1)}, u32[]{:S(2)}, u32[]{:S(2)}) collective-permute-start(f32[96,256]{1,0:T(8,128)S(1)} %get-tuple-element.55.refs_15_), channel_id=1, source_target_pairs={{0,4},{4,0},{8,12},{12,8},{16,20},{20,16},{24,28},{28,24},{1,5},{5... | collective-permute-start | bytes 294920 | tf_op jit(solution)/shard_map/ppermute | solution.py:413
  20.3 22.2 %collective-permute-start.6 = (f32[96,256]{1,0:T(8,128)S(1)}, f32[96,256]{1,0:T(8,128)S(1)}, u32[]{:S(2)}, u32[]{:S(2)}) collective-permute-start(f32[96,256]{1,0:T(8,128)S(1)} %collective-permute-done.5), channel_id=1, source_target_pairs={{0,8},{8,16},{16,24},{24,28},{4,0},{12,4},{20,12},{28,20},{1,9},{9... | collective-permute-start | bytes 294920 | tf_op jit(solution)/shard_map/ppermute | solution.py:412
  21.8 1.2 %collective-permute-start.10 = (f32[8,128]{1,0:T(8,128)S(1)}, f32[8,128]{1,0:T(8,128)S(1)}, u32[]{:S(2)}, u32[]{:S(2)}) collective-permute-start(f32[8,128]{1,0:T(8,128)S(1)} %get-tuple-element.51.refs_6_.refs_7_.own.peak), channel_id=1, source_target_pairs={{0,4},{4,0},{8,12},{12,8},{16,20},{20,16},{24,28},{28,24},{1,5},{5... | collective-permute-start | bytes 12296 | tf_op jit(solution)/shard_map/ppermute | solution.py:388
  23.0 3.6 %collective-permute-start.11 = (f32[8,128]{1,0:T(8,128)S(1)}, f32[8,128]{1,0:T(8,128)S(1)}, u32[]{:S(2)}, u32[]{:S(2)}) collective-permute-start(f32[8,128]{1,0:T(8,128)S(1)} %max.15), channel_id=1, source_target_pairs={{0,8},{4,12},{8,0},{12,4},{16,24},{20,28},{24,16},{28,20},{1,9},{5... | collective-permute-start | bytes 12296 | tf_op jit(solution)/shard_map/ppermute | solution.py:388
  26.6 4.5 %collective-permute-start.12 = (f32[8,128]{1,0:T(8,128)S(1)}, f32[8,128]{1,0:T(8,128)S(1)}, u32[]{:S(2)}, u32[]{:S(2)}) collective-permute-start(f32[8,128]{1,0:T(8,128)S(1)} %max.16), channel_id=1, source_target_pairs={{0,16},{4,20},{8,24},{12,28},{16,0},{20,4},{24,8},{28,12},{1,17},{... | collective-permute-start | bytes 12296 | tf_op jit(solution)/shard_map/ppermute | solution.py:388
  31.1 3.6 %collective-permute-start.13 = (f32[8,128]{1,0:T(8,128)S(1)}, f32[8,128]{1,0:T(8,128)S(1)}, u32[]{:S(2)}, u32[]{:S(2)}) collective-permute-start(f32[8,128]{1,0:T(8,128)S(1)} %max.17), channel_id=1, source_target_pairs={{0,1},{1,0},{2,3},{3,2},{4,5},{5,4},{6,7},{7,6},{8,9},{9,8},{10,11... | collective-permute-start | bytes 12296 | tf_op jit(solution)/shard_map/ppermute | solution.py:388
  34.8 3.6 %collective-permute-start.14 = (f32[8,128]{1,0:T(8,128)S(1)}, f32[8,128]{1,0:T(8,128)S(1)}, u32[]{:S(2)}, u32[]{:S(2)}) collective-permute-start(f32[8,128]{1,0:T(8,128)S(1)} %max.18), channel_id=1, source_target_pairs={{0,2},{1,3},{2,0},{3,1},{4,6},{5,7},{6,4},{7,5},{8,10},{9,11},{10,... | collective-permute-start | bytes 12296 | tf_op jit(solution)/shard_map/ppermute | solution.py:388
  43.2 3.1 %collective-permute-start.15 = (f32[96,256]{1,0:T(8,128)S(1)}, f32[96,256]{1,0:T(8,128)S(1)}, u32[]{:S(2)}, u32[]{:S(2)}) collective-permute-start(f32[96,256]{1,0:T(8,128)S(1)} %get-tuple-element.59), channel_id=1, source_target_pairs={{0,4},{4,0},{8,12},{12,8},{16,20},{20,16},{24,28},{28,24},{1,5},{5... | collective-permute-start | bytes 294920 | tf_op jit(solution)/shard_map/ppermute | solution.py:409
  43.3 9.3 %collective-permute-start.17 = (f32[96,256]{1,0:T(8,128)S(1)}, f32[96,256]{1,0:T(8,128)S(1)}, u32[]{:S(2)}, u32[]{:S(2)}) collective-permute-start(f32[96,256]{1,0:T(8,128)S(1)} %get-tuple-element.60), channel_id=1, source_target_pairs={{0,3},{1,2},{2,1},{3,0},{4,7},{5,6},{6,5},{7,4},{8,11},{9,10},{10,... | collective-permute-start | bytes 294920 | tf_op jit(solution)/shard_map/ppermute | solution.py:410
  45.8 6.8 %collective-permute-start.18 = (f32[96,256]{1,0:T(8,128)S(1)}, f32[96,256]{1,0:T(8,128)S(1)}, u32[]{:S(2)}, u32[]{:S(2)}) collective-permute-start(f32[96,256]{1,0:T(8,128)S(1)} %get-tuple-element.61), channel_id=1, source_target_pairs={{0,1},{1,0},{2,3},{3,2},{4,5},{5,4},{6,7},{7,6},{8,9},{9,8},{10,11... | collective-permute-start | bytes 294920 | tf_op jit(solution)/shard_map/ppermute | solution.py:411
  46.4 6.3 %collective-permute-start.19 = (f32[96,256]{1,0:T(8,128)S(1)}, f32[96,256]{1,0:T(8,128)S(1)}, u32[]{:S(2)}, u32[]{:S(2)}) collective-permute-start(f32[96,256]{1,0:T(8,128)S(1)} %get-tuple-element.62), channel_id=1, source_target_pairs={{0,4},{4,0},{8,12},{12,8},{16,20},{20,16},{24,28},{28,24},{1,5},{5... | collective-permute-start | bytes 294920 | tf_op jit(solution)/shard_map/ppermute | solution.py:413
  46.4 6.3 %collective-permute-start.16 = (f32[96,256]{1,0:T(8,128)S(1)}, f32[96,256]{1,0:T(8,128)S(1)}, u32[]{:S(2)}, u32[]{:S(2)}) collective-permute-start(f32[96,256]{1,0:T(8,128)S(1)} %collective-permute-done.15), channel_id=1, source_target_pairs={{0,8},{8,16},{16,24},{24,28},{4,0},{12,4},{20,12},{28,20},{1,9},{9... | collective-permute-start | bytes 294920 | tf_op jit(solution)/shard_map/ppermute | solution.py:412
  53.3 2.1 %collective-permute-start.20 = (f32[96,256]{1,0:T(8,128)S(1)}, f32[96,256]{1,0:T(8,128)S(1)}, u32[]{:S(2)}, u32[]{:S(2)}) collective-permute-start(f32[96,256]{1,0:T(8,128)S(1)} %get-tuple-element.66), channel_id=1, source_target_pairs={{0,4},{4,0},{8,12},{12,8},{16,20},{20,16},{24,28},{28,24},{1,5},{5... | collective-permute-start | bytes 294920 | tf_op jit(solution)/shard_map/ppermute | solution.py:409
  53.4 7.9 %collective-permute-start.22 = (f32[96,256]{1,0:T(8,128)S(1)}, f32[96,256]{1,0:T(8,128)S(1)}, u32[]{:S(2)}, u32[]{:S(2)}) collective-permute-start(f32[96,256]{1,0:T(8,128)S(1)} %get-tuple-element.67), channel_id=1, source_target_pairs={{0,3},{1,2},{2,1},{3,0},{4,7},{5,6},{6,5},{7,4},{8,11},{9,10},{10,... | collective-permute-start | bytes 294920 | tf_op jit(solution)/shard_map/ppermute | solution.py:410
  54.9 6.4 %collective-permute-start.23 = (f32[96,256]{1,0:T(8,128)S(1)}, f32[96,256]{1,0:T(8,128)S(1)}, u32[]{:S(2)}, u32[]{:S(2)}) collective-permute-start(f32[96,256]{1,0:T(8,128)S(1)} %get-tuple-element.68), channel_id=1, source_target_pairs={{0,1},{1,0},{2,3},{3,2},{4,5},{5,4},{6,7},{7,6},{8,9},{9,8},{10,11... | collective-permute-start | bytes 294920 | tf_op jit(solution)/shard_map/ppermute | solution.py:411
  55.4 5.9 %collective-permute-start.24 = (f32[96,256]{1,0:T(8,128)S(1)}, f32[96,256]{1,0:T(8,128)S(1)}, u32[]{:S(2)}, u32[]{:S(2)}) collective-permute-start(f32[96,256]{1,0:T(8,128)S(1)} %get-tuple-element.69), channel_id=1, source_target_pairs={{0,4},{4,0},{8,12},{12,8},{16,20},{20,16},{24,28},{28,24},{1,5},{5... | collective-permute-start | bytes 294920 | tf_op jit(solution)/shard_map/ppermute | solution.py:413
  55.4 5.9 %collective-permute-start.21 = (f32[96,256]{1,0:T(8,128)S(1)}, f32[96,256]{1,0:T(8,128)S(1)}, u32[]{:S(2)}, u32[]{:S(2)}) collective-permute-start(f32[96,256]{1,0:T(8,128)S(1)} %collective-permute-done.20), channel_id=1, source_target_pairs={{0,8},{8,16},{16,24},{24,28},{4,0},{12,4},{20,12},{28,20},{1,9},{9... | collective-permute-start | bytes 294920 | tf_op jit(solution)/shard_map/ppermute | solution.py:412
  62.5 1.3 %collective-permute-start.25 = (f32[48,128]{1,0:T(8,128)S(1)}, f32[48,128]{1,0:T(8,128)S(1)}, u32[]{:S(2)}, u32[]{:S(2)}) collective-permute-start(f32[48,128]{1,0:T(8,128)S(1)} %shard_map.63), channel_id=1, source_target_pairs={{0,4},{4,0},{8,12},{12,8},{16,20},{20,16},{24,28},{28,24},{1,5},{5... | collective-permute-start | bytes 73736 | tf_op jit(solution)/shard_map/ppermute | solution.py:388
  63.7 5.6 %collective-permute-start.27 = (f32[48,128]{1,0:T(8,128)S(1)}, f32[48,128]{1,0:T(8,128)S(1)}, u32[]{:S(2)}, u32[]{:S(2)}) collective-permute-start(f32[48,128]{1,0:T(8,128)S(1)} %add.12), channel_id=1, source_target_pairs={{0,24},{4,28},{8,16},{12,20},{16,8},{20,12},{24,0},{28,4},{1,25},{... | collective-permute-start | bytes 73736 | tf_op jit(solution)/shard_map/ppermute | solution.py:394
  65.8 4.1 %collective-permute-start.28 = (f32[48,128]{1,0:T(8,128)S(1)}, f32[48,128]{1,0:T(8,128)S(1)}, u32[]{:S(2)}, u32[]{:S(2)}) collective-permute-start(f32[48,128]{1,0:T(8,128)S(1)} %add.12), channel_id=1, source_target_pairs={{0,8},{4,12},{8,0},{12,4},{16,24},{20,28},{24,16},{28,20},{1,9},{5... | collective-permute-start | bytes 73736 | tf_op jit(solution)/shard_map/ppermute | solution.py:394
  65.9 4.7 %collective-permute-start.26 = (f32[48,128]{1,0:T(8,128)S(1)}, f32[48,128]{1,0:T(8,128)S(1)}, u32[]{:S(2)}, u32[]{:S(2)}) collective-permute-start(f32[48,128]{1,0:T(8,128)S(1)} %add.12), channel_id=1, source_target_pairs={{0,16},{4,20},{8,24},{12,28},{16,0},{20,4},{24,8},{28,12},{1,17},{... | collective-permute-start | bytes 73736 | tf_op jit(solution)/shard_map/ppermute | solution.py:394
  70.6 4.8 %collective-permute-start.29 = (f32[48,128]{1,0:T(8,128)S(1)}, f32[48,128]{1,0:T(8,128)S(1)}, u32[]{:S(2)}, u32[]{:S(2)}) collective-permute-start(f32[48,128]{1,0:T(8,128)S(1)} %add_add_fusion.refs_0_), channel_id=1, source_target_pairs={{0,3},{1,2},{2,1},{3,0},{4,7},{5,6},{6,5},{7,4},{8,11},{9,10},{10,... | collective-permute-start | bytes 73736 | tf_op jit(solution)/shard_map/ppermute | solution.py:394
  73.1 3.8 %collective-permute-start.30 = (f32[48,128]{1,0:T(8,128)S(1)}, f32[48,128]{1,0:T(8,128)S(1)}, u32[]{:S(2)}, u32[]{:S(2)}) collective-permute-start(f32[48,128]{1,0:T(8,128)S(1)} %add_add_fusion.refs_0_), channel_id=1, source_target_pairs={{0,2},{1,3},{2,0},{3,1},{4,6},{5,7},{6,4},{7,5},{8,10},{9,11},{10,... | collective-permute-start | bytes 73736 | tf_op jit(solution)/shard_map/ppermute | solution.py:394
  73.7 3.8 %collective-permute-start.31 = (f32[48,128]{1,0:T(8,128)S(1)}, f32[48,128]{1,0:T(8,128)S(1)}, u32[]{:S(2)}, u32[]{:S(2)}) collective-permute-start(f32[48,128]{1,0:T(8,128)S(1)} %add_add_fusion.refs_0_), channel_id=1, source_target_pairs={{0,1},{1,0},{2,3},{3,2},{4,5},{5,4},{6,7},{7,6},{8,9},{9,8},{10,11... | collective-permute-start | bytes 73736 | tf_op jit(solution)/shard_map/ppermute | solution.py:394

commit v4 on v3

--- a/solution.py
+++ b/solution.py
@@ -98,16 +98,17 @@
     return (upper + lower) / 2.0, (upper - lower) / 2.0
 
 
-def first_kernel(sizes, cols, counts, lists_any, basis_any, weights_any, *refs):
+def first_kernel(sizes, counts, cols_any, lists_any, basis_any, weights_any, *refs):
     place, stored, begin, degree, peak, marks = refs[:6]
     outs = refs[6:10]
-    lists, basis, weights, hits, sems = refs[10:]
+    lists, basis, weights, hits, cols, sems = refs[10:]
     blocks, slots = weights.shape[:2]
     cells, edges = place.shape
     width = edges // len(outs)
     loads = [
         pltpu.make_async_copy(lists_any.at[0, 0], lists, sems.at[blocks]),
         pltpu.make_async_copy(basis_any.at[0, 0], basis, sems.at[blocks + 1]),
+        pltpu.make_async_copy(cols_any, cols, sems.at[blocks + 2]),
     ]
     blocks_in = [
         pltpu.make_async_copy(weights_any.at[0, 0, m], weights.at[m], sems.at[m]) for m in range(blocks)
@@ -116,10 +117,10 @@
         load.start()
     count = counts[...]
     degree[...] = jnp.zeros_like(degree)
-    for load in loads:
-        load.wait()
+    loads[0].wait()
     for load in blocks_in:
         load.start()
+    loads[1].wait()
     order = []
     for axis, shift in SIDES:
         dim = ("gx", "gy").index(axis)
@@ -145,6 +146,7 @@
         out[...] = picked[:, i * width : (i + 1) * width]
     joined = dot_nt(jnp.ones((16, LANES), BF16), hits[...])[:8]
     rows = lax.broadcasted_iota(jnp.int32, (LANES, LANES), 0)
+    loads[2].wait()
     for m in range(blocks):
         blocks_in[m].wait()
         live = rows + m * LANES < count
@@ -176,8 +178,8 @@
     return folded(dot(stacked(values), place[...]))
 
 
-def joined_up(parts):
-    return jnp.concatenate([part[...] for part in parts], axis=1)
+def joined_up(parts, vecs):
+    return jnp.concatenate([part[:vecs] for part in parts], axis=1)
 
 
 def chunks(cells):
@@ -208,20 +210,23 @@
 
 
 def edges_kernel(number, r0, r1, r2, r3, edge_local, same, own, peak, before, *outs):
-    crossed = folded(dot(stacked(joined_up((r0, r1, r2, r3))), same[...]))
+    vecs = edge_local.shape[0]
+    crossed = folded(dot(stacked(joined_up((r0, r1, r2, r3), vecs)), same[...]))
     if number == 0:
         value = edge_local[...] - crossed
     elif number == 1:
         centre, half = scalars(peak)
         top = own[0:1, 0:1]
-        first, second = joined_up(before[:4]), joined_up(before[4:])
+        first, second = joined_up(before[:4], vecs), joined_up(before[4:], vecs)
         value = second_field(centre, half, top, edge_local[...] - crossed / top, second, first)[1]
     else:
         _, half = scalars(peak)
         value = edge_local[...] - (2.0 / half) * crossed
     width = value.shape[1] // len(outs)
     for i, out in enumerate(outs):
-        out[...] = value[:, i * width : (i + 1) * width]
+        out[:vecs] = value[:, i * width : (i + 1) * width]
+        if out.shape[0] > vecs:
+            out[vecs:] = jnp.broadcast_to(peak[0:1, 0:1], (out.shape[0] - vecs, width))
 
 
 def second_field(centre, half, top, twice, once, begin):
@@ -240,7 +245,7 @@
     cells = place.shape[0]
     top = own[0:1, 0:1]
     centre, half = scalars(peak)
-    arrived = stacked(joined_up((r0, r1, r2, r3)))
+    arrived = stacked(joined_up((r0, r1, r2, r3), local.shape[0]))
     for part in chunks(cells):
         crossed = folded(dot(arrived, back[:, part]))
         if number == 0:
@@ -301,7 +306,7 @@
 def gram_kernel(r0, r1, r2, r3, edge_local, same, peak, base, gram):
     _, half = scalars(peak)
     scale = 2.0 / half
-    arrived = joined_up((r0, r1, r2, r3))
+    arrived = joined_up((r0, r1, r2, r3), edge_local.shape[0])
     crossed = folded(dot(stacked(arrived), same[...]))
     mixed = product_nt(scale * (edge_local[...] - (0.5 * scale) * crossed), arrived)
     gram[...] = packed(base[...] - mixed - mixed.T)
@@ -309,7 +314,7 @@
 
 def last_kernel(r0, r1, r2, r3, local, back, peak, terms):
     _, half = scalars(peak)
-    arrived = stacked(joined_up((r0, r1, r2, r3)))
+    arrived = stacked(joined_up((r0, r1, r2, r3), local.shape[0]))
     for part in chunks(back.shape[1]):
         hi, lo = split(local[:, part] - (2.0 / half) * folded(dot(arrived, back[:, part])))
         terms[:, part] = jnp.concatenate([hi, lo, hi], axis=0)
@@ -425,24 +430,28 @@
             shape(8, 4 * edges, dtype=jnp.int32),
         ]
         + sends,
-        [SM, VM] + [HBM] * 3,
+        [VM] + [HBM] * 4,
         scratch_shapes=[
             pltpu.VMEM((4, edges), jnp.int32),
             pltpu.VMEM((vecs, cells), F32),
             pltpu.VMEM((blocks, slots, block, block), F32),
             pltpu.VMEM((cells, LANES), BF16),
-            pltpu.SemaphoreType.DMA((blocks + 2,)),
+            pltpu.SMEM(cols.shape, jnp.int32),
+            pltpu.SemaphoreType.DMA((blocks + 3,)),
         ],
     )(
-        cols,
         live_counts,
-        *(pltpu.with_memory_space_constraint(x, pltpu.HBM) for x in (edge_rows, basis, block_vals)),
+        *(pltpu.with_memory_space_constraint(x, pltpu.HBM) for x in (cols, edge_rows, basis, block_vals)),
     )
     stages = [
         (axis, 1 << b) for axis, size in zip(("gx", "gy"), sizes) for b in range(size.bit_length() - 1)
     ]
     arrived = exchange(outgoing)
-    peak = spread(own, jnp.maximum, stages)
+    riding = sizes[1] == 4
+    across = [stage for stage in stages if not (riding and stage[0] == "gy")]
+    peak = spread(own, jnp.maximum, across)
+    if riding:
+        opposite = lax.ppermute(peak, "gy", xor_pairs(4, 2))
     local, edge_local, same, back = call(
         open_kernel,
         [
@@ -457,13 +466,17 @@
 
     history, earlier = [outgoing], [begin, begin]
     for number in range(3):
-        bound = peak if number else own
+        wide = riding and number == 0
+        if riding and number == 1:
+            ridden = [part[vecs:, :LANES] for part, (axis, _) in zip(arrived, SIDES) if axis == "gy"]
+            peak = jnp.maximum(jnp.maximum(peak, opposite), jnp.maximum(*ridden))
+        bound = peak if number or riding else own
         before = [x for parts in history for x in parts] if number == 1 else []
         outgoing = call(
             lambda *refs, number=number, count=len(before): edges_kernel(
                 number, *refs[:8], refs[8 : 8 + count], *refs[8 + count :]
             ),
-            sends,
+            [shape(vecs + 8 * (wide and axis == "gy"), edges) for axis, _ in SIDES],
             [VM] * (8 + len(before)),
         )(*arrived, edge_local, same, own, bound, *before)
         history.append(outgoing)
@@ -473,7 +486,7 @@
             [field, field, edge_field] + [shape(vecs, vecs)] * (number == 2),
             [SM] + [VM] * 14,
             scratch_shapes=scratch,
-        )(cols, live_counts, *arrived, local, stored, degree, place, back, own, bound, *earlier)
+        )(cols, live_counts, *arrived, local, stored, degree, place, back, own, bound if number else own, *earlier)
         earlier = [begin, now] if number == 0 else [now, now]
         arrived = coming
 

time: 82.8 us -> 75.8 us (0.915)
  waiting for transfers between devices: 16 us -> 13.1 us
  starting transfers between devices: 32.1 us -> 30.1 us
  Pallas kernels: 32.9 us -> 31.5 us
    ppermute x6 -> x4, waiting for transfers between devices: 11.2 us -> 4.39 us  [spread(): value = combine(value, lax.ppermute(value, axis, pairs))]
    ppermute x6 -> x4, starting transfers between devices: 6.52 us -> 4.22 us  [spread(): value = combine(value, lax.ppermute(value, axis, pairs))]
    ppermute x4, waiting for transfers between devices: 0.01 us -> 2.18 us  [exchange(): x_far = lax.ppermute(x_far, 'gx', turn_pairs(sizes[0]))]
    ppermute x6, waiting for transfers between devices: 4.7 us -> 6.44 us  [all_of(): lax.ppermute(value, axis, xor_pairs(size, bit))]
    pallas_call x1, Pallas kernels: 5.67 us -> 4.17 us  [per_device(): call(functools.partial(first_kernel, sizes), [shape(cells, 4 * edges, dty...]
    ppermute x0 -> x1, starting transfers between devices: none -> 1.48 us  [per_device(): opposite = lax.ppermute(peak, 'gy', xor_pairs(4, 2))]
    ppermute x4, starting transfers between devices: 5.65 us -> 4.27 us  [exchange(): x_far = lax.ppermute(x_far, 'gx', turn_pairs(sizes[0]))]
    ppermute x4, starting transfers between devices: 0.77 us -> 1.76 us  [exchange(): x_far = lax.ppermute(x_far, 'gx', near_pairs(sizes[0]))]
  transfers between devices with their start and end apart: 32 -> 31, of which waited for: 12 -> 9; matrix products, arithmetic and copies ran while one was open for 0% -> 0% of each run, Pallas kernels for 23% -> 25%
where the time goes in v4:
time: 75.8 us; the launch traced here: 75.6 us
  Pallas kernels  31.5 us (42%)
  starting transfers between devices  30.1 us (40%)
  waiting for transfers between devices  13.1 us (17%)
  between operations  0.93 us (1%)
    pallas_call x3, Pallas kernels, per_device(): call(functools.partial(field_kernel, number), [field, field, edge_field]...  13.8 us
    ppermute x4, starting transfers between devices, exchange(): y_far = lax.ppermute(y_far, 'gy', far_pairs(sizes[1]))  8.94 us
    ppermute x6, starting transfers between devices, all_of(): lax.ppermute(value, axis, xor_pairs(size, bit))  7.04 us
    ppermute x6, waiting for transfers between devices, all_of(): lax.ppermute(value, axis, xor_pairs(size, bit))  6.44 us
    pallas_call x1, Pallas kernels, per_device(): call(functools.partial(encode_kernel, root), shape(1, 1, vecs, cells), [V...  5.09 us
    ppermute x4, waiting for transfers between devices, spread(): value = combine(value, lax.ppermute(value, axis, pairs))  4.39 us
    pallas_call x1, Pallas kernels, per_device(): call(open_kernel, [field, edge_field, shape(4 * edges, 4 * edges, dtype=B...  4.27 us
    ppermute x4, starting transfers between devices, exchange(): x_far = lax.ppermute(x_far, 'gx', turn_pairs(sizes[0]))  4.27 us
  transfers between devices with their start and end apart: 31, of which 9 were waited for; matrix products, arithmetic and copies ran while one was open for 0% of the time, Pallas kernels for 25%

profile of v4, /device:TPU:0, one launch (start us, length us, event | category | flops | bytes accessed | tf_op | source)
XLA Modules:
  0.0 75.6 jit_solution(6233432050691576955)
XLA Ops:
  0.7 4.2 %shard_map.55 = (bf16[2048,1024]{1,0:T(8,128)(2,1)S(1)}, bf16[16,256,640]{2,1,0:T(8,128)(2,1)S(1)}, f32[96,2048]{1,0:T(8,128)S(1)}, f32[8,2048]{1,0:T(8,128)S(1)...) custom-call(s32[1,1]{1,0:T(1,128)S(6)} %copy.6.counts, ...), custom_call_target="tpu_custom_call" | custom-call | tf_op jit(solution)/shard_map/pallas_call | solution.py:422
  4.8 0.6 collective-permute-start
  5.4 3.5 %collective-permute-start.2 = (f32[96,256]{1,0:T(8,128)S(1)}, f32[96,256]{1,0:T(8,128)S(1)}, u32[]{:S(2)}, u32[]{:S(2)}) collective-permute-start(f32[96,256]{1,0:T(8,128)S(1)} %get-tuple-element.41.refs_9_), channel_id=1, source_target_pairs={{0,3},{1,2},{2,1},{3,0},{4,7},{5,6},{6,5},{7,4},{8,11},{9,10},{10,... | collective-permute-start | bytes 294920 | tf_op jit(solution)/shard_map/ppermute | solution.py:415
  8.9 0.5 collective-permute-start.3
  9.5 0.0 collective-permute-start.4
  9.5 1.6 %collective-permute-start.1 = (f32[96,256]{1,0:T(8,128)S(1)}, f32[96,256]{1,0:T(8,128)S(1)}, u32[]{:S(2)}, u32[]{:S(2)}) collective-permute-start(f32[96,256]{1,0:T(8,128)S(1)} %collective-permute-done), channel_id=1, source_target_pairs={{0,8},{8,16},{16,24},{24,28},{4,0},{12,4},{20,12},{28,20},{1,9},{9... | collective-permute-start | bytes 294920 | tf_op jit(solution)/shard_map/ppermute | solution.py:417
  11.0 0.0 collective-permute-start.5
  11.0 1.2 %collective-permute-done.5 = f32[8,128]{1,0:T(8,128)S(1)} collective-permute-done((f32[8,128]{1,0:T(8,128)S(1)}, f32[8,128]{1,0:T(8,128)S(1)}, u32[]{:S(2)}, u32[]{:S(2)}) %collective-permute-start.5) | collective-permute-done | bytes 4128 | tf_op jit(solution)/shard_map/ppermute | solution.py:393
  12.2 1.6 %collective-permute-start.6 = (f32[8,128]{1,0:T(8,128)S(1)}, f32[8,128]{1,0:T(8,128)S(1)}, u32[]{:S(2)}, u32[]{:S(2)}) collective-permute-start(f32[8,128]{1,0:T(8,128)S(1)} %max.18), channel_id=1, source_target_pairs={{0,8},{4,12},{8,0},{12,4},{16,24},{20,28},{24,16},{28,20},{1,9},{5... | collective-permute-start | bytes 12296 | tf_op jit(solution)/shard_map/ppermute | solution.py:393
  13.8 2.0 %collective-permute-done.6 = f32[8,128]{1,0:T(8,128)S(1)} collective-permute-done((f32[8,128]{1,0:T(8,128)S(1)}, f32[8,128]{1,0:T(8,128)S(1)}, u32[]{:S(2)}, u32[]{:S(2)}) %collective-permute-start.6) | collective-permute-done | bytes 4128 | tf_op jit(solution)/shard_map/ppermute | solution.py:393
  15.8 2.6 %collective-permute-start.7 = (f32[8,128]{1,0:T(8,128)S(1)}, f32[8,128]{1,0:T(8,128)S(1)}, u32[]{:S(2)}, u32[]{:S(2)}) collective-permute-start(f32[8,128]{1,0:T(8,128)S(1)} %max.19), channel_id=1, source_target_pairs={{0,16},{4,20},{8,24},{12,28},{16,0},{20,4},{24,8},{28,12},{1,17},{... | collective-permute-start | bytes 12296 | tf_op jit(solution)/shard_map/ppermute | solution.py:393
  18.4 4.3 %shard_map.56 = (f32[96,2048]{1,0:T(8,128)S(1)}, f32[96,1024]{1,0:T(8,128)S(1)}, bf16[1024,1024]{1,0:T(8,128)(2,1)S(1)}, bf16[1024,2048]{1,0:T(8,128)(2,1)S(1)}) custom-call(s32[1,5,1,16]{3,2,1,0:T(1,128)S(1)} %bitcast.2, s32[1,1]{1,0:T(1,128)S(6)} %copy.6.counts, f32[96,2048]{1,0:T(8,128)S(1)} %get-tuple-element.44.begin.once, ...), custom_call_target="tpu_custom_call" | custom-call | tf_op jit(solution)/shard_map/pallas_call | solution.py:455
  22.8 0.6 shard_map.57
  23.4 1.5 %collective-permute-start.10 = (f32[104,256]{1,0:T(8,128)S(1)}, f32[104,256]{1,0:T(8,128)S(1)}, u32[]{:S(2)}, u32[]{:S(2)}) collective-permute-start(f32[104,256]{1,0:T(8,128)S(1)} %get-tuple-element.53.refs_13_), channel_id=1, source_target_pairs={{0,3},{1,2},{2,1},{3,0},{4,7},{5,6},{6,5},{7,4},{8,11},{9,10},{10,... | collective-permute-start | bytes 319496 | tf_op jit(solution)/shard_map/ppermute | solution.py:415
  24.9 0.6 collective-permute-start.11
  25.4 1.5 %collective-permute-start.13 = (f32[8,128]{1,0:T(8,128)S(1)}, f32[8,128]{1,0:T(8,128)S(1)}, u32[]{:S(2)}, u32[]{:S(2)}) collective-permute-start(f32[8,128]{1,0:T(8,128)S(1)} %max.20.refs_7_), channel_id=1, source_target_pairs={{0,2},{1,3},{2,0},{3,1},{4,6},{5,7},{6,4},{7,5},{8,10},{9,11},{10,... | collective-permute-start | bytes 12296 | tf_op jit(solution)/shard_map/ppermute | solution.py:454
  26.9 0.2 collective-permute-start.12
  27.2 4.1 %shard_map.58 = (f32[96,2048]{1,0:T(8,128)S(1)}, f32[96,2048]{1,0:T(8,128)S(1)}, f32[96,1024]{1,0:T(8,128)S(1)}) custom-call(s32[1,5,1,16]{3,2,1,0:T(1,128)S(1)} %bitcast.3, s32[1,1]{1,0:T(1,128)S(6)} %copy.6.counts, f32[96,256]{1,0:T(8,128)S(1)} %collective-permute-done.1.refs_0_.r0, f32[96,256]{1,0:T(8,128)S(1)} %collective-permute-done.2.refs_1_.r1, ...), custom_call_target="tpu_custom_call" | custom-call | tf_op jit(solution)/shard_map/pallas_call | solution.py:484
  31.3 0.5 collective-permute-start.9
  31.9 2.2 %collective-permute-done.9.refs_0_.r0 = f32[96,256]{1,0:T(8,128)S(1)} collective-permute-done((f32[96,256]{1,0:T(8,128)S(1)}, f32[96,256]{1,0:T(8,128)S(1)}, u32[]{:S(2)}, u32[]{:S(2)}) %collective-permute-start.9) | collective-permute-done | bytes 98336 | tf_op jit(solution)/shard_map/ppermute | solution.py:417
  34.0 0.7 shard_map.59
  34.7 1.1 %collective-permute-start.14 = (f32[96,256]{1,0:T(8,128)S(1)}, f32[96,256]{1,0:T(8,128)S(1)}, u32[]{:S(2)}, u32[]{:S(2)}) collective-permute-start(f32[96,256]{1,0:T(8,128)S(1)} %get-tuple-element.59), channel_id=1, source_target_pairs={{0,4},{4,0},{8,12},{12,8},{16,20},{20,16},{24,28},{28,24},{1,5},{5... | collective-permute-start | bytes 294920 | tf_op jit(solution)/shard_map/ppermute | solution.py:414
  35.8 1.4 %collective-permute-start.16 = (f32[96,256]{1,0:T(8,128)S(1)}, f32[96,256]{1,0:T(8,128)S(1)}, u32[]{:S(2)}, u32[]{:S(2)}) collective-permute-start(f32[96,256]{1,0:T(8,128)S(1)} %get-tuple-element.60), channel_id=1, source_target_pairs={{0,3},{1,2},{2,1},{3,0},{4,7},{5,6},{6,5},{7,4},{8,11},{9,10},{10,... | collective-permute-start | bytes 294920 | tf_op jit(solution)/shard_map/ppermute | solution.py:415
  37.3 0.6 collective-permute-start.17
  37.8 1.5 %collective-permute-start.15 = (f32[96,256]{1,0:T(8,128)S(1)}, f32[96,256]{1,0:T(8,128)S(1)}, u32[]{:S(2)}, u32[]{:S(2)}) collective-permute-start(f32[96,256]{1,0:T(8,128)S(1)} %collective-permute-done.14), channel_id=1, source_target_pairs={{0,8},{8,16},{16,24},{24,28},{4,0},{12,4},{20,12},{28,20},{1,9},{9... | collective-permute-start | bytes 294920 | tf_op jit(solution)/shard_map/ppermute | solution.py:417
  39.3 4.7 %shard_map.60 = (f32[96,2048]{1,0:T(8,128)S(1)}, f32[96,2048]{1,0:T(8,128)S(1)}, f32[96,1024]{1,0:T(8,128)S(1)}) custom-call(s32[1,5,1,16]{3,2,1,0:T(1,128)S(1)} %bitcast.4, s32[1,1]{1,0:T(1,128)S(6)} %copy.6.counts, f32[96,256]{1,0:T(8,128)S(1)} %collective-permute-done.9.refs_0_.r0, f32[104,256]{1,0:T(8,128)S(1)} %collective-permute-done.10.refs_1_.r1, ...), custom_call_target="tpu_custom_call" | custom-call | tf_op jit(solution)/shard_map/pallas_call | solution.py:484
  44.0 0.6 shard_map.61
  44.7 0.1 collective-permute-start.19
  44.7 2.5 %collective-permute-start.21 = (f32[96,256]{1,0:T(8,128)S(1)}, f32[96,256]{1,0:T(8,128)S(1)}, u32[]{:S(2)}, u32[]{:S(2)}) collective-permute-start(f32[96,256]{1,0:T(8,128)S(1)} %get-tuple-element.67), channel_id=1, source_target_pairs={{0,3},{1,2},{2,1},{3,0},{4,7},{5,6},{6,5},{7,4},{8,11},{9,10},{10,... | collective-permute-start | bytes 294920 | tf_op jit(solution)/shard_map/ppermute | solution.py:415
  47.2 0.5 collective-permute-start.22
  47.8 0.7 collective-permute-start.20
  48.5 5.0 %shard_map.62 = (f32[96,2048]{1,0:T(8,128)}, f32[96,2048]{1,0:T(8,128)S(1)}, f32[96,1024]{1,0:T(8,128)S(1)}, f32[96,96]{1,0:T(8,128)S(1)}) custom-call(s32[1,5,1,16]{3,2,1,0:T(1,128)S(1)} %bitcast.5, s32[1,1]{1,0:T(1,128)S(6)} %copy.6.counts, f32[96,256]{1,0:T(8,128)S(1)} %collective-permute-done.15.refs_0_.r0, ...), custom_call_target="tpu_custom_call" | custom-call | tf_op jit(solution)/shard_map/pallas_call | solution.py:484
  53.5 1.1 %shard_map.63 = f32[48,128]{1,0:T(8,128)S(1)} custom-call(f32[96,256]{1,0:T(8,128)S(1)} %collective-permute-done.20.r0, f32[96,256]{1,0:T(8,128)S(1)} %collective-permute-done.21.r1, f32[96,256]{1,0:T(8,128)S(1)} %collective-permute-done.22.r2, f32[96,256]{1,0:T(8,128)S(1)} %collective-permute-done.23.r3, f32[96,1024]{1,0:T(8,128)S(1)} %get-tuple-element.72.edge_local, ...), custom_call_target="tpu_custom_call" | custom-call | tf_op jit(solution)/shard_map/pallas_call | solution.py:493
  54.6 0.1 collective-permute-start.24
  54.7 1.2 %collective-permute-done.24 = f32[48,128]{1,0:T(8,128)S(1)} collective-permute-done((f32[48,128]{1,0:T(8,128)S(1)}, f32[48,128]{1,0:T(8,128)S(1)}, u32[]{:S(2)}, u32[]{:S(2)}) %collective-permute-start.24) | collective-permute-done | bytes 24608 | tf_op jit(solution)/shard_map/ppermute | solution.py:393
  55.9 1.5 %collective-permute-start.27 = (f32[48,128]{1,0:T(8,128)S(1)}, f32[48,128]{1,0:T(8,128)S(1)}, u32[]{:S(2)}, u32[]{:S(2)}) collective-permute-start(f32[48,128]{1,0:T(8,128)S(1)} %add.12), channel_id=1, source_target_pairs={{0,8},{4,12},{8,0},{12,4},{16,24},{20,28},{24,16},{28,20},{1,9},{5... | collective-permute-start | bytes 73736 | tf_op jit(solution)/shard_map/ppermute | solution.py:399
  57.4 1.4 %collective-permute-start.26 = (f32[48,128]{1,0:T(8,128)S(1)}, f32[48,128]{1,0:T(8,128)S(1)}, u32[]{:S(2)}, u32[]{:S(2)}) collective-permute-start(f32[48,128]{1,0:T(8,128)S(1)} %add.12), channel_id=1, source_target_pairs={{0,24},{4,28},{8,16},{12,20},{16,8},{20,12},{24,0},{28,4},{1,25},{... | collective-permute-start | bytes 73736 | tf_op jit(solution)/shard_map/ppermute | solution.py:399
  58.7 0.7 collective-permute-start.25
  59.4 0.3 collective-permute-done.27
  59.7 3.3 %collective-permute-done.26 = f32[48,128]{1,0:T(8,128)S(1)} collective-permute-done((f32[48,128]{1,0:T(8,128)S(1)}, f32[48,128]{1,0:T(8,128)S(1)}, u32[]{:S(2)}, u32[]{:S(2)}) %collective-permute-start.26) | collective-permute-done | bytes 24608 | tf_op jit(solution)/shard_map/ppermute | solution.py:399
  63.0 0.7 collective-permute-done.25
  63.7 1.5 %collective-permute-start.30 = (f32[48,128]{1,0:T(8,128)S(1)}, f32[48,128]{1,0:T(8,128)S(1)}, u32[]{:S(2)}, u32[]{:S(2)}) collective-permute-start(f32[48,128]{1,0:T(8,128)S(1)} %add_add_fusion.refs_0_), channel_id=1, source_target_pairs={{0,1},{1,0},{2,3},{3,2},{4,5},{5,4},{6,7},{7,6},{8,9},{9,8},{10,11... | collective-permute-start | bytes 73736 | tf_op jit(solution)/shard_map/ppermute | solution.py:399
  65.2 0.5 collective-permute-start.29
  65.8 1.5 %collective-permute-start.28 = (f32[48,128]{1,0:T(8,128)S(1)}, f32[48,128]{1,0:T(8,128)S(1)}, u32[]{:S(2)}, u32[]{:S(2)}) collective-permute-start(f32[48,128]{1,0:T(8,128)S(1)} %add_add_fusion.refs_0_), channel_id=1, source_target_pairs={{0,3},{1,2},{2,1},{3,0},{4,7},{5,6},{6,5},{7,4},{8,11},{9,10},{10,... | collective-permute-start | bytes 73736 | tf_op jit(solution)/shard_map/ppermute | solution.py:399
  67.3 1.1 %shard_map.64.refs_4_ = bf16[288,2048]{1,0:T(8,128)(2,1)S(1)} custom-call(f32[96,256]{1,0:T(8,128)S(1)} %collective-permute-done.20.r0, f32[96,256]{1,0:T(8,128)S(1)} %collective-permute-done.21.r1, f32[96,256]{1,0:T(8,128)S(1)} %collective-permute-done.22.r2, f32[96,256]{1,0:T(8,128)S(1)} %collective-permute-done.23.r3, ...), custom_call_target="tpu_custom_call" | custom-call | tf_op jit(solution)/shard_map/pallas_call | solution.py:499
  68.4 0.7 collective-permute-done.29.refs_2_
  69.1 1.4 %collective-permute-done.28.refs_1_ = f32[48,128]{1,0:T(8,128)S(1)} collective-permute-done((f32[48,128]{1,0:T(8,128)S(1)}, f32[48,128]{1,0:T(8,128)S(1)}, u32[]{:S(2)}, u32[]{:S(2)}) %collective-permute-start.28) | collective-permute-done | bytes 24608 | tf_op jit(solution)/shard_map/ppermute | solution.py:399
  70.5 5.1 %shard_map.65 = f32[1,1,96,2048]{3,2,1,0:T(8,128)} custom-call(f32[48,128]{1,0:T(8,128)S(1)} %add_add_fusion.refs_0_, f32[48,128]{1,0:T(8,128)S(1)} %collective-permute-done.28.refs_1_, f32[48,128]{1,0:T(8,128)S(1)} %collective-permute-done.29.refs_2_, f32[48,128]{1,0:T(8,128)S(1)} %collective-permute-done.30.refs_3_, bf16[288,2048]{1,0:T(8,128)(2,1)S(1)} %shard_map.64.refs_4_), custom_call_target="tpu_custom_call" | custom-call | tf_op jit(solution)/shard_map/pallas_call | solution.py:501
  (33 shorter events, 0.1 us)
Async XLA Ops:
  0.0 18.4 %copy-start = (s32[1,1,16,5]{2,1,3,0:T(1,128)S(1)}, s32[1,1,16,5]{2,1,3,0:T(1,128)}, u32[]{:S(2)}) copy-start(s32[1,1,16,5]{2,1,3,0:T(1,128)} %param.7) | copy-start | bytes 964
  4.8 4.6 %collective-permute-start = (f32[96,256]{1,0:T(8,128)S(1)}, f32[96,256]{1,0:T(8,128)S(1)}, u32[]{:S(2)}, u32[]{:S(2)}) collective-permute-start(f32[96,256]{1,0:T(8,128)S(1)} %get-tuple-element.40.refs_8_), channel_id=1, source_target_pairs={{0,4},{4,0},{8,12},{12,8},{16,20},{20,16},{24,28},{28,24},{1,5},{5... | collective-permute-start | bytes 294920 | tf_op jit(solution)/shard_map/ppermute | solution.py:414
  5.4 17.3 %collective-permute-start.2 = (f32[96,256]{1,0:T(8,128)S(1)}, f32[96,256]{1,0:T(8,128)S(1)}, u32[]{:S(2)}, u32[]{:S(2)}) collective-permute-start(f32[96,256]{1,0:T(8,128)S(1)} %get-tuple-element.41.refs_9_), channel_id=1, source_target_pairs={{0,3},{1,2},{2,1},{3,0},{4,7},{5,6},{6,5},{7,4},{8,11},{9,10},{10,... | collective-permute-start | bytes 294920 | tf_op jit(solution)/shard_map/ppermute | solution.py:415
  8.9 13.8 %collective-permute-start.3 = (f32[96,256]{1,0:T(8,128)S(1)}, f32[96,256]{1,0:T(8,128)S(1)}, u32[]{:S(2)}, u32[]{:S(2)}) collective-permute-start(f32[96,256]{1,0:T(8,128)S(1)} %get-tuple-element.42.refs_10_), channel_id=1, source_target_pairs={{0,1},{1,0},{2,3},{3,2},{4,5},{5,4},{6,7},{7,6},{8,9},{9,8},{10,11... | collective-permute-start | bytes 294920 | tf_op jit(solution)/shard_map/ppermute | solution.py:416
  9.5 13.3 %collective-permute-start.4 = (f32[96,256]{1,0:T(8,128)S(1)}, f32[96,256]{1,0:T(8,128)S(1)}, u32[]{:S(2)}, u32[]{:S(2)}) collective-permute-start(f32[96,256]{1,0:T(8,128)S(1)} %get-tuple-element.43.refs_11_), channel_id=1, source_target_pairs={{0,4},{4,0},{8,12},{12,8},{16,20},{20,16},{24,28},{28,24},{1,5},{5... | collective-permute-start | bytes 294920 | tf_op jit(solution)/shard_map/ppermute | solution.py:418
  9.5 13.3 %collective-permute-start.1 = (f32[96,256]{1,0:T(8,128)S(1)}, f32[96,256]{1,0:T(8,128)S(1)}, u32[]{:S(2)}, u32[]{:S(2)}) collective-permute-start(f32[96,256]{1,0:T(8,128)S(1)} %collective-permute-done), channel_id=1, source_target_pairs={{0,8},{8,16},{16,24},{24,28},{4,0},{12,4},{20,12},{28,20},{1,9},{9... | collective-permute-start | bytes 294920 | tf_op jit(solution)/shard_map/ppermute | solution.py:417
  11.0 1.2 %collective-permute-start.5 = (f32[8,128]{1,0:T(8,128)S(1)}, f32[8,128]{1,0:T(8,128)S(1)}, u32[]{:S(2)}, u32[]{:S(2)}) collective-permute-start(f32[8,128]{1,0:T(8,128)S(1)} %get-tuple-element.51.refs_6_.own.peak), channel_id=1, source_target_pairs={{0,4},{4,0},{8,12},{12,8},{16,20},{20,16},{24,28},{28,24},{1,5},{5... | collective-permute-start | bytes 12296 | tf_op jit(solution)/shard_map/ppermute | solution.py:393
  12.2 3.6 %collective-permute-start.6 = (f32[8,128]{1,0:T(8,128)S(1)}, f32[8,128]{1,0:T(8,128)S(1)}, u32[]{:S(2)}, u32[]{:S(2)}) collective-permute-start(f32[8,128]{1,0:T(8,128)S(1)} %max.18), channel_id=1, source_target_pairs={{0,8},{4,12},{8,0},{12,4},{16,24},{20,28},{24,16},{28,20},{1,9},{5... | collective-permute-start | bytes 12296 | tf_op jit(solution)/shard_map/ppermute | solution.py:393
  15.8 6.9 %collective-permute-start.7 = (f32[8,128]{1,0:T(8,128)S(1)}, f32[8,128]{1,0:T(8,128)S(1)}, u32[]{:S(2)}, u32[]{:S(2)}) collective-permute-start(f32[8,128]{1,0:T(8,128)S(1)} %max.19), channel_id=1, source_target_pairs={{0,16},{4,20},{8,24},{12,28},{16,0},{20,4},{24,8},{28,12},{1,17},{... | collective-permute-start | bytes 12296 | tf_op jit(solution)/shard_map/ppermute | solution.py:393
  23.4 8.5 %collective-permute-start.10 = (f32[104,256]{1,0:T(8,128)S(1)}, f32[104,256]{1,0:T(8,128)S(1)}, u32[]{:S(2)}, u32[]{:S(2)}) collective-permute-start(f32[104,256]{1,0:T(8,128)S(1)} %get-tuple-element.53.refs_13_), channel_id=1, source_target_pairs={{0,3},{1,2},{2,1},{3,0},{4,7},{5,6},{6,5},{7,4},{8,11},{9,10},{10,... | collective-permute-start | bytes 319496 | tf_op jit(solution)/shard_map/ppermute | solution.py:415
  24.9 7.0 %collective-permute-start.11 = (f32[104,256]{1,0:T(8,128)S(1)}, f32[104,256]{1,0:T(8,128)S(1)}, u32[]{:S(2)}, u32[]{:S(2)}) collective-permute-start(f32[104,256]{1,0:T(8,128)S(1)} %get-tuple-element.54.refs_14_), channel_id=1, source_target_pairs={{0,1},{1,0},{2,3},{3,2},{4,5},{5,4},{6,7},{7,6},{8,9},{9,8},{10,11... | collective-permute-start | bytes 319496 | tf_op jit(solution)/shard_map/ppermute | solution.py:416
  25.4 5.9 %collective-permute-start.8 = (f32[96,256]{1,0:T(8,128)S(1)}, f32[96,256]{1,0:T(8,128)S(1)}, u32[]{:S(2)}, u32[]{:S(2)}) collective-permute-start(f32[96,256]{1,0:T(8,128)S(1)} %get-tuple-element.52.refs_12_), channel_id=1, source_target_pairs={{0,4},{4,0},{8,12},{12,8},{16,20},{20,16},{24,28},{28,24},{1,5},{5... | collective-permute-start | bytes 294920 | tf_op jit(solution)/shard_map/ppermute | solution.py:414
  25.4 6.4 %collective-permute-start.13 = (f32[8,128]{1,0:T(8,128)S(1)}, f32[8,128]{1,0:T(8,128)S(1)}, u32[]{:S(2)}, u32[]{:S(2)}) collective-permute-start(f32[8,128]{1,0:T(8,128)S(1)} %max.20.refs_7_), channel_id=1, source_target_pairs={{0,2},{1,3},{2,0},{3,1},{4,6},{5,7},{6,4},{7,5},{8,10},{9,11},{10,... | collective-permute-start | bytes 12296 | tf_op jit(solution)/shard_map/ppermute | solution.py:454
  26.9 4.9 %collective-permute-start.12 = (f32[96,256]{1,0:T(8,128)S(1)}, f32[96,256]{1,0:T(8,128)S(1)}, u32[]{:S(2)}, u32[]{:S(2)}) collective-permute-start(f32[96,256]{1,0:T(8,128)S(1)} %get-tuple-element.55.refs_15_), channel_id=1, source_target_pairs={{0,4},{4,0},{8,12},{12,8},{16,20},{20,16},{24,28},{28,24},{1,5},{5... | collective-permute-start | bytes 294920 | tf_op jit(solution)/shard_map/ppermute | solution.py:418
  31.3 2.7 %collective-permute-start.9 = (f32[96,256]{1,0:T(8,128)S(1)}, f32[96,256]{1,0:T(8,128)S(1)}, u32[]{:S(2)}, u32[]{:S(2)}) collective-permute-start(f32[96,256]{1,0:T(8,128)S(1)} %collective-permute-done.8), channel_id=1, source_target_pairs={{0,8},{8,16},{16,24},{24,28},{4,0},{12,4},{20,12},{28,20},{1,9},{9... | collective-permute-start | bytes 294920 | tf_op jit(solution)/shard_map/ppermute | solution.py:417
  34.7 3.1 %collective-permute-start.14 = (f32[96,256]{1,0:T(8,128)S(1)}, f32[96,256]{1,0:T(8,128)S(1)}, u32[]{:S(2)}, u32[]{:S(2)}) collective-permute-start(f32[96,256]{1,0:T(8,128)S(1)} %get-tuple-element.59), channel_id=1, source_target_pairs={{0,4},{4,0},{8,12},{12,8},{16,20},{20,16},{24,28},{28,24},{1,5},{5... | collective-permute-start | bytes 294920 | tf_op jit(solution)/shard_map/ppermute | solution.py:414
  35.8 8.1 %collective-permute-start.16 = (f32[96,256]{1,0:T(8,128)S(1)}, f32[96,256]{1,0:T(8,128)S(1)}, u32[]{:S(2)}, u32[]{:S(2)}) collective-permute-start(f32[96,256]{1,0:T(8,128)S(1)} %get-tuple-element.60), channel_id=1, source_target_pairs={{0,3},{1,2},{2,1},{3,0},{4,7},{5,6},{6,5},{7,4},{8,11},{9,10},{10,... | collective-permute-start | bytes 294920 | tf_op jit(solution)/shard_map/ppermute | solution.py:415
  37.3 6.7 %collective-permute-start.17 = (f32[96,256]{1,0:T(8,128)S(1)}, f32[96,256]{1,0:T(8,128)S(1)}, u32[]{:S(2)}, u32[]{:S(2)}) collective-permute-start(f32[96,256]{1,0:T(8,128)S(1)} %get-tuple-element.61), channel_id=1, source_target_pairs={{0,1},{1,0},{2,3},{3,2},{4,5},{5,4},{6,7},{7,6},{8,9},{9,8},{10,11... | collective-permute-start | bytes 294920 | tf_op jit(solution)/shard_map/ppermute | solution.py:416
  37.8 6.2 %collective-permute-start.18 = (f32[96,256]{1,0:T(8,128)S(1)}, f32[96,256]{1,0:T(8,128)S(1)}, u32[]{:S(2)}, u32[]{:S(2)}) collective-permute-start(f32[96,256]{1,0:T(8,128)S(1)} %get-tuple-element.62), channel_id=1, source_target_pairs={{0,4},{4,0},{8,12},{12,8},{16,20},{20,16},{24,28},{28,24},{1,5},{5... | collective-permute-start | bytes 294920 | tf_op jit(solution)/shard_map/ppermute | solution.py:418
  37.8 6.2 %collective-permute-start.15 = (f32[96,256]{1,0:T(8,128)S(1)}, f32[96,256]{1,0:T(8,128)S(1)}, u32[]{:S(2)}, u32[]{:S(2)}) collective-permute-start(f32[96,256]{1,0:T(8,128)S(1)} %collective-permute-done.14), channel_id=1, source_target_pairs={{0,8},{8,16},{16,24},{24,28},{4,0},{12,4},{20,12},{28,20},{1,9},{9... | collective-permute-start | bytes 294920 | tf_op jit(solution)/shard_map/ppermute | solution.py:417
  44.7 3.1 %collective-permute-start.19 = (f32[96,256]{1,0:T(8,128)S(1)}, f32[96,256]{1,0:T(8,128)S(1)}, u32[]{:S(2)}, u32[]{:S(2)}) collective-permute-start(f32[96,256]{1,0:T(8,128)S(1)} %get-tuple-element.66), channel_id=1, source_target_pairs={{0,4},{4,0},{8,12},{12,8},{16,20},{20,16},{24,28},{28,24},{1,5},{5... | collective-permute-start | bytes 294920 | tf_op jit(solution)/shard_map/ppermute | solution.py:414
  44.7 8.7 %collective-permute-start.21 = (f32[96,256]{1,0:T(8,128)S(1)}, f32[96,256]{1,0:T(8,128)S(1)}, u32[]{:S(2)}, u32[]{:S(2)}) collective-permute-start(f32[96,256]{1,0:T(8,128)S(1)} %get-tuple-element.67), channel_id=1, source_target_pairs={{0,3},{1,2},{2,1},{3,0},{4,7},{5,6},{6,5},{7,4},{8,11},{9,10},{10,... | collective-permute-start | bytes 294920 | tf_op jit(solution)/shard_map/ppermute | solution.py:415
  47.2 6.2 %collective-permute-start.22 = (f32[96,256]{1,0:T(8,128)S(1)}, f32[96,256]{1,0:T(8,128)S(1)}, u32[]{:S(2)}, u32[]{:S(2)}) collective-permute-start(f32[96,256]{1,0:T(8,128)S(1)} %get-tuple-element.68), channel_id=1, source_target_pairs={{0,1},{1,0},{2,3},{3,2},{4,5},{5,4},{6,7},{7,6},{8,9},{9,8},{10,11... | collective-permute-start | bytes 294920 | tf_op jit(solution)/shard_map/ppermute | solution.py:416
  47.7 5.7 %collective-permute-start.23 = (f32[96,256]{1,0:T(8,128)S(1)}, f32[96,256]{1,0:T(8,128)S(1)}, u32[]{:S(2)}, u32[]{:S(2)}) collective-permute-start(f32[96,256]{1,0:T(8,128)S(1)} %get-tuple-element.69), channel_id=1, source_target_pairs={{0,4},{4,0},{8,12},{12,8},{16,20},{20,16},{24,28},{28,24},{1,5},{5... | collective-permute-start | bytes 294920 | tf_op jit(solution)/shard_map/ppermute | solution.py:418
  47.8 5.7 %collective-permute-start.20 = (f32[96,256]{1,0:T(8,128)S(1)}, f32[96,256]{1,0:T(8,128)S(1)}, u32[]{:S(2)}, u32[]{:S(2)}) collective-permute-start(f32[96,256]{1,0:T(8,128)S(1)} %collective-permute-done.19), channel_id=1, source_target_pairs={{0,8},{8,16},{16,24},{24,28},{4,0},{12,4},{20,12},{28,20},{1,9},{9... | collective-permute-start | bytes 294920 | tf_op jit(solution)/shard_map/ppermute | solution.py:417
  54.6 1.3 %collective-permute-start.24 = (f32[48,128]{1,0:T(8,128)S(1)}, f32[48,128]{1,0:T(8,128)S(1)}, u32[]{:S(2)}, u32[]{:S(2)}) collective-permute-start(f32[48,128]{1,0:T(8,128)S(1)} %shard_map.63), channel_id=1, source_target_pairs={{0,4},{4,0},{8,12},{12,8},{16,20},{20,16},{24,28},{28,24},{1,5},{5... | collective-permute-start | bytes 73736 | tf_op jit(solution)/shard_map/ppermute | solution.py:393
  55.9 3.8 %collective-permute-start.27 = (f32[48,128]{1,0:T(8,128)S(1)}, f32[48,128]{1,0:T(8,128)S(1)}, u32[]{:S(2)}, u32[]{:S(2)}) collective-permute-start(f32[48,128]{1,0:T(8,128)S(1)} %add.12), channel_id=1, source_target_pairs={{0,8},{4,12},{8,0},{12,4},{16,24},{20,28},{24,16},{28,20},{1,9},{5... | collective-permute-start | bytes 73736 | tf_op jit(solution)/shard_map/ppermute | solution.py:399
  57.4 5.6 %collective-permute-start.26 = (f32[48,128]{1,0:T(8,128)S(1)}, f32[48,128]{1,0:T(8,128)S(1)}, u32[]{:S(2)}, u32[]{:S(2)}) collective-permute-start(f32[48,128]{1,0:T(8,128)S(1)} %add.12), channel_id=1, source_target_pairs={{0,24},{4,28},{8,16},{12,20},{16,8},{20,12},{24,0},{28,4},{1,25},{... | collective-permute-start | bytes 73736 | tf_op jit(solution)/shard_map/ppermute | solution.py:399
  58.7 5.0 %collective-permute-start.25 = (f32[48,128]{1,0:T(8,128)S(1)}, f32[48,128]{1,0:T(8,128)S(1)}, u32[]{:S(2)}, u32[]{:S(2)}) collective-permute-start(f32[48,128]{1,0:T(8,128)S(1)} %add.12), channel_id=1, source_target_pairs={{0,16},{4,20},{8,24},{12,28},{16,0},{20,4},{24,8},{28,12},{1,17},{... | collective-permute-start | bytes 73736 | tf_op jit(solution)/shard_map/ppermute | solution.py:399
  63.7 4.6 %collective-permute-start.30 = (f32[48,128]{1,0:T(8,128)S(1)}, f32[48,128]{1,0:T(8,128)S(1)}, u32[]{:S(2)}, u32[]{:S(2)}) collective-permute-start(f32[48,128]{1,0:T(8,128)S(1)} %add_add_fusion.refs_0_), channel_id=1, source_target_pairs={{0,1},{1,0},{2,3},{3,2},{4,5},{5,4},{6,7},{7,6},{8,9},{9,8},{10,11... | collective-permute-start | bytes 73736 | tf_op jit(solution)/shard_map/ppermute | solution.py:399
  65.2 3.8 %collective-permute-start.29 = (f32[48,128]{1,0:T(8,128)S(1)}, f32[48,128]{1,0:T(8,128)S(1)}, u32[]{:S(2)}, u32[]{:S(2)}) collective-permute-start(f32[48,128]{1,0:T(8,128)S(1)} %add_add_fusion.refs_0_), channel_id=1, source_target_pairs={{0,2},{1,3},{2,0},{3,1},{4,6},{5,7},{6,4},{7,5},{8,10},{9,11},{10,... | collective-permute-start | bytes 73736 | tf_op jit(solution)/shard_map/ppermute | solution.py:399
  65.8 4.7 %collective-permute-start.28 = (f32[48,128]{1,0:T(8,128)S(1)}, f32[48,128]{1,0:T(8,128)S(1)}, u32[]{:S(2)}, u32[]{:S(2)}) collective-permute-start(f32[48,128]{1,0:T(8,128)S(1)} %add_add_fusion.refs_0_), channel_id=1, source_target_pairs={{0,3},{1,2},{2,1},{3,0},{4,7},{5,6},{6,5},{7,4},{8,11},{9,10},{10,... | collective-permute-start | bytes 73736 | tf_op jit(solution)/shard_map/ppermute | solution.py:399

commit v5 on v4

--- a/solution.py
+++ b/solution.py
@@ -257,7 +257,6 @@
             later[:, part] = first
         else:
             value = local[:, part] - (2.0 / half) * crossed
-            later[:, part] = begin[:, part]
         field[:, part] = value
     multiply(cols, field, stored, inside)
     for part in chunks(cells):
@@ -267,7 +266,8 @@
             later[:, part] = degree[0:1, part] * field[:, part] - kept
         else:
             value = (degree[0:1, part] - centre) * field[:, part] - kept
-            later[:, part] = (2.0 / half) * value - later[:, part]
+            before = later[:, part] if number == 1 else begin[:, part]
+            later[:, part] = (2.0 / half) * value - before
     edge_local[...] = gather(later[...], place)
     if number == 2:
         refs[3][...] = product_nt(later[...], later[...])
@@ -320,11 +320,12 @@
         terms[:, part] = jnp.concatenate([hi, lo, hi], axis=0)
 
 
-def eliminate(block, start, right):
+def eliminate(block, start, right, tiles):
     size, width = block.shape
+    for j in range(size):
+        tiles[j] = jnp.broadcast_to(block[:, start + j : start + j + 1], (size, width))
     near = [
-        [jnp.broadcast_to(block[i : i + 1, start + j : start + j + 1], (size, width)) for j in range(i + 1)]
-        for i in range(size)
+        [jnp.broadcast_to(tiles[j, i : i + 1], (size, width)) for j in range(i + 1)] for i in range(size)
     ]
     rows, factors, inverses = list(right), [[] for _ in range(size)], []
     for k in range(size):
@@ -344,7 +345,7 @@
 
 
 def encode_kernel(root, *refs):
-    *parts, values, out = refs
+    *parts, values, out, tiles = refs
     gram = unpacked(total(part[...] for part in parts))
     vecs = gram.shape[0]
     size = 8
@@ -356,7 +357,7 @@
         inside = jnp.logical_and(lane >= start, lane < start + size)
         unit = jnp.where(inside, (lane - start == sub).astype(F32), rows[g])
         spread_rows = [jnp.broadcast_to(unit[j : j + 1], (size, vecs)) for j in range(size)]
-        half, whole = eliminate(rows[g], start, spread_rows)
+        half, whole = eliminate(rows[g], start, spread_rows, tiles.at[g % 2])
         for i in range(g + 1, vecs // size):
             kept = jnp.where(inside, 0.0, rows[i])
             rows[i] = kept - total(
@@ -498,7 +499,7 @@
         parts = [spread(gram, jnp.add, stages[1:])]
     now = call(last_kernel, shape(3 * vecs, cells, dtype=BF16), [VM] * 7)(*arrived, local, back, peak)
     root = math.sqrt(cells * sizes[0] * sizes[1])
-    return call(functools.partial(encode_kernel, root), shape(1, 1, vecs, cells), [VM] * (len(parts) + 1))(
+    return call(functools.partial(encode_kernel, root), shape(1, 1, vecs, cells), [VM] * (len(parts) + 1), scratch_shapes=[pltpu.VMEM((2, 8, 8, vecs), F32)])(
         *parts, now
     )
 

time: 75.8 us -> 75.3 us (level)
  no operation moved by 1% of the time
where the time goes in v5:
time: 75.3 us; the launch traced here: 75.1 us
  Pallas kernels  30.9 us (41%)
  starting transfers between devices  30.1 us (40%)
  waiting for transfers between devices  13.1 us (17%)
  between operations  0.93 us (1%)
    pallas_call x3, Pallas kernels, per_device(): call(functools.partial(field_kernel, number), [field, field, edge_field]...  13.8 us
    ppermute x4, starting transfers between devices, exchange(): y_far = lax.ppermute(y_far, 'gy', far_pairs(sizes[1]))  8.94 us
    ppermute x6, starting transfers between devices, all_of(): lax.ppermute(value, axis, xor_pairs(size, bit))  7.04 us
    ppermute x6, waiting for transfers between devices, all_of(): lax.ppermute(value, axis, xor_pairs(size, bit))  6.44 us
    pallas_call x1, Pallas kernels, per_device(): call(functools.partial(encode_kernel, root), shape(1, 1, vecs, cells), [V...  4.57 us
    ppermute x4, waiting for transfers between devices, spread(): value = combine(value, lax.ppermute(value, axis, pairs))  4.39 us
    pallas_call x1, Pallas kernels, per_device(): call(open_kernel, [field, edge_field, shape(4 * edges, 4 * edges, dtype=B...  4.27 us
    ppermute x4, starting transfers between devices, exchange(): x_far = lax.ppermute(x_far, 'gx', turn_pairs(sizes[0]))  4.27 us
  transfers between devices with their start and end apart: 31, of which 9 were waited for; matrix products, arithmetic and copies ran while one was open for 0% of the time, Pallas kernels for 25%

profile of v5, /device:TPU:0, one launch (start us, length us, event | category | flops | bytes accessed | tf_op | source)
XLA Modules:
  0.0 75.1 jit_solution(1241998384477251017)
XLA Ops:
  0.7 4.2 %shard_map.55 = (bf16[2048,1024]{1,0:T(8,128)(2,1)S(1)}, bf16[16,256,640]{2,1,0:T(8,128)(2,1)S(1)}, f32[96,2048]{1,0:T(8,128)S(1)}, f32[8,2048]{1,0:T(8,128)S(1)...) custom-call(s32[1,1]{1,0:T(1,128)S(6)} %copy.6.counts, ...), custom_call_target="tpu_custom_call" | custom-call | tf_op jit(solution)/shard_map/pallas_call | solution.py:423
  4.8 0.6 collective-permute-start
  5.4 3.5 %collective-permute-start.2 = (f32[96,256]{1,0:T(8,128)S(1)}, f32[96,256]{1,0:T(8,128)S(1)}, u32[]{:S(2)}, u32[]{:S(2)}) collective-permute-start(f32[96,256]{1,0:T(8,128)S(1)} %get-tuple-element.41.refs_9_), channel_id=1, source_target_pairs={{0,3},{1,2},{2,1},{3,0},{4,7},{5,6},{6,5},{7,4},{8,11},{9,10},{10,... | collective-permute-start | bytes 294920 | tf_op jit(solution)/shard_map/ppermute | solution.py:416
  8.9 0.5 collective-permute-start.3
  9.5 0.0 collective-permute-start.4
  9.5 1.6 %collective-permute-start.1 = (f32[96,256]{1,0:T(8,128)S(1)}, f32[96,256]{1,0:T(8,128)S(1)}, u32[]{:S(2)}, u32[]{:S(2)}) collective-permute-start(f32[96,256]{1,0:T(8,128)S(1)} %collective-permute-done), channel_id=1, source_target_pairs={{0,8},{8,16},{16,24},{24,28},{4,0},{12,4},{20,12},{28,20},{1,9},{9... | collective-permute-start | bytes 294920 | tf_op jit(solution)/shard_map/ppermute | solution.py:418
  11.0 0.0 collective-permute-start.5
  11.0 1.2 %collective-permute-done.5 = f32[8,128]{1,0:T(8,128)S(1)} collective-permute-done((f32[8,128]{1,0:T(8,128)S(1)}, f32[8,128]{1,0:T(8,128)S(1)}, u32[]{:S(2)}, u32[]{:S(2)}) %collective-permute-start.5) | collective-permute-done | bytes 4128 | tf_op jit(solution)/shard_map/ppermute | solution.py:394
  12.2 1.6 %collective-permute-start.6 = (f32[8,128]{1,0:T(8,128)S(1)}, f32[8,128]{1,0:T(8,128)S(1)}, u32[]{:S(2)}, u32[]{:S(2)}) collective-permute-start(f32[8,128]{1,0:T(8,128)S(1)} %max.18), channel_id=1, source_target_pairs={{0,8},{4,12},{8,0},{12,4},{16,24},{20,28},{24,16},{28,20},{1,9},{5... | collective-permute-start | bytes 12296 | tf_op jit(solution)/shard_map/ppermute | solution.py:394
  13.8 2.0 %collective-permute-done.6 = f32[8,128]{1,0:T(8,128)S(1)} collective-permute-done((f32[8,128]{1,0:T(8,128)S(1)}, f32[8,128]{1,0:T(8,128)S(1)}, u32[]{:S(2)}, u32[]{:S(2)}) %collective-permute-start.6) | collective-permute-done | bytes 4128 | tf_op jit(solution)/shard_map/ppermute | solution.py:394
  15.8 2.6 %collective-permute-start.7 = (f32[8,128]{1,0:T(8,128)S(1)}, f32[8,128]{1,0:T(8,128)S(1)}, u32[]{:S(2)}, u32[]{:S(2)}) collective-permute-start(f32[8,128]{1,0:T(8,128)S(1)} %max.19), channel_id=1, source_target_pairs={{0,16},{4,20},{8,24},{12,28},{16,0},{20,4},{24,8},{28,12},{1,17},{... | collective-permute-start | bytes 12296 | tf_op jit(solution)/shard_map/ppermute | solution.py:394
  18.4 4.3 %shard_map.56 = (f32[96,2048]{1,0:T(8,128)S(1)}, f32[96,1024]{1,0:T(8,128)S(1)}, bf16[1024,1024]{1,0:T(8,128)(2,1)S(1)}, bf16[1024,2048]{1,0:T(8,128)(2,1)S(1)}) custom-call(s32[1,5,1,16]{3,2,1,0:T(1,128)S(1)} %bitcast.2, s32[1,1]{1,0:T(1,128)S(6)} %copy.6.counts, f32[96,2048]{1,0:T(8,128)S(1)} %get-tuple-element.44.begin.once, ...), custom_call_target="tpu_custom_call" | custom-call | tf_op jit(solution)/shard_map/pallas_call | solution.py:456
  22.8 0.6 shard_map.57
  23.4 1.5 %collective-permute-start.10 = (f32[104,256]{1,0:T(8,128)S(1)}, f32[104,256]{1,0:T(8,128)S(1)}, u32[]{:S(2)}, u32[]{:S(2)}) collective-permute-start(f32[104,256]{1,0:T(8,128)S(1)} %get-tuple-element.53.refs_13_), channel_id=1, source_target_pairs={{0,3},{1,2},{2,1},{3,0},{4,7},{5,6},{6,5},{7,4},{8,11},{9,10},{10,... | collective-permute-start | bytes 319496 | tf_op jit(solution)/shard_map/ppermute | solution.py:416
  24.9 0.6 collective-permute-start.11
  25.4 1.5 %collective-permute-start.13 = (f32[8,128]{1,0:T(8,128)S(1)}, f32[8,128]{1,0:T(8,128)S(1)}, u32[]{:S(2)}, u32[]{:S(2)}) collective-permute-start(f32[8,128]{1,0:T(8,128)S(1)} %max.20.refs_7_), channel_id=1, source_target_pairs={{0,2},{1,3},{2,0},{3,1},{4,6},{5,7},{6,4},{7,5},{8,10},{9,11},{10,... | collective-permute-start | bytes 12296 | tf_op jit(solution)/shard_map/ppermute | solution.py:455
  26.9 0.2 collective-permute-start.12
  27.2 4.1 %shard_map.58 = (f32[96,2048]{1,0:T(8,128)S(1)}, f32[96,2048]{1,0:T(8,128)S(1)}, f32[96,1024]{1,0:T(8,128)S(1)}) custom-call(s32[1,5,1,16]{3,2,1,0:T(1,128)S(1)} %bitcast.3, s32[1,1]{1,0:T(1,128)S(6)} %copy.6.counts, f32[96,256]{1,0:T(8,128)S(1)} %collective-permute-done.1.refs_0_.r0, f32[96,256]{1,0:T(8,128)S(1)} %collective-permute-done.2.refs_1_.r1, ...), custom_call_target="tpu_custom_call" | custom-call | tf_op jit(solution)/shard_map/pallas_call | solution.py:485
  31.3 0.5 collective-permute-start.9
  31.9 2.2 %collective-permute-done.9.refs_0_.r0 = f32[96,256]{1,0:T(8,128)S(1)} collective-permute-done((f32[96,256]{1,0:T(8,128)S(1)}, f32[96,256]{1,0:T(8,128)S(1)}, u32[]{:S(2)}, u32[]{:S(2)}) %collective-permute-start.9) | collective-permute-done | bytes 98336 | tf_op jit(solution)/shard_map/ppermute | solution.py:418
  34.0 0.7 shard_map.59
  34.7 1.1 %collective-permute-start.14 = (f32[96,256]{1,0:T(8,128)S(1)}, f32[96,256]{1,0:T(8,128)S(1)}, u32[]{:S(2)}, u32[]{:S(2)}) collective-permute-start(f32[96,256]{1,0:T(8,128)S(1)} %get-tuple-element.59), channel_id=1, source_target_pairs={{0,4},{4,0},{8,12},{12,8},{16,20},{20,16},{24,28},{28,24},{1,5},{5... | collective-permute-start | bytes 294920 | tf_op jit(solution)/shard_map/ppermute | solution.py:415
  35.8 1.4 %collective-permute-start.16 = (f32[96,256]{1,0:T(8,128)S(1)}, f32[96,256]{1,0:T(8,128)S(1)}, u32[]{:S(2)}, u32[]{:S(2)}) collective-permute-start(f32[96,256]{1,0:T(8,128)S(1)} %get-tuple-element.60), channel_id=1, source_target_pairs={{0,3},{1,2},{2,1},{3,0},{4,7},{5,6},{6,5},{7,4},{8,11},{9,10},{10,... | collective-permute-start | bytes 294920 | tf_op jit(solution)/shard_map/ppermute | solution.py:416
  37.3 0.6 collective-permute-start.17
  37.8 1.5 %collective-permute-start.15 = (f32[96,256]{1,0:T(8,128)S(1)}, f32[96,256]{1,0:T(8,128)S(1)}, u32[]{:S(2)}, u32[]{:S(2)}) collective-permute-start(f32[96,256]{1,0:T(8,128)S(1)} %collective-permute-done.14), channel_id=1, source_target_pairs={{0,8},{8,16},{16,24},{24,28},{4,0},{12,4},{20,12},{28,20},{1,9},{9... | collective-permute-start | bytes 294920 | tf_op jit(solution)/shard_map/ppermute | solution.py:418
  39.3 4.7 %shard_map.60 = (f32[96,2048]{1,0:T(8,128)S(1)}, f32[96,2048]{1,0:T(8,128)S(1)}, f32[96,1024]{1,0:T(8,128)S(1)}) custom-call(s32[1,5,1,16]{3,2,1,0:T(1,128)S(1)} %bitcast.4, s32[1,1]{1,0:T(1,128)S(6)} %copy.6.counts, f32[96,256]{1,0:T(8,128)S(1)} %collective-permute-done.9.refs_0_.r0, f32[104,256]{1,0:T(8,128)S(1)} %collective-permute-done.10.refs_1_.r1, ...), custom_call_target="tpu_custom_call" | custom-call | tf_op jit(solution)/shard_map/pallas_call | solution.py:485
  44.0 0.6 shard_map.61
  44.7 0.1 collective-permute-start.19
  44.7 2.5 %collective-permute-start.21 = (f32[96,256]{1,0:T(8,128)S(1)}, f32[96,256]{1,0:T(8,128)S(1)}, u32[]{:S(2)}, u32[]{:S(2)}) collective-permute-start(f32[96,256]{1,0:T(8,128)S(1)} %get-tuple-element.67), channel_id=1, source_target_pairs={{0,3},{1,2},{2,1},{3,0},{4,7},{5,6},{6,5},{7,4},{8,11},{9,10},{10,... | collective-permute-start | bytes 294920 | tf_op jit(solution)/shard_map/ppermute | solution.py:416
  47.2 0.5 collective-permute-start.22
  47.8 0.7 collective-permute-start.20
  48.5 5.0 %shard_map.62 = (f32[96,2048]{1,0:T(8,128)}, f32[96,2048]{1,0:T(8,128)S(1)}, f32[96,1024]{1,0:T(8,128)S(1)}, f32[96,96]{1,0:T(8,128)S(1)}) custom-call(s32[1,5,1,16]{3,2,1,0:T(1,128)S(1)} %bitcast.5, s32[1,1]{1,0:T(1,128)S(6)} %copy.6.counts, f32[96,256]{1,0:T(8,128)S(1)} %collective-permute-done.15.refs_0_.r0, ...), custom_call_target="tpu_custom_call" | custom-call | tf_op jit(solution)/shard_map/pallas_call | solution.py:485
  53.5 1.1 %shard_map.63 = f32[48,128]{1,0:T(8,128)S(1)} custom-call(f32[96,256]{1,0:T(8,128)S(1)} %collective-permute-done.20.r0, f32[96,256]{1,0:T(8,128)S(1)} %collective-permute-done.21.r1, f32[96,256]{1,0:T(8,128)S(1)} %collective-permute-done.22.r2, f32[96,256]{1,0:T(8,128)S(1)} %collective-permute-done.23.r3, f32[96,1024]{1,0:T(8,128)S(1)} %get-tuple-element.72.edge_local, ...), custom_call_target="tpu_custom_call" | custom-call | tf_op jit(solution)/shard_map/pallas_call | solution.py:494
  54.6 0.1 collective-permute-start.24
  54.7 1.2 %collective-permute-done.24 = f32[48,128]{1,0:T(8,128)S(1)} collective-permute-done((f32[48,128]{1,0:T(8,128)S(1)}, f32[48,128]{1,0:T(8,128)S(1)}, u32[]{:S(2)}, u32[]{:S(2)}) %collective-permute-start.24) | collective-permute-done | bytes 24608 | tf_op jit(solution)/shard_map/ppermute | solution.py:394
  55.9 1.5 %collective-permute-start.27 = (f32[48,128]{1,0:T(8,128)S(1)}, f32[48,128]{1,0:T(8,128)S(1)}, u32[]{:S(2)}, u32[]{:S(2)}) collective-permute-start(f32[48,128]{1,0:T(8,128)S(1)} %add.12), channel_id=1, source_target_pairs={{0,8},{4,12},{8,0},{12,4},{16,24},{20,28},{24,16},{28,20},{1,9},{5... | collective-permute-start | bytes 73736 | tf_op jit(solution)/shard_map/ppermute | solution.py:400
  57.4 1.4 %collective-permute-start.26 = (f32[48,128]{1,0:T(8,128)S(1)}, f32[48,128]{1,0:T(8,128)S(1)}, u32[]{:S(2)}, u32[]{:S(2)}) collective-permute-start(f32[48,128]{1,0:T(8,128)S(1)} %add.12), channel_id=1, source_target_pairs={{0,24},{4,28},{8,16},{12,20},{16,8},{20,12},{24,0},{28,4},{1,25},{... | collective-permute-start | bytes 73736 | tf_op jit(solution)/shard_map/ppermute | solution.py:400
  58.7 0.7 collective-permute-start.25
  59.4 0.3 collective-permute-done.27
  59.7 3.3 %collective-permute-done.26 = f32[48,128]{1,0:T(8,128)S(1)} collective-permute-done((f32[48,128]{1,0:T(8,128)S(1)}, f32[48,128]{1,0:T(8,128)S(1)}, u32[]{:S(2)}, u32[]{:S(2)}) %collective-permute-start.26) | collective-permute-done | bytes 24608 | tf_op jit(solution)/shard_map/ppermute | solution.py:400
  63.0 0.7 collective-permute-done.25
  63.7 1.5 %collective-permute-start.30 = (f32[48,128]{1,0:T(8,128)S(1)}, f32[48,128]{1,0:T(8,128)S(1)}, u32[]{:S(2)}, u32[]{:S(2)}) collective-permute-start(f32[48,128]{1,0:T(8,128)S(1)} %add_add_fusion.refs_0_), channel_id=1, source_target_pairs={{0,1},{1,0},{2,3},{3,2},{4,5},{5,4},{6,7},{7,6},{8,9},{9,8},{10,11... | collective-permute-start | bytes 73736 | tf_op jit(solution)/shard_map/ppermute | solution.py:400
  65.2 0.5 collective-permute-start.29
  65.8 1.5 %collective-permute-start.28 = (f32[48,128]{1,0:T(8,128)S(1)}, f32[48,128]{1,0:T(8,128)S(1)}, u32[]{:S(2)}, u32[]{:S(2)}) collective-permute-start(f32[48,128]{1,0:T(8,128)S(1)} %add_add_fusion.refs_0_), channel_id=1, source_target_pairs={{0,3},{1,2},{2,1},{3,0},{4,7},{5,6},{6,5},{7,4},{8,11},{9,10},{10,... | collective-permute-start | bytes 73736 | tf_op jit(solution)/shard_map/ppermute | solution.py:400
  67.3 1.1 %shard_map.64.refs_4_ = bf16[288,2048]{1,0:T(8,128)(2,1)S(1)} custom-call(f32[96,256]{1,0:T(8,128)S(1)} %collective-permute-done.20.r0, f32[96,256]{1,0:T(8,128)S(1)} %collective-permute-done.21.r1, f32[96,256]{1,0:T(8,128)S(1)} %collective-permute-done.22.r2, f32[96,256]{1,0:T(8,128)S(1)} %collective-permute-done.23.r3, ...), custom_call_target="tpu_custom_call" | custom-call | tf_op jit(solution)/shard_map/pallas_call | solution.py:500
  68.4 0.7 collective-permute-done.29.refs_2_
  69.1 1.4 %collective-permute-done.28.refs_1_ = f32[48,128]{1,0:T(8,128)S(1)} collective-permute-done((f32[48,128]{1,0:T(8,128)S(1)}, f32[48,128]{1,0:T(8,128)S(1)}, u32[]{:S(2)}, u32[]{:S(2)}) %collective-permute-start.28) | collective-permute-done | bytes 24608 | tf_op jit(solution)/shard_map/ppermute | solution.py:400
  70.5 4.6 %shard_map.65 = f32[1,1,96,2048]{3,2,1,0:T(8,128)} custom-call(f32[48,128]{1,0:T(8,128)S(1)} %add_add_fusion.refs_0_, f32[48,128]{1,0:T(8,128)S(1)} %collective-permute-done.28.refs_1_, f32[48,128]{1,0:T(8,128)S(1)} %collective-permute-done.29.refs_2_, f32[48,128]{1,0:T(8,128)S(1)} %collective-permute-done.30.refs_3_, bf16[288,2048]{1,0:T(8,128)(2,1)S(1)} %shard_map.64.refs_4_), custom_call_target="tpu_custom_call" | custom-call | tf_op jit(solution)/shard_map/pallas_call | solution.py:502
  (33 shorter events, 0.1 us)
Async XLA Ops:
  0.0 18.4 %copy-start = (s32[1,1,16,5]{2,1,3,0:T(1,128)S(1)}, s32[1,1,16,5]{2,1,3,0:T(1,128)}, u32[]{:S(2)}) copy-start(s32[1,1,16,5]{2,1,3,0:T(1,128)} %param.7) | copy-start | bytes 964
  4.8 4.6 %collective-permute-start = (f32[96,256]{1,0:T(8,128)S(1)}, f32[96,256]{1,0:T(8,128)S(1)}, u32[]{:S(2)}, u32[]{:S(2)}) collective-permute-start(f32[96,256]{1,0:T(8,128)S(1)} %get-tuple-element.40.refs_8_), channel_id=1, source_target_pairs={{0,4},{4,0},{8,12},{12,8},{16,20},{20,16},{24,28},{28,24},{1,5},{5... | collective-permute-start | bytes 294920 | tf_op jit(solution)/shard_map/ppermute | solution.py:415
  5.4 17.3 %collective-permute-start.2 = (f32[96,256]{1,0:T(8,128)S(1)}, f32[96,256]{1,0:T(8,128)S(1)}, u32[]{:S(2)}, u32[]{:S(2)}) collective-permute-start(f32[96,256]{1,0:T(8,128)S(1)} %get-tuple-element.41.refs_9_), channel_id=1, source_target_pairs={{0,3},{1,2},{2,1},{3,0},{4,7},{5,6},{6,5},{7,4},{8,11},{9,10},{10,... | collective-permute-start | bytes 294920 | tf_op jit(solution)/shard_map/ppermute | solution.py:416
  8.9 13.8 %collective-permute-start.3 = (f32[96,256]{1,0:T(8,128)S(1)}, f32[96,256]{1,0:T(8,128)S(1)}, u32[]{:S(2)}, u32[]{:S(2)}) collective-permute-start(f32[96,256]{1,0:T(8,128)S(1)} %get-tuple-element.42.refs_10_), channel_id=1, source_target_pairs={{0,1},{1,0},{2,3},{3,2},{4,5},{5,4},{6,7},{7,6},{8,9},{9,8},{10,11... | collective-permute-start | bytes 294920 | tf_op jit(solution)/shard_map/ppermute | solution.py:417
  9.5 13.3 %collective-permute-start.4 = (f32[96,256]{1,0:T(8,128)S(1)}, f32[96,256]{1,0:T(8,128)S(1)}, u32[]{:S(2)}, u32[]{:S(2)}) collective-permute-start(f32[96,256]{1,0:T(8,128)S(1)} %get-tuple-element.43.refs_11_), channel_id=1, source_target_pairs={{0,4},{4,0},{8,12},{12,8},{16,20},{20,16},{24,28},{28,24},{1,5},{5... | collective-permute-start | bytes 294920 | tf_op jit(solution)/shard_map/ppermute | solution.py:419
  9.5 13.3 %collective-permute-start.1 = (f32[96,256]{1,0:T(8,128)S(1)}, f32[96,256]{1,0:T(8,128)S(1)}, u32[]{:S(2)}, u32[]{:S(2)}) collective-permute-start(f32[96,256]{1,0:T(8,128)S(1)} %collective-permute-done), channel_id=1, source_target_pairs={{0,8},{8,16},{16,24},{24,28},{4,0},{12,4},{20,12},{28,20},{1,9},{9... | collective-permute-start | bytes 294920 | tf_op jit(solution)/shard_map/ppermute | solution.py:418
  11.0 1.2 %collective-permute-start.5 = (f32[8,128]{1,0:T(8,128)S(1)}, f32[8,128]{1,0:T(8,128)S(1)}, u32[]{:S(2)}, u32[]{:S(2)}) collective-permute-start(f32[8,128]{1,0:T(8,128)S(1)} %get-tuple-element.51.refs_6_.own.peak), channel_id=1, source_target_pairs={{0,4},{4,0},{8,12},{12,8},{16,20},{20,16},{24,28},{28,24},{1,5},{5... | collective-permute-start | bytes 12296 | tf_op jit(solution)/shard_map/ppermute | solution.py:394
  12.2 3.6 %collective-permute-start.6 = (f32[8,128]{1,0:T(8,128)S(1)}, f32[8,128]{1,0:T(8,128)S(1)}, u32[]{:S(2)}, u32[]{:S(2)}) collective-permute-start(f32[8,128]{1,0:T(8,128)S(1)} %max.18), channel_id=1, source_target_pairs={{0,8},{4,12},{8,0},{12,4},{16,24},{20,28},{24,16},{28,20},{1,9},{5... | collective-permute-start | bytes 12296 | tf_op jit(solution)/shard_map/ppermute | solution.py:394
  15.8 6.9 %collective-permute-start.7 = (f32[8,128]{1,0:T(8,128)S(1)}, f32[8,128]{1,0:T(8,128)S(1)}, u32[]{:S(2)}, u32[]{:S(2)}) collective-permute-start(f32[8,128]{1,0:T(8,128)S(1)} %max.19), channel_id=1, source_target_pairs={{0,16},{4,20},{8,24},{12,28},{16,0},{20,4},{24,8},{28,12},{1,17},{... | collective-permute-start | bytes 12296 | tf_op jit(solution)/shard_map/ppermute | solution.py:394
  23.4 8.5 %collective-permute-start.10 = (f32[104,256]{1,0:T(8,128)S(1)}, f32[104,256]{1,0:T(8,128)S(1)}, u32[]{:S(2)}, u32[]{:S(2)}) collective-permute-start(f32[104,256]{1,0:T(8,128)S(1)} %get-tuple-element.53.refs_13_), channel_id=1, source_target_pairs={{0,3},{1,2},{2,1},{3,0},{4,7},{5,6},{6,5},{7,4},{8,11},{9,10},{10,... | collective-permute-start | bytes 319496 | tf_op jit(solution)/shard_map/ppermute | solution.py:416
  24.9 7.0 %collective-permute-start.11 = (f32[104,256]{1,0:T(8,128)S(1)}, f32[104,256]{1,0:T(8,128)S(1)}, u32[]{:S(2)}, u32[]{:S(2)}) collective-permute-start(f32[104,256]{1,0:T(8,128)S(1)} %get-tuple-element.54.refs_14_), channel_id=1, source_target_pairs={{0,1},{1,0},{2,3},{3,2},{4,5},{5,4},{6,7},{7,6},{8,9},{9,8},{10,11... | collective-permute-start | bytes 319496 | tf_op jit(solution)/shard_map/ppermute | solution.py:417
  25.4 5.9 %collective-permute-start.8 = (f32[96,256]{1,0:T(8,128)S(1)}, f32[96,256]{1,0:T(8,128)S(1)}, u32[]{:S(2)}, u32[]{:S(2)}) collective-permute-start(f32[96,256]{1,0:T(8,128)S(1)} %get-tuple-element.52.refs_12_), channel_id=1, source_target_pairs={{0,4},{4,0},{8,12},{12,8},{16,20},{20,16},{24,28},{28,24},{1,5},{5... | collective-permute-start | bytes 294920 | tf_op jit(solution)/shard_map/ppermute | solution.py:415
  25.4 6.4 %collective-permute-start.13 = (f32[8,128]{1,0:T(8,128)S(1)}, f32[8,128]{1,0:T(8,128)S(1)}, u32[]{:S(2)}, u32[]{:S(2)}) collective-permute-start(f32[8,128]{1,0:T(8,128)S(1)} %max.20.refs_7_), channel_id=1, source_target_pairs={{0,2},{1,3},{2,0},{3,1},{4,6},{5,7},{6,4},{7,5},{8,10},{9,11},{10,... | collective-permute-start | bytes 12296 | tf_op jit(solution)/shard_map/ppermute | solution.py:455
  26.9 4.9 %collective-permute-start.12 = (f32[96,256]{1,0:T(8,128)S(1)}, f32[96,256]{1,0:T(8,128)S(1)}, u32[]{:S(2)}, u32[]{:S(2)}) collective-permute-start(f32[96,256]{1,0:T(8,128)S(1)} %get-tuple-element.55.refs_15_), channel_id=1, source_target_pairs={{0,4},{4,0},{8,12},{12,8},{16,20},{20,16},{24,28},{28,24},{1,5},{5... | collective-permute-start | bytes 294920 | tf_op jit(solution)/shard_map/ppermute | solution.py:419
  31.3 2.7 %collective-permute-start.9 = (f32[96,256]{1,0:T(8,128)S(1)}, f32[96,256]{1,0:T(8,128)S(1)}, u32[]{:S(2)}, u32[]{:S(2)}) collective-permute-start(f32[96,256]{1,0:T(8,128)S(1)} %collective-permute-done.8), channel_id=1, source_target_pairs={{0,8},{8,16},{16,24},{24,28},{4,0},{12,4},{20,12},{28,20},{1,9},{9... | collective-permute-start | bytes 294920 | tf_op jit(solution)/shard_map/ppermute | solution.py:418
  34.7 3.1 %collective-permute-start.14 = (f32[96,256]{1,0:T(8,128)S(1)}, f32[96,256]{1,0:T(8,128)S(1)}, u32[]{:S(2)}, u32[]{:S(2)}) collective-permute-start(f32[96,256]{1,0:T(8,128)S(1)} %get-tuple-element.59), channel_id=1, source_target_pairs={{0,4},{4,0},{8,12},{12,8},{16,20},{20,16},{24,28},{28,24},{1,5},{5... | collective-permute-start | bytes 294920 | tf_op jit(solution)/shard_map/ppermute | solution.py:415
  35.8 8.1 %collective-permute-start.16 = (f32[96,256]{1,0:T(8,128)S(1)}, f32[96,256]{1,0:T(8,128)S(1)}, u32[]{:S(2)}, u32[]{:S(2)}) collective-permute-start(f32[96,256]{1,0:T(8,128)S(1)} %get-tuple-element.60), channel_id=1, source_target_pairs={{0,3},{1,2},{2,1},{3,0},{4,7},{5,6},{6,5},{7,4},{8,11},{9,10},{10,... | collective-permute-start | bytes 294920 | tf_op jit(solution)/shard_map/ppermute | solution.py:416
  37.3 6.7 %collective-permute-start.17 = (f32[96,256]{1,0:T(8,128)S(1)}, f32[96,256]{1,0:T(8,128)S(1)}, u32[]{:S(2)}, u32[]{:S(2)}) collective-permute-start(f32[96,256]{1,0:T(8,128)S(1)} %get-tuple-element.61), channel_id=1, source_target_pairs={{0,1},{1,0},{2,3},{3,2},{4,5},{5,4},{6,7},{7,6},{8,9},{9,8},{10,11... | collective-permute-start | bytes 294920 | tf_op jit(solution)/shard_map/ppermute | solution.py:417
  37.8 6.2 %collective-permute-start.18 = (f32[96,256]{1,0:T(8,128)S(1)}, f32[96,256]{1,0:T(8,128)S(1)}, u32[]{:S(2)}, u32[]{:S(2)}) collective-permute-start(f32[96,256]{1,0:T(8,128)S(1)} %get-tuple-element.62), channel_id=1, source_target_pairs={{0,4},{4,0},{8,12},{12,8},{16,20},{20,16},{24,28},{28,24},{1,5},{5... | collective-permute-start | bytes 294920 | tf_op jit(solution)/shard_map/ppermute | solution.py:419
  37.8 6.2 %collective-permute-start.15 = (f32[96,256]{1,0:T(8,128)S(1)}, f32[96,256]{1,0:T(8,128)S(1)}, u32[]{:S(2)}, u32[]{:S(2)}) collective-permute-start(f32[96,256]{1,0:T(8,128)S(1)} %collective-permute-done.14), channel_id=1, source_target_pairs={{0,8},{8,16},{16,24},{24,28},{4,0},{12,4},{20,12},{28,20},{1,9},{9... | collective-permute-start | bytes 294920 | tf_op jit(solution)/shard_map/ppermute | solution.py:418
  44.7 3.1 %collective-permute-start.19 = (f32[96,256]{1,0:T(8,128)S(1)}, f32[96,256]{1,0:T(8,128)S(1)}, u32[]{:S(2)}, u32[]{:S(2)}) collective-permute-start(f32[96,256]{1,0:T(8,128)S(1)} %get-tuple-element.66), channel_id=1, source_target_pairs={{0,4},{4,0},{8,12},{12,8},{16,20},{20,16},{24,28},{28,24},{1,5},{5... | collective-permute-start | bytes 294920 | tf_op jit(solution)/shard_map/ppermute | solution.py:415
  44.7 8.7 %collective-permute-start.21 = (f32[96,256]{1,0:T(8,128)S(1)}, f32[96,256]{1,0:T(8,128)S(1)}, u32[]{:S(2)}, u32[]{:S(2)}) collective-permute-start(f32[96,256]{1,0:T(8,128)S(1)} %get-tuple-element.67), channel_id=1, source_target_pairs={{0,3},{1,2},{2,1},{3,0},{4,7},{5,6},{6,5},{7,4},{8,11},{9,10},{10,... | collective-permute-start | bytes 294920 | tf_op jit(solution)/shard_map/ppermute | solution.py:416
  47.2 6.2 %collective-permute-start.22 = (f32[96,256]{1,0:T(8,128)S(1)}, f32[96,256]{1,0:T(8,128)S(1)}, u32[]{:S(2)}, u32[]{:S(2)}) collective-permute-start(f32[96,256]{1,0:T(8,128)S(1)} %get-tuple-element.68), channel_id=1, source_target_pairs={{0,1},{1,0},{2,3},{3,2},{4,5},{5,4},{6,7},{7,6},{8,9},{9,8},{10,11... | collective-permute-start | bytes 294920 | tf_op jit(solution)/shard_map/ppermute | solution.py:417
  47.7 5.7 %collective-permute-start.23 = (f32[96,256]{1,0:T(8,128)S(1)}, f32[96,256]{1,0:T(8,128)S(1)}, u32[]{:S(2)}, u32[]{:S(2)}) collective-permute-start(f32[96,256]{1,0:T(8,128)S(1)} %get-tuple-element.69), channel_id=1, source_target_pairs={{0,4},{4,0},{8,12},{12,8},{16,20},{20,16},{24,28},{28,24},{1,5},{5... | collective-permute-start | bytes 294920 | tf_op jit(solution)/shard_map/ppermute | solution.py:419
  47.8 5.7 %collective-permute-start.20 = (f32[96,256]{1,0:T(8,128)S(1)}, f32[96,256]{1,0:T(8,128)S(1)}, u32[]{:S(2)}, u32[]{:S(2)}) collective-permute-start(f32[96,256]{1,0:T(8,128)S(1)} %collective-permute-done.19), channel_id=1, source_target_pairs={{0,8},{8,16},{16,24},{24,28},{4,0},{12,4},{20,12},{28,20},{1,9},{9... | collective-permute-start | bytes 294920 | tf_op jit(solution)/shard_map/ppermute | solution.py:418
  54.6 1.3 %collective-permute-start.24 = (f32[48,128]{1,0:T(8,128)S(1)}, f32[48,128]{1,0:T(8,128)S(1)}, u32[]{:S(2)}, u32[]{:S(2)}) collective-permute-start(f32[48,128]{1,0:T(8,128)S(1)} %shard_map.63), channel_id=1, source_target_pairs={{0,4},{4,0},{8,12},{12,8},{16,20},{20,16},{24,28},{28,24},{1,5},{5... | collective-permute-start | bytes 73736 | tf_op jit(solution)/shard_map/ppermute | solution.py:394
  55.9 3.8 %collective-permute-start.27 = (f32[48,128]{1,0:T(8,128)S(1)}, f32[48,128]{1,0:T(8,128)S(1)}, u32[]{:S(2)}, u32[]{:S(2)}) collective-permute-start(f32[48,128]{1,0:T(8,128)S(1)} %add.12), channel_id=1, source_target_pairs={{0,8},{4,12},{8,0},{12,4},{16,24},{20,28},{24,16},{28,20},{1,9},{5... | collective-permute-start | bytes 73736 | tf_op jit(solution)/shard_map/ppermute | solution.py:400
  57.4 5.6 %collective-permute-start.26 = (f32[48,128]{1,0:T(8,128)S(1)}, f32[48,128]{1,0:T(8,128)S(1)}, u32[]{:S(2)}, u32[]{:S(2)}) collective-permute-start(f32[48,128]{1,0:T(8,128)S(1)} %add.12), channel_id=1, source_target_pairs={{0,24},{4,28},{8,16},{12,20},{16,8},{20,12},{24,0},{28,4},{1,25},{... | collective-permute-start | bytes 73736 | tf_op jit(solution)/shard_map/ppermute | solution.py:400
  58.7 5.0 %collective-permute-start.25 = (f32[48,128]{1,0:T(8,128)S(1)}, f32[48,128]{1,0:T(8,128)S(1)}, u32[]{:S(2)}, u32[]{:S(2)}) collective-permute-start(f32[48,128]{1,0:T(8,128)S(1)} %add.12), channel_id=1, source_target_pairs={{0,16},{4,20},{8,24},{12,28},{16,0},{20,4},{24,8},{28,12},{1,17},{... | collective-permute-start | bytes 73736 | tf_op jit(solution)/shard_map/ppermute | solution.py:400
  63.7 4.6 %collective-permute-start.30 = (f32[48,128]{1,0:T(8,128)S(1)}, f32[48,128]{1,0:T(8,128)S(1)}, u32[]{:S(2)}, u32[]{:S(2)}) collective-permute-start(f32[48,128]{1,0:T(8,128)S(1)} %add_add_fusion.refs_0_), channel_id=1, source_target_pairs={{0,1},{1,0},{2,3},{3,2},{4,5},{5,4},{6,7},{7,6},{8,9},{9,8},{10,11... | collective-permute-start | bytes 73736 | tf_op jit(solution)/shard_map/ppermute | solution.py:400
  65.2 3.8 %collective-permute-start.29 = (f32[48,128]{1,0:T(8,128)S(1)}, f32[48,128]{1,0:T(8,128)S(1)}, u32[]{:S(2)}, u32[]{:S(2)}) collective-permute-start(f32[48,128]{1,0:T(8,128)S(1)} %add_add_fusion.refs_0_), channel_id=1, source_target_pairs={{0,2},{1,3},{2,0},{3,1},{4,6},{5,7},{6,4},{7,5},{8,10},{9,11},{10,... | collective-permute-start | bytes 73736 | tf_op jit(solution)/shard_map/ppermute | solution.py:400
  65.8 4.7 %collective-permute-start.28 = (f32[48,128]{1,0:T(8,128)S(1)}, f32[48,128]{1,0:T(8,128)S(1)}, u32[]{:S(2)}, u32[]{:S(2)}) collective-permute-start(f32[48,128]{1,0:T(8,128)S(1)} %add_add_fusion.refs_0_), channel_id=1, source_target_pairs={{0,3},{1,2},{2,1},{3,0},{4,7},{5,6},{6,5},{7,4},{8,11},{9,10},{10,... | collective-permute-start | bytes 73736 | tf_op jit(solution)/shard_map/ppermute | solution.py:400
